TPU v7x, 32 devices: a whole 2x2x4 slice. The times are simulated.
32 devices in a mesh: seq: 4 (over x, core), tp: 8 (over z, y).
Axes of the slice: x: 2, y: 2, z: 4, core: 2. Of those that a mesh axis runs over, the one named last changes fastest.
Arguments:
- hidden_in: bfloat16 [2048, 3584], P('seq', 'tp'), may hold values from -6 to 6
- mamba_gain: float32 [3584], replicated, may hold values from 0.1 to 1.9
- w_xz: bfloat16 [2, 1536, 3584], P(None, 'tp'), may hold values from -0.09375 to 0.09375
- w_bc: bfloat16 [3584, 128], replicated, may hold values from -0.09375 to 0.09375
- w_dt: bfloat16 [24, 3584], P('tp'), may hold values from -0.09375 to 0.09375
- dt_bias: float32 [24], P('tp'), may hold values from -2 to 0
- decay_rate: float32 [24], P('tp'), may hold values from 0.00024414062 to 0.3
- conv_x: float32 [4, 1536], P(None, 'tp'), may hold values from -3 to 3
- conv_bc: float32 [4, 128], replicated, may hold values from -3 to 3
- skip_gain: float32 [24], P('tp'), may hold values from 0.5 to 1.5
- inner_gain: float32 [1536], P('tp'), may hold values from 0.1 to 1.9
- w_out: bfloat16 [1536, 3584], P('tp'), may hold values from -0.15625 to 0.15625
- attn_gain: float32 [3584], replicated, may hold values from 0.1 to 1.9
- w_qkv: bfloat16 [3, 1792, 3584], P(None, 'tp'), may hold values from -0.13363062 to 0.13363062
- w_o: bfloat16 [1792, 3584], P('tp'), may hold values from -0.125 to 0.125
- seg_ids: int32 [2048], P('seq'), may hold values from 0 to 3, as said below
- pad_mask: int32 [2048], P('seq'), may hold values from 0 to 1, as said below
- tenant_bounds: int32 [4, 2], replicated, may hold values from 0 to 2048, as said below
Outputs:
- hidden_out: bfloat16 [2048, 3584], P('seq', 'tp')
- kv_cache: bfloat16 [2, 1792, 2048], P(None, 'tp', 'seq')
- tenant_states: float32 [4, 24, 64, 64], P(None, 'tp')
Inputs may be any that keep to these rules, and one draw needn't show every extreme that they name: seg_ids never falls along the tokens; each tenant is one run of at least 128 tokens. `pad_mask`: each tenant's padding is its last tokens, at least one and at most a quarter of its run. `tenant_bounds`: row t holds where tenant t's run in seg_ids starts and one past where it ends; the runs follow one another and cover all 2048 tokens.
All inputs are finite; a program needn't handle non-finite values.
Results may differ from a plain program's by a relative error of at most 0.017.
Values may be sent and summed in bfloat16 or wider, within the bound.
No kernel may reach another device: no remote copies, remote signals or barrier semaphores. Data moves between devices by JAX's collectives and lax.ppermute only.
A program may use at most 128 MiB of HBM per device.

v0:
```python
import jax
import jax.numpy as jnp
from jax import lax
from jax.sharding import PartitionSpec as P

HEADS_DEV = 1


HIGHEST = lax.Precision.HIGHEST


def from_behind(value, axis, by):
    devices = lax.axis_size(axis)
    pairs = [(i, i + by) for i in range(devices) if 0 <= i + by < devices]
    return lax.ppermute(value, axis, pairs)


def rms_scale(rows):
    return lax.rsqrt(jnp.mean(rows * rows, axis=-1, keepdims=True) + 1e-05)


def times_rows(left, weights):
    return lax.dot_general(
        left, weights, (((1,), (1,)), ((), ())), preferred_element_type=jnp.float32
    )


def tenant_of(places, run_starts):
    return jnp.sum((places[:, None] >= run_starts[None, :]).astype(jnp.int32), axis=1) - 1


def row_terms(weights, activations):
    return lax.dot_general(
        weights, activations, (((0,), (1,)), ((), ())), preferred_element_type=jnp.float32
    )


def attend_block(
    carry,
    piece,
    start,
    query_heads,
    query_places,
    query_tenant,
    first_start,
    run_starts,
    head_count,
    score_scale,
):
    key_rows, value_rows, keep_rows = piece
    count = key_rows.shape[0]
    key_heads = key_rows.reshape(count, head_count, -1)
    value_heads = value_rows.reshape(count, head_count, -1)

    def update(state):
        running_max, running_total, running_sum = state
        key_places = jnp.arange(count, dtype=jnp.int32)
        key_tenant = tenant_of(key_places, run_starts)
        visible = (
            (key_tenant[None, :] == query_tenant[:, None])
            & (key_places[None, :] <= query_places[:, None])
            & (keep_rows[None, :] > 0)
        )
        scores = (
            jnp.einsum("qhd,khd->hqk", query_heads, key_heads, preferred_element_type=jnp.float32)
            * score_scale
        )
        scores = jnp.where(visible[None], scores, -1e30)
        fresh_max = jnp.maximum(running_max, jnp.max(scores, axis=-1))
        weights = jnp.exp(scores - fresh_max[..., None]) * visible[None].astype(jnp.float32)
        running_total = jnp.sum(weights, axis=-1)
        running_sum = jnp.einsum(
            "hqk,khd->hqd",
            weights.astype(jnp.bfloat16),
            value_heads,
            preferred_element_type=jnp.float32,
        )
        return (fresh_max, running_total, running_sum)

    wanted = (start <= query_places[-1]) & (start + count - 1 >= first_start)
    return lax.cond(wanted, update, lambda state: state, carry)


def on_device(
    hidden_in,
    mamba_gain,
    w_xz,
    w_bc,
    w_dt,
    dt_bias,
    decay_rate,
    conv_x,
    conv_bc,
    skip_gain,
    inner_gain,
    w_out,
    attn_gain,
    w_qkv,
    w_o,
    seg_ids,
    pad_mask,
    tenant_bounds,
):
    tok_rows = hidden_in.shape[0]
    width = mamba_gain.shape[0]
    tp_count = lax.axis_size("tp")
    seq_base = lax.axis_index("seq") * tok_rows
    places = seq_base + jnp.arange(tok_rows, dtype=jnp.int32)
    run_starts = tenant_bounds[:, 0]
    run_ends = tenant_bounds[:, 1]
    tenant_count = tenant_bounds.shape[0]
    full_in = lax.all_gather(hidden_in, "tp", axis=1, tiled=True)
    wide = full_in.astype(jnp.float32)
    normed = (wide * rms_scale(wide) * mamba_gain).astype(jnp.bfloat16)
    inner_dev = w_xz.shape[1]
    projected = times_rows(normed, w_xz.reshape(2 * inner_dev, width))
    bc_raw = jnp.dot(normed, w_bc, preferred_element_type=jnp.float32)
    live_rows = pad_mask.astype(jnp.float32)
    step_size = jax.nn.softplus(times_rows(normed, w_dt) + dt_bias) * live_rows[:, None]
    raw_input = jnp.concatenate([projected[:, :inner_dev], bc_raw], axis=1)
    conv_kernel = jnp.concatenate([conv_x, conv_bc], axis=1)
    tap_count = conv_kernel.shape[0]
    before = from_behind(raw_input[tok_rows - (tap_count - 1) :], "seq", 1)
    extended = jnp.concatenate([before, raw_input], axis=0)
    before_places = seq_base - (tap_count - 1) + jnp.arange(tap_count - 1, dtype=jnp.int32)
    ext_tenant = jnp.concatenate([tenant_of(before_places, run_starts), seg_ids])
    conv_sum = jnp.zeros_like(raw_input)
    for tap_row in range(tap_count):
        same_tenant = (ext_tenant[tap_row : tap_row + tok_rows] == seg_ids).astype(jnp.float32)
        conv_sum = (
            conv_sum
            + conv_kernel[tap_row] * extended[tap_row : tap_row + tok_rows] * same_tenant[:, None]
        )
    activated = jax.nn.silu(conv_sum)
    state_size = w_bc.shape[1] // 2
    heads_dev = decay_rate.shape[0]
    head_dim = inner_dev // heads_dev
    x_heads = activated[:, :inner_dev].reshape(tok_rows, heads_dev, head_dim)
    input_b = activated[:, inner_dev : inner_dev + state_size]
    output_c = activated[:, inner_dev + state_size :]
    begins = (ext_tenant[tap_count - 2 : tap_count - 2 + tok_rows] != seg_ids).astype(jnp.int32)
    run_label = jnp.cumsum(begins)
    log_total = jnp.cumsum(-step_size * decay_rate, axis=0).T
    row_number = jnp.arange(tok_rows, dtype=jnp.int32)
    lower_same = (row_number[None, :] <= row_number[:, None]) & (
        run_label[:, None] == run_label[None, :]
    )
    log_gap = log_total[:, :, None] - log_total[:, None, :]
    decay_pairs = jnp.where(lower_same[None], jnp.exp(jnp.minimum(log_gap, 0.0)), 0.0)
    c_dot_b = jnp.dot(output_c, input_b.T, precision=HIGHEST)
    mixing = decay_pairs * c_dot_b[None] * step_size.T[:, None, :]
    y_local = jnp.einsum("hij,jhp->ihp", mixing, x_heads, precision=HIGHEST)
    picked = jnp.concatenate(
        [
            jnp.clip(run_ends - 1 - seq_base, 0, tok_rows - 1),
            jnp.full((1,), tok_rows - 1, jnp.int32),
        ]
    )
    owned = ((run_ends - 1 >= seq_base) & (run_ends - 1 < seq_base + tok_rows)).astype(jnp.float32)
    picked_hot = row_number[None, :] == picked[:, None]
    log_picked = jnp.dot(picked_hot.astype(jnp.float32), log_total.T, precision=HIGHEST)
    run_picked = jnp.sum(jnp.where(picked_hot, run_label[None, :], 0), axis=1)
    reaching = (row_number[None, :] <= picked[:, None]) & (
        run_label[None, :] == run_picked[:, None]
    )
    toward = (
        jnp.where(
            reaching[:, None, :],
            jnp.exp(jnp.minimum(log_picked[:, :, None] - log_total[None], 0.0)),
            0.0,
        )
        * step_size.T[None]
    )
    local_states = jnp.einsum("khj,jhp,jn->khpn", toward, x_heads, input_b, precision=HIGHEST)
    carry_factor = jnp.exp(log_picked) * (run_picked == 0).astype(jnp.float32)[:, None]
    block_decay = carry_factor[-1]
    block_state = local_states[-1]
    incoming = jnp.zeros_like(block_state)
    for hop_count in range(lax.axis_size("seq") - 1):
        incoming = from_behind(
            (block_decay[:, None, None] * incoming + block_state).astype(jnp.bfloat16), "seq", 1
        ).astype(jnp.float32)
    entry_factor = jnp.exp(log_total.T) * (run_label == 0).astype(jnp.float32)[:, None]
    y_carry = (
        jnp.einsum("in,hpn->ihp", output_c, incoming, precision=HIGHEST) * entry_factor[:, :, None]
    )
    tenant_part = (carry_factor[:-1, :, None, None] * incoming[None] + local_states[:-1]) * owned[
        :, None, None, None
    ]
    tenant_states = lax.psum(tenant_part.astype(jnp.bfloat16), "seq").astype(jnp.float32)
    y_full = y_local + y_carry + skip_gain[None, :, None] * x_heads
    gated = y_full.reshape(tok_rows, inner_dev) * jax.nn.silu(projected[:, inner_dev:])
    square_sum = lax.psum(jnp.sum(gated * gated, axis=1), "tp")
    inner_scale = lax.rsqrt(square_sum / (inner_dev * tp_count) + 1e-05)
    scaled = (gated * inner_scale[:, None] * inner_gain).astype(jnp.bfloat16)
    my_rows = lax.psum_scatter(
        row_terms(w_out, scaled).astype(jnp.bfloat16), "tp", scatter_dimension=0, tiled=True
    ).astype(jnp.float32)
    mixed_part = (hidden_in.astype(jnp.float32) + my_rows.T).astype(jnp.bfloat16)
    after_mix = lax.all_gather(mixed_part, "tp", axis=1, tiled=True)
    wide_mix = after_mix.astype(jnp.float32)
    normed_attn = (wide_mix * rms_scale(wide_mix) * attn_gain).astype(jnp.bfloat16)
    att_dev = w_qkv.shape[1]
    qkv_rows = times_rows(normed_attn, w_qkv.reshape(3 * att_dev, width)).astype(jnp.bfloat16)
    key_rows = qkv_rows[:, att_dev : 2 * att_dev]
    value_rows = qkv_rows[:, 2 * att_dev :]
    kv_cache = jnp.stack([key_rows.T, value_rows.T])
    head_count = HEADS_DEV
    head_size = att_dev // head_count
    query_heads = qkv_rows[:, :att_dev].reshape(tok_rows, head_count, head_size)
    keep_rows = pad_mask.astype(jnp.bfloat16)
    first_start = jnp.sum(
        jnp.where(jnp.arange(tenant_count, dtype=jnp.int32) == seg_ids[0], run_starts, 0)
    )
    score_scale = head_size ** (-0.5)
    initial = (
        jnp.full((head_count, tok_rows), -1e30, jnp.float32),
        jnp.zeros((head_count, tok_rows), jnp.float32),
        jnp.zeros((head_count, tok_rows, head_size), jnp.float32),
    )
    running_max, running_total, running_sum = attend_block(
        initial,
        (
            lax.all_gather(key_rows, "seq", axis=0, tiled=True),
            lax.all_gather(value_rows, "seq", axis=0, tiled=True),
            lax.all_gather(keep_rows, "seq", axis=0, tiled=True),
        ),
        jnp.int32(0),
        query_heads,
        places,
        seg_ids,
        first_start,
        run_starts,
        head_count,
        score_scale,
    )
    context = (running_sum / running_total[..., None]).astype(jnp.bfloat16)
    context_rows = context.transpose(1, 0, 2).reshape(tok_rows, att_dev)
    attn_part = lax.psum_scatter(
        row_terms(w_o, context_rows).astype(jnp.bfloat16), "tp", scatter_dimension=0, tiled=True
    ).astype(jnp.float32)
    hidden_out = (mixed_part.astype(jnp.float32) + attn_part.T).astype(jnp.bfloat16)
    return (hidden_out, kv_cache, tenant_states)


def solution(mesh):
    return jax.shard_map(
        on_device,
        mesh=mesh,
        in_specs=(
            P("seq", "tp"),
            P(),
            P(None, "tp", None),
            P(),
            P("tp", None),
            P("tp"),
            P("tp"),
            P(None, "tp"),
            P(),
            P("tp"),
            P("tp"),
            P("tp", None),
            P(),
            P(None, "tp", None),
            P("tp", None),
            P("seq"),
            P("seq"),
            P(),
        ),
        out_specs=(P("seq", "tp"), P(None, "tp", "seq"), P(None, "tp", None, None)),
        check_vma=False,
    )
```

profile of v0, /device:TPU:0, one launch (start us, length us, event | category | flops | bytes accessed | tf_op | source)
XLA Modules:
  0.0 445.4 jit_solution(3268128073207426532)
XLA Ops:
  7.3 0.7 all-gather.4.cloned.1.call-update
  8.0 0.8 clamp_bitcast_fusion
  8.8 0.2 convert_reduce_fusion.1
  9.0 0.8 pad_add_fusion
  9.7 0.8 convert_bitcast_fusion
  10.5 0.3 reduce-window.15
  10.9 0.9 fusion.91
  12.1 0.2 select_reduce_fusion
  12.3 0.8 fusion.101
  13.1 0.2 fusion.57
  13.4 66.4 %all-gather.4.cloned.1.call-done = bf16[512,3584]{0,1:T(8,128)(2,1)} async-done(((bf16[512,448]{0,1:T(8,128)(2,1)}), bf16[512,3584]{0,1:T(8,128)(2,1)}) %all-gather.4.cloned.1.call-update) | async-done | bytes 3670032 | tf_op jit(solution)/shard_map/all_gather | solution.py:112
  79.8 2.9 fusion.16
  82.7 3.3 negate_multiply_fusion
  86.1 0.9 reduce-window.19
  87.0 0.2 slice_reduce_fusion
  87.1 0.2 reduce-window.24
  87.4 0.2 exponential_multiply_fusion
  87.6 0.2 slice_reduce_fusion.1
  87.8 3.9 fusion.99
  91.8 1.5 fusion.97
  93.3 1.3 collective-permute-start
  94.7 0.9 collective-permute-done
  95.6 0.3 maximum_maximum_fusion
  95.9 0.6 divide_multiply_fusion
  96.6 1.7 fusion.46
  98.4 5.3 %collective-permute-start.1 = (bf16[3,64,64]{2,1,0:T(8,128)(2,1)S(1)}, bf16[3,64,64]{2,1,0:T(8,128)(2,1)S(1)}, u32[]{:S(2)}, u32[]{:S(2)}) collective-permute-start(bf16[3,64,64]{2,1,0:T(8,128)(2,1)S(1)} %add_convert_fusion.2), channel_id=1, source_target_pairs={{0,8},{8,16},{16,24},{1,9},{9,17},{17,25},{2,10},{10,18},{18,26},{... | collective-permute-start | bytes 73736 | tf_op jit(solution)/shard_map/ppermute | solution.py:15
  103.8 0.8 collective-permute-done.1
  104.7 4.7 %collective-permute-start.2 = (bf16[3,64,64]{2,1,0:T(8,128)(2,1)S(1)}, bf16[3,64,64]{2,1,0:T(8,128)(2,1)S(1)}, u32[]{:S(2)}, u32[]{:S(2)}) collective-permute-start(bf16[3,64,64]{2,1,0:T(8,128)(2,1)S(1)} %add_convert_fusion.1), channel_id=1, source_target_pairs={{0,8},{8,16},{16,24},{1,9},{9,17},{17,25},{2,10},{10,18},{18,26},{... | collective-permute-start | bytes 73736 | tf_op jit(solution)/shard_map/ppermute | solution.py:15
  109.4 1.0 fusion.76
  110.5 4.5 %collective-permute-start.3 = (bf16[3,64,64]{2,1,0:T(8,128)(2,1)S(1)}, bf16[3,64,64]{2,1,0:T(8,128)(2,1)S(1)}, u32[]{:S(2)}, u32[]{:S(2)}) collective-permute-start(bf16[3,64,64]{2,1,0:T(8,128)(2,1)S(1)} %add_convert_fusion), channel_id=1, source_target_pairs={{0,8},{8,16},{16,24},{1,9},{9,17},{17,25},{2,10},{10,18},{18,26},{... | collective-permute-start | bytes 73736 | tf_op jit(solution)/shard_map/ppermute | solution.py:15
  115.1 3.9 fusion.49
  119.0 0.4 fusion.53
  119.5 18.9 %psum.14 = f32[512]{0:T(512)S(1)} all-reduce(f32[512]{0:T(512)S(1)} %get-tuple-element.77), channel_id=1, replica_groups=mesh['seq'=4,'tp'=8] {'tp'}, use_global_device_ids=true, to_apply=%region_8.9 | all-reduce | flops 512 | bytes 4096 | tf_op jit(solution)/shard_map/psum | solution.py:193
  138.4 4.4 fusion.22
  142.8 6.0 %copy.50 = bf16[3584,512]{1,0:T(8,128)(2,1)} copy(bf16[3584,512]{0,1:T(8,128)(2,1)} %fusion.22) | data formatting | bytes 7340032
  148.8 1.0 copy.40
  149.9 78.3 %reduce-scatter.7.cloned.1.call-done = bf16[448,512]{1,0:T(8,128)(2,1)} async-done(((bf16[3584,512]{1,0:T(8,128)(2,1)}), bf16[448,512]{1,0:T(8,128)(2,1)}) %reduce-scatter.7.cloned.1.call-update) | async-done | bytes 458768
  228.1 2.0 copy.51
  230.2 1.3 fusion.56
  231.5 1.0 copy.41
  232.5 0.5 slice.121
  233.1 0.6 slice.120
  233.6 1.3 fusion.93
  236.1 5.2 %all-gather = bf16[4,1,512]{2,1,0:T(2,128)(2,1)S(1)} all-gather(bf16[1,1,512]{2,1,0:T(2,128)(2,1)S(1)} %reshape.310), channel_id=1, replica_groups=mesh['seq'=4,'tp'=8] {'seq'}, dimensions={0}, use_global_device_ids=true | all-gather | bytes 5120 | tf_op jit(solution)/shard_map/all_gather | solution.py:226
  241.3 1.8 fusion.68
  243.2 55.9 %all-gather.6.cloned.1.call-done = bf16[512,3584]{0,1:T(8,128)(2,1)} async-done(((bf16[512,448]{0,1:T(8,128)(2,1)}), bf16[512,3584]{0,1:T(8,128)(2,1)}) %all-gather.6.cloned.1.call-update) | async-done | bytes 3670032 | tf_op jit(solution)/shard_map/all_gather | solution.py:200
  299.2 2.9 fusion.19
  302.1 7.1 %fusion.43 = bf16[512,672]{0,1:T(8,128)(2,1)} fusion(bf16[672,3584]{1,0:T(8,128)(2,1)} %bitcast.115, bf16[512,3584]{0,1:T(8,128)(2,1)} %all-gather.6.cloned.1.call-done, f32[3584]{0:T(1024)S(1)} %copy-done.12, f32[512]{0:T(512)S(1)} %add_rsqrt_fusion), kind=kOutput, calls=%fused_computation.52 | convolution fusion | flops 2473934848 | bytes 9191424 | tf_op jit(solution)/shard_map/dot_general | solution.py:23
  309.1 1.8 slice_bitcast_fusion.3
  311.0 9.7 %all_gather.19 = bf16[2048,224]{0,1:T(8,128)(2,1)} all-gather(bf16[512,224]{0,1:T(8,128)(2,1)S(1)} %get-tuple-element.85), channel_id=1, replica_groups=mesh['seq'=4,'tp'=8] {'seq'}, dimensions={0}, use_global_device_ids=true | all-gather | bytes 1146880 | tf_op jit(solution)/shard_map/all_gather | solution.py:225
  320.7 11.1 %all_gather.18 = bf16[2048,224]{0,1:T(8,128)(2,1)} all-gather(bf16[512,224]{0,1:T(8,128)(2,1)S(1)} %get-tuple-element.86), channel_id=1, replica_groups=mesh['seq'=4,'tp'=8] {'seq'}, dimensions={0}, use_global_device_ids=true | all-gather | bytes 1146880 | tf_op jit(solution)/shard_map/all_gather | solution.py:224
  331.8 10.9 %conditional.1 = (f32[1,512]{1,0:T(1,128)S(1)}, f32[1,512,224]{1,2,0:T(8,128)}) conditional(s32[]{:T(128)} %convert_element_type.146, () %tuple.16, (s32[4,1]{0,1:T(1,128)S(1)}, s32[512]{0:T(512)S(1)}, s32[512]{0:T(512)S(1)}, bf16[4,1,512]{2,1,0:T(2,128)(2,1)S(1)}, bf16[512,672]{0,1:T(8,128)(2,1)}, /*index=5*/bf16[2048,224]{0,1:T(8,128)(2,1)}, ...), branch_computations={%region_12.13_spmd, %region_13.17_spmd} | conditional | flops 965764608 | bytes 20287550 | solution.py:81
  332.0 2.3 copy.42
  334.2 3.1 fusion.2
  337.4 3.1 fusion.7
  340.4 2.3 fusion.4
  342.7 4.6 %fusion.23 = bf16[3584,512]{0,1:T(8,128)(2,1)} fusion(bf16[224,3584]{1,0:T(8,128)(2,1)} %param.34, f32[1,512,224]{1,2,0:T(8,128)} %get-tuple-element.30, f32[512]{0:T(512)S(1)} %bitcast.107), kind=kOutput, calls=%fused_computation.33 | convolution fusion | flops 824147968 | bytes 5736448 | tf_op jit(solution)/shard_map/dot_general | solution.py:33
  347.3 5.9 %copy.52 = bf16[3584,512]{1,0:T(8,128)(2,1)} copy(bf16[3584,512]{0,1:T(8,128)(2,1)} %fusion.23) | data formatting | bytes 7340032
  353.3 1.7 copy.46
  355.0 1.7 pad_maximum_fusion.1
  356.7 76.2 %reduce-scatter.9.cloned.1.call-done = bf16[448,512]{1,0:T(8,128)(2,1)} async-done(((bf16[3584,512]{1,0:T(8,128)(2,1)}), bf16[448,512]{1,0:T(8,128)(2,1)}) %reduce-scatter.9.cloned.1.call-update) | async-done | bytes 458768
  432.9 2.0 copy.53
  434.9 2.0 fusion.55
  436.9 2.0 copy.45
  (77 shorter events, 1.8 us)
Async XLA Ops:
  7.2 80.6 %copy-start = (bf16[2,192,3584]{2,1,0:T(8,128)(2,1)S(1)}, bf16[2,192,3584]{2,1,0:T(8,128)(2,1)}, u32[]{:S(2)}) copy-start(bf16[2,192,3584]{2,1,0:T(8,128)(2,1)} %param.22) | copy-start | bytes 8257540
  7.2 75.5 %copy-start.11 = (f32[3584]{0:T(1024)S(1)}, f32[3584]{0:T(1024)}, u32[]{:S(2)}) copy-start(f32[3584]{0:T(1024)} %param.21) | copy-start | bytes 43012
  7.2 75.5 %copy-start.13 = (f32[3]{0:T(128)S(1)}, f32[3]{0:T(128)}, u32[]{:S(2)}) copy-start(f32[3]{0:T(128)} %param.26) | copy-start | bytes 40
  7.2 75.5 %copy-start.14 = (f32[3]{0:T(128)S(1)}, f32[3]{0:T(128)}, u32[]{:S(2)}) copy-start(f32[3]{0:T(128)} %param.25) | copy-start | bytes 40
  7.2 75.5 %copy-start.10 = (bf16[3,3584]{1,0:T(4,128)(2,1)S(1)}, bf16[3,3584]{1,0:T(4,128)(2,1)}, u32[]{:S(2)}) copy-start(bf16[3,3584]{1,0:T(4,128)(2,1)} %param.24) | copy-start | bytes 64516
  7.2 72.6 %all-gather.4.cloned.1.call-start = ((), (), s32[]{:S(2)}) async-start(), calls=%async_computation.2 | async-start | bytes 4128768 | tf_op jit(solution)/shard_map/all_gather | solution.py:112
  8.0 220.2 %reduce-scatter.7.cloned.1.call-start = ((), (), s32[]{:S(2)}) async-start(), calls=%async_computation.5 | async-start | bytes 4128768
  87.8 3.9 copy-start.1
  87.8 3.9 copy-start.9
  93.3 2.3 collective-permute-start
  98.3 12.1 %copy-start.2 = (f32[5,3,64,64]{3,2,0,1:T(8,128)}, f32[5,3,64,64]{3,2,0,1:T(8,128)S(1)}, u32[]{:S(2)}) copy-start(f32[5,3,64,64]{3,2,0,1:T(8,128)S(1)} %fusion.46) | copy-start | bytes 737284
  98.3 20.7 %copy-start.8 = (f32[3]{0:T(128)S(1)}, f32[3]{0:T(128)}, u32[]{:S(2)}) copy-start(f32[3]{0:T(128)} %param.29) | copy-start | bytes 40
  98.4 6.2 %collective-permute-start.1 = (bf16[3,64,64]{2,1,0:T(8,128)(2,1)S(1)}, bf16[3,64,64]{2,1,0:T(8,128)(2,1)S(1)}, u32[]{:S(2)}, u32[]{:S(2)}) collective-permute-start(bf16[3,64,64]{2,1,0:T(8,128)(2,1)S(1)} %add_convert_fusion.2), channel_id=1, source_target_pairs={{0,8},{8,16},{16,24},{1,9},{9,17},{17,25},{2,10},{10,18},{18,26},{... | collective-permute-start | bytes 73736 | tf_op jit(solution)/shard_map/ppermute | solution.py:15
  104.7 5.7 %collective-permute-start.2 = (bf16[3,64,64]{2,1,0:T(8,128)(2,1)S(1)}, bf16[3,64,64]{2,1,0:T(8,128)(2,1)S(1)}, u32[]{:S(2)}, u32[]{:S(2)}) collective-permute-start(bf16[3,64,64]{2,1,0:T(8,128)(2,1)S(1)} %add_convert_fusion.1), channel_id=1, source_target_pairs={{0,8},{8,16},{16,24},{1,9},{9,17},{17,25},{2,10},{10,18},{18,26},{... | collective-permute-start | bytes 73736 | tf_op jit(solution)/shard_map/ppermute | solution.py:15
  110.5 27.8 %copy-start.6 = (f32[192]{0:T(256)S(1)}, f32[192]{0:T(256)}, u32[]{:S(2)}) copy-start(f32[192]{0:T(256)} %param.30) | copy-start | bytes 2308
  110.5 8.4 %collective-permute-start.3 = (bf16[3,64,64]{2,1,0:T(8,128)(2,1)S(1)}, bf16[3,64,64]{2,1,0:T(8,128)(2,1)S(1)}, u32[]{:S(2)}, u32[]{:S(2)}) collective-permute-start(bf16[3,64,64]{2,1,0:T(8,128)(2,1)S(1)} %add_convert_fusion), channel_id=1, source_target_pairs={{0,8},{8,16},{16,24},{1,9},{9,17},{17,25},{2,10},{10,18},{18,26},{... | collective-permute-start | bytes 73736 | tf_op jit(solution)/shard_map/ppermute | solution.py:15
  142.8 6.1 %copy-start.3 = (bf16[512,448]{0,1:T(8,128)(2,1)S(1)}, bf16[512,448]{0,1:T(8,128)(2,1)}, u32[]{:S(2)}) copy-start(bf16[512,448]{0,1:T(8,128)(2,1)} %param.20) | copy-start | bytes 1376260
  148.7 83.8 %copy-start.5 = (s32[512]{0:T(512)S(1)}, s32[512]{0:T(512)}, u32[]{:S(2)}) copy-start(s32[512]{0:T(512)} %param.35) | copy-start | bytes 6148
  148.7 84.9 %copy-start.7 = (s32[4,2]{0,1:T(2,128)S(1)}, s32[4,2]{0,1:T(2,128)}, u32[]{:S(2)}) copy-start(s32[4,2]{0,1:T(2,128)} %param.37) | copy-start | bytes 100
  148.8 150.4 %all-gather.6.cloned.1.call-start = ((), (), s32[]{:S(2)}) async-start(), calls=%async_computation.3 | async-start | bytes 4128768 | tf_op jit(solution)/shard_map/all_gather | solution.py:200
  149.9 152.2 %copy-start.12 = (f32[3584]{0:T(1024)S(1)}, f32[3584]{0:T(1024)}, u32[]{:S(2)}) copy-start(f32[3584]{0:T(1024)} %param.32) | copy-start | bytes 43012
  232.5 120.8 %all-reduce.2.cloned.1.call-start = ((), (), s32[]{:S(2)}) async-start(), calls=%async_computation.4 | async-start | bytes 393216 | tf_op jit(solution)/shard_map/psum | solution.py:190
  243.2 189.7 %reduce-scatter.9.cloned.1.call-start = ((), (), s32[]{:S(2)}) async-start(), calls=%async_computation.6 | async-start | bytes 4128768
  334.2 3.1 copy-start.4
Sparse Core Ops, SparseCore 0:
  10.2 69.5 all-gather.3
  148.9 79.2 reduce-scatter.6
  232.6 66.5 all-gather.5
  301.9 30.5 all-reduce.1
  353.4 79.4 reduce-scatter.8
where the time goes:
time: 447 us; the launch traced here: 445 us
  waiting for transfers between devices  279 us (62%)
  blocking collectives  44.9 us (10%)
  matrix products  38 us (9%)
  local copies, waits for them, and re-layouts  27.5 us (6%)
  other arithmetic  24.2 us (5%)
  starting transfers between devices  16 us (4%)
  between operations  15.4 us (3%)
    unnamed x7, waiting for transfers between devices  155 us
    all_gather x1, waiting for transfers between devices, on_device(): full_in = lax.all_gather(hidden_in, 'tp', axis=1, tiled=True)  66.4 us
    all_gather x1, waiting for transfers between devices, on_device(): after_mix = lax.all_gather(mixed_part, 'tp', axis=1, tiled=True)  55.9 us
    unnamed x37, local copies, waits for them, and re-layouts  20.7 us
    psum x1, blocking collectives, on_device(): square_sum = lax.psum(jnp.sum(gated * gated, axis=1), 'tp')  18.9 us
    ppermute x4, starting transfers between devices, from_behind(): return lax.ppermute(value, axis, pairs)  15.8 us
    dot_general x3, matrix products, times_rows(): lax.dot_general(left, weights, (((1,), (1,)), ((), ())), preferred_elemen...  14.3 us
    all_gather x1, blocking collectives, on_device(): lax.all_gather(key_rows, 'seq', axis=0, tiled=True)  11.1 us
  transfers between devices with their start and end apart: 9, of which 6 were waited for; matrix products, arithmetic and copies ran while one was open for 12% of the time, Pallas kernels for 0%

commit v1 on v0

v1 whole, which is shorter than its diff:
```python
import functools

import jax
import jax.numpy as jnp
import numpy as np
from jax import lax
from jax.experimental import pallas as pl
from jax.experimental.pallas import tpu as pltpu
from jax.sharding import PartitionSpec as P

F32 = jnp.float32
BF16 = jnp.bfloat16
EPS = 1e-05
NEG = -1e30


def ring_order(count):
    columns = {8: 2, 32: 4}.get(count, 0)
    if not columns:
        return list(range(count))
    rows = count // columns
    order = [row * columns for row in range(rows)]
    for row in reversed(range(rows)):
        inner = list(range(1, columns))
        if (rows - 1 - row) % 2:
            inner.reverse()
        order += [row * columns + column for column in inner]
    return order


def sources(count):
    order = ring_order(count)
    place = {device: i for i, device in enumerate(order)}
    table = np.zeros((count, count), np.int32)
    for device in range(count):
        at = place[device]
        slots = [order[at]]
        for hop in range(1, (count - 1) // 2 + 1):
            slots += [order[(at - hop) % count], order[(at + hop) % count]]
        if count % 2 == 0 and count > 1:
            slots.append(order[(at + count // 2) % count])
        table[device] = slots
    return table


def ring_gather(piece, axis, count):
    order = ring_order(count)
    ahead = [(order[i], order[(i + 1) % count]) for i in range(count)]
    behind = [(order[i], order[(i - 1) % count]) for i in range(count)]
    pieces = [piece]
    one = two = piece
    for _ in range((count - 1) // 2):
        one = lax.ppermute(one, axis, ahead)
        two = lax.ppermute(two, axis, behind)
        pieces += [one, two]
    if count % 2 == 0 and count > 1:
        half = piece.shape[0] // 2
        if half % 16 == 0:
            one = lax.ppermute(one[:half], axis, ahead)
            two = lax.ppermute(two[half:], axis, behind)
            pieces += [one, two]
        else:
            pieces.append(lax.ppermute(one, axis, ahead))
    return pieces


def lay_out(slots_ref, piece_refs, rows, full_ref):
    columns = full_ref.shape[1]
    total = jnp.zeros((8, columns), F32)
    slot = 0
    done = 0
    for piece in piece_refs:
        count = piece.shape[0]
        strip = next(s for s in (64, 32, 16, 8) if count % s == 0)
        start = slots_ref[slot] * rows + done

        def body(i, carry, piece=piece, strip=strip, start=start):
            part = piece[pl.ds(pl.multiple_of(i * strip, strip), strip), :]
            full_ref[pl.ds(pl.multiple_of(start + i * strip, 16), strip), :] = part
            wide = part.astype(F32)
            return carry + jnp.sum((wide * wide).reshape(strip // 8, 8, columns), axis=0)

        total = lax.fori_loop(0, count // strip, body, total)
        done += count
        if done == rows:
            slot, done = slot + 1, 0
    return jnp.sum(total, axis=0, keepdims=True)


def call(kernel, out_shape, operands, smem=(), scratch=(), flops=0):
    specs = [
        pl.BlockSpec(memory_space=pltpu.SMEM if i in smem else pltpu.VMEM)
        for i in range(len(operands))
    ]
    size = sum(o.size * o.dtype.itemsize for o in operands)
    return pl.pallas_call(
        kernel,
        out_shape=out_shape,
        in_specs=specs,
        out_specs=jax.tree.map(lambda _: pl.BlockSpec(memory_space=pltpu.VMEM), out_shape),
        scratch_shapes=list(scratch),
        compiler_params=pltpu.CompilerParams(vmem_limit_bytes=40 << 20),
        cost_estimate=pl.CostEstimate(flops=flops, bytes_accessed=size, transcendentals=0),
    )(*operands)


def silu(value):
    return value / (1.0 + jnp.exp(-value))


def in_kernel(pieces, rows, conv_rows, inner, *refs):
    slots_ref = refs[0]
    piece_refs = refs[1 : 1 + pieces]
    w_ref, raw_ref, z_ref, dt_ref, tail_ref, full_ref, acc_ref = refs[1 + pieces :]
    width = full_ref.shape[0]
    squares = lay_out(slots_ref, piece_refs, rows, full_ref)
    scale = lax.rsqrt(squares / width + EPS)
    acc_ref[...] = jnp.dot(w_ref[...], full_ref[...], preferred_element_type=F32)
    raw_ref[...] = acc_ref[:conv_rows, :] * scale
    z_ref[...] = acc_ref[conv_rows : conv_rows + inner, :] * scale
    dt_ref[...] = acc_ref[conv_rows + inner :, :] * scale
    last = raw_ref.shape[1] - 128
    tail_ref[...] = raw_ref[:, last:].T[120:, :]


def mix_kernel(
    tenants,
    heads,
    scal_ref,
    raw_ref,
    dt_ref,
    halo_ref,
    taps_ref,
    head_ref,
    rel_ref,
    live_ref,
    pad_ref,
    y_ref,
    c_ref,
    entry_ref,
    pay_ref,
    local_ref,
    ext_ref,
    x_ref,
    xdt_ref,
):
    conv_rows, toks = raw_ref.shape
    inner = y_ref.shape[0]
    hd = inner // heads
    rel = rel_ref[...]
    lane = lax.broadcasted_iota(jnp.int32, (1, toks), 1)
    before = jnp.concatenate([jnp.zeros((120, conv_rows), F32), halo_ref[...]], axis=0).T
    ext_ref[:, :128] = before
    ext_ref[:, 128:] = raw_ref[...]
    strip = 64
    keep = [(rel >= shift).astype(F32) for shift in range(4)]
    for i in range(conv_rows // strip):
        rows = pl.ds(i * strip, strip)
        ext = ext_ref[rows, :]
        taps = taps_ref[rows, :]
        total = taps[:, 3:4] * ext[:, 128:]
        for shift in range(1, 4):
            moved = pltpu.roll(ext, shift, 1)[:, 128:]
            total = total + taps[:, 3 - shift : 4 - shift] * moved * keep[shift]
        x_ref[rows, :] = silu(total)
    step = dt_ref[...] + head_ref[:, 0:1]
    step = (jnp.maximum(step, 0.0) + jnp.log1p(jnp.exp(-jnp.abs(step)))) * live_ref[...]
    logs = -step * head_ref[:, 1:2]
    shift = 1
    while shift < toks:
        logs = logs + jnp.where(lane >= shift, pltpu.roll(logs, shift, 1), 0.0)
        shift *= 2
    start = lane - rel
    entry_ref[...] = jnp.exp(logs) * (start < 0).astype(F32)
    for h in range(heads):
        xdt_ref[h * hd : (h + 1) * hd, :] = x_ref[h * hd : (h + 1) * hd, :] * step[h : h + 1, :]
    input_b = x_ref[inner : inner + 64, :]
    output_c = x_ref[inner + 64 : inner + 128, :].astype(BF16)
    c_ref[...] = output_c
    bc_tok = x_ref[inner : inner + 128, :].T
    b_tok = bc_tok[:, :64].astype(BF16)
    columns = [
        jnp.broadcast_to(logs[h : h + 1, :], (128, toks)).T for h in range(heads)
    ]
    for block in range(toks // 128):
        here = slice(block * 128, (block + 1) * 128)
        upto = (block + 1) * 128
        key = lax.broadcasted_iota(jnp.int32, (upto, 128), 0)
        seen = (key <= lane[:, here]) & (key >= start[:, here])
        bias = jnp.where(seen, 0.0, NEG)
        c_dot_b = jnp.dot(b_tok[:upto, :], output_c[:, here], preferred_element_type=F32)
        for h in range(heads):
            gap = logs[h : h + 1, here] - columns[h][:upto, :]
            mixing = (jnp.exp(jnp.minimum(gap, 0.0) + bias) * c_dot_b).astype(BF16)
            rows = slice(h * hd, (h + 1) * hd)
            y_ref[rows, here] = (
                jnp.dot(
                    xdt_ref[rows, :upto].astype(BF16), mixing, preferred_element_type=F32
                )
                + head_ref[h : h + 1, 2:3] * x_ref[rows, here]
            )
    wide_b = bc_tok.astype(BF16)
    tok = lax.broadcasted_iota(jnp.int32, (inner, 128), 1)
    for k in range(tenants + 1):
        pick, first = scal_ref[k], scal_ref[8 + k]
        at = jnp.sum(jnp.where(lane == pick, logs, 0.0), axis=1, keepdims=True)
        inside = (lane <= pick) & (lane >= first)
        toward = jnp.exp(jnp.minimum(at - logs, 0.0) + jnp.where(inside, 0.0, NEG))
        carried = jnp.exp(at) * jnp.where(first < 0, 1.0, 0.0)
        lhs = jnp.concatenate(
            [
                (xdt_ref[h * hd : (h + 1) * hd, :] * toward[h : h + 1, :]).astype(BF16)
                for h in range(heads)
            ],
            axis=0,
        )
        state = jnp.dot(lhs, wide_b, preferred_element_type=F32)
        factor = jnp.concatenate(
            [jnp.broadcast_to(carried[h : h + 1, :], (hd, 128)) for h in range(heads)], axis=0
        )
        if k < tenants:
            local_ref[k * inner : (k + 1) * inner, :] = jnp.where(tok < 64, state, factor)
        else:
            high = factor.astype(BF16).astype(F32)
            packed = jnp.where(tok < 64, state, jnp.where(tok < 96, high, factor - high))
            pay_ref[:inner, :] = packed.astype(BF16)
    pay_ref[inner:, :] = pad_ref[...].astype(BF16)


def gate_kernel(tenants, heads, count, *refs):
    scal_ref = refs[0]
    pay_refs = refs[1 : 1 + count]
    y_ref, z_ref, c_ref, entry_ref, local_ref, g_ref, tenant_ref = refs[1 + count :]
    inner = y_ref.shape[0]
    hd = inner // heads
    incoming = jnp.zeros((inner, 64), F32)
    decay = jnp.ones((inner, 1), F32)
    for pay in pay_refs:
        wide = pay[:inner, :].astype(F32)
        incoming = incoming + decay * wide[:, :64]
        decay = decay * (wide[:, 64:65] + wide[:, 96:97])
    for h in range(heads):
        rows = slice(h * hd, (h + 1) * hd)
        carry = jnp.dot(incoming[rows, :].astype(BF16), c_ref[...], preferred_element_type=F32)
        y_full = y_ref[rows, :] + carry * entry_ref[h : h + 1, :]
        g_ref[rows, :] = (y_full * silu(z_ref[rows, :])).astype(BF16)
    for k in range(tenants):
        rows = slice(k * inner, (k + 1) * inner)
        owned = scal_ref[16 + k].astype(F32)
        local = local_ref[rows, :]
        tenant_ref[rows, :] = ((local[:, 64:65] * incoming + local[:, :64]) * owned).astype(BF16)


def mixed_kernel(pieces, rows, *refs):
    slots_ref = refs[0]
    piece_refs = refs[1 : 1 + pieces]
    w_ref, hidden_ref, out_ref, full_ref = refs[1 + pieces :]
    squares = lay_out(slots_ref, piece_refs, rows, full_ref)
    scale = lax.rsqrt(squares / full_ref.shape[0] + EPS)
    product = jnp.dot(w_ref[...], full_ref[...], preferred_element_type=F32)
    out_ref[...] = (hidden_ref[...].astype(F32) + product * scale).astype(BF16)


def qkv_kernel(pieces, rows, *refs):
    slots_ref = refs[0]
    piece_refs = refs[1 : 1 + pieces]
    w_ref, q_ref, kv_ref, full_ref = refs[1 + pieces :]
    squares = lay_out(slots_ref, piece_refs, rows, full_ref)
    scale = lax.rsqrt(squares / full_ref.shape[0] + EPS)
    product = jnp.dot(w_ref[...], full_ref[...], preferred_element_type=F32)
    att = q_ref.shape[0]
    q_ref[...] = (product[:att] * scale).astype(BF16)
    kv_ref[...] = (product[att:] * scale).astype(BF16)


def attend_kernel(blocks, score_scale, *refs):
    scal_ref, q_ref = refs[:2]
    kv_refs = refs[2 : 2 + blocks]
    pad_ref, rel_ref, ctx_ref, q_aug, k_aug, peak_ref, total_ref, sum_ref = refs[2 + blocks :]
    att, toks = q_ref.shape
    extra = q_aug.shape[0] - att
    row = lax.broadcasted_iota(jnp.int32, (extra, toks), 0)
    q_aug[:att, :] = q_ref[...]
    q_aug[att:, :] = jnp.where(row == 0, 1.0, 0.0).astype(BF16)
    place = scal_ref[0] * toks + lax.broadcasted_iota(jnp.int32, (1, toks), 1)
    start = place - rel_ref[...]
    peak_ref[...] = jnp.full(peak_ref.shape, NEG, F32)
    total_ref[...] = jnp.zeros(total_ref.shape, F32)
    sum_ref[...] = jnp.zeros(sum_ref.shape, F32)
    for b in range(blocks):

        @pl.when(scal_ref[32 + b] > 0)
        def _(b=b):
            count = kv_refs[b].shape[1]
            k_aug[:att, :] = kv_refs[b][:att, :]
            bias = (pad_ref[b : b + 1, :] - 1.0) * 1e30
            k_aug[att:, :] = jnp.where(row == 0, bias, 0.0).astype(BF16)
            scores = (
                lax.dot_general(
                    k_aug[...], q_aug[...], (((0,), (0,)), ((), ())), preferred_element_type=F32
                )
                * score_scale
            )
            key = scal_ref[16 + b] * count + lax.broadcasted_iota(jnp.int32, (count, toks), 0)
            scores = jnp.where((key <= place) & (key >= start), scores, NEG)
            peak = jnp.maximum(peak_ref[...], jnp.max(scores, axis=0, keepdims=True))
            weights = jnp.exp(scores - peak)
            keep = jnp.exp(peak_ref[...] - peak)
            peak_ref[...] = peak
            total_ref[...] = total_ref[...] * keep + jnp.sum(weights, axis=0, keepdims=True)
            sum_ref[...] = sum_ref[...] * keep + jnp.dot(
                kv_refs[b][att:, :], weights.astype(BF16), preferred_element_type=F32
            )

    ctx_ref[...] = (sum_ref[...] / total_ref[...]).astype(BF16)


def last_kernel(pieces, rows, *refs):
    slots_ref = refs[0]
    piece_refs = refs[1 : 1 + pieces]
    w_ref, mixed_ref, out_ref, full_ref = refs[1 + pieces :]
    lay_out(slots_ref, piece_refs, rows, full_ref)
    product = jnp.dot(w_ref[...], full_ref[...], preferred_element_type=F32)
    out_ref[...] = (mixed_ref[...].astype(F32) + product).T.astype(BF16)


def on_device(
    tp_count,
    seq_count,
    hidden_in,
    mamba_gain,
    w_xz,
    w_bc,
    w_dt,
    dt_bias,
    decay_rate,
    conv_x,
    conv_bc,
    skip_gain,
    inner_gain,
    w_out,
    attn_gain,
    w_qkv,
    w_o,
    seg_ids,
    pad_mask,
    tenant_bounds,
):
    toks, part = hidden_in.shape
    width = mamba_gain.shape[0]
    inner = w_xz.shape[1]
    heads = decay_rate.shape[0]
    att = w_qkv.shape[1]
    tenants = tenant_bounds.shape[0]
    bc = w_bc.shape[1]
    conv_rows = inner + bc
    seq = lax.axis_index("seq")
    tp = lax.axis_index("tp")
    sds = jax.ShapeDtypeStruct

    hidden_t = hidden_in.T
    full_in = ring_gather(hidden_t, "tp", tp_count)
    pieces = len(full_in)
    slots = jnp.asarray(sources(tp_count))[tp]

    seq_base = seq * toks
    run_starts, run_ends = tenant_bounds[:, 0], tenant_bounds[:, 1]
    places = seq_base + jnp.arange(toks, dtype=jnp.int32)
    tenant_ids = jnp.arange(tenants, dtype=jnp.int32)
    my_start = jnp.sum(
        jnp.where(seg_ids[:, None] == tenant_ids[None, :], run_starts[None, :], 0), axis=1
    )
    rel = (places - my_start)[None, :]
    live = pad_mask.astype(F32)[None, :]
    pad_block = jnp.pad(pad_mask.astype(F32).reshape(toks // 128, 128), ((0, 16 - toks // 128), (0, 0)))
    picks = jnp.concatenate(
        [jnp.clip(run_ends - 1 - seq_base, 0, toks - 1), jnp.full((1,), toks - 1, jnp.int32)]
    )
    firsts = jnp.concatenate([run_starts, my_start[-1:]]) - seq_base
    owned = ((run_ends - 1 >= seq_base) & (run_ends - 1 < seq_base + toks)).astype(jnp.int32)
    scal = jnp.concatenate(
        [
            jnp.pad(picks, (0, 8 - tenants - 1)),
            jnp.pad(firsts, (0, 8 - tenants - 1)),
            jnp.pad(owned, (0, 8 - tenants)),
        ]
    )
    head_table = jnp.pad(
        jnp.stack([dt_bias, decay_rate, skip_gain], axis=1), ((0, 8 - heads), (0, 128 - 3))
    )
    taps = jnp.pad(jnp.concatenate([conv_x, conv_bc], axis=1).T, ((0, 0), (0, 124)))

    w_in = (
        jnp.concatenate([w_xz[0], w_bc.T, w_xz[1], jnp.pad(w_dt, ((0, 8 - heads), (0, 0)))], axis=0)
        .astype(F32)
        * mamba_gain
    ).astype(BF16)
    w_att = (w_qkv.reshape(3 * att, width).astype(F32) * attn_gain).astype(BF16)

    w_rows = jnp.concatenate([(w_out.astype(F32) * inner_gain[:, None]).astype(BF16), w_o], axis=0)
    share = w_rows.shape[0] // seq_count
    mine = lax.dynamic_slice_in_dim(w_rows, seq * share, share, axis=0)
    mine = mine.reshape(share, tp_count, part).transpose(1, 0, 2)
    swapped = lax.all_to_all(mine, "tp", 0, 0, tiled=False)
    w_cols = lax.all_gather(swapped, "seq", axis=0, tiled=False)
    w_cols = w_cols.transpose(1, 0, 2, 3).reshape(tp_count, inner + att, part)
    w_out_t = w_cols[:, :inner].reshape(tp_count * inner, part).T
    w_o_t = w_cols[:, inner:].reshape(tp_count * att, part).T

    in_rows = conv_rows + inner + 8
    raw, z, dt_raw, tail = call(
        functools.partial(in_kernel, pieces, part, conv_rows, inner),
        (
            sds((conv_rows, toks), F32),
            sds((inner, toks), F32),
            sds((8, toks), F32),
            sds((8, conv_rows), F32),
        ),
        (slots, *full_in, w_in),
        smem=(0,),
        scratch=[pltpu.VMEM((width, toks), BF16), pltpu.VMEM((in_rows, toks), F32)],
        flops=2 * in_rows * width * toks,
    )
    halo = lax.ppermute(tail, "seq", [(i, i + 1) for i in range(seq_count - 1)])
    y, c_rows, entry, pay, local = call(
        functools.partial(mix_kernel, tenants, heads),
        (
            sds((inner, toks), F32),
            sds((bc // 2, toks), BF16),
            sds((8, toks), F32),
            sds((inner + 16, 128), BF16),
            sds((tenants * inner, 128), F32),
        ),
        (scal, raw, dt_raw, halo, taps, head_table, rel, live, pad_block),
        smem=(0,),
        scratch=[
            pltpu.VMEM((conv_rows, toks + 128), F32),
            pltpu.VMEM((conv_rows, toks), F32),
            pltpu.VMEM((inner, toks), F32),
        ],
        flops=10**9,
    )
    pays = [
        lax.ppermute(pay, "seq", [(i, i + by) for i in range(seq_count - by)])
        for by in range(1, seq_count)
    ]
    gated, tenant_part = call(
        functools.partial(gate_kernel, tenants, heads, len(pays)),
        (sds((inner, toks), BF16), sds((tenants * inner, bc // 2), BF16)),
        (scal, *pays, y, z, c_rows, entry, local),
        smem=(0,),
        flops=10**8,
    )
    tenant_states = (
        lax.psum(tenant_part, "seq")
        .astype(F32)
        .reshape(tenants, heads, inner // heads, bc // 2)
    )
    full_gated = ring_gather(gated, "tp", tp_count)
    mixed = call(
        functools.partial(mixed_kernel, len(full_gated), inner),
        sds((part, toks), BF16),
        (slots, *full_gated, w_out_t, hidden_t),
        smem=(0,),
        scratch=[pltpu.VMEM((tp_count * inner, toks), BF16)],
        flops=2 * part * tp_count * inner * toks,
    )
    full_mixed = ring_gather(mixed, "tp", tp_count)
    queries, kv = call(
        functools.partial(qkv_kernel, len(full_mixed), part),
        (sds((att, toks), BF16), sds((2 * att, toks), BF16)),
        (slots, *full_mixed, w_att),
        smem=(0,),
        scratch=[pltpu.VMEM((width, toks), BF16)],
        flops=6 * att * width * toks,
    )
    kv_cache = kv.reshape(2, att, toks)

    def pad_row(block):
        return block[inner : inner + toks // 128].astype(F32).reshape(1, toks)

    if seq_count == 4:
        near = lax.ppermute(kv, "seq", [(0, 1), (2, 3)])
        far = lax.ppermute(kv, "seq", [(0, 2), (1, 3)])
        other = lax.ppermute(far, "seq", [(2, 3), (3, 2)])
        buffers = [kv, near, far, other]
        odd = seq % 2
        block_ids = jnp.stack([seq, seq - 1 + 2 * (1 - odd), seq - 2, seq - 1 - 2 * odd])
        rows = [pad_row(p) for p in pays]
        pads = [live, rows[0], rows[1], jnp.where(odd > 0, rows[2], rows[0])]
    else:
        gathered = lax.all_gather(kv, "seq", axis=0, tiled=False)
        buffers = [gathered[i] for i in range(seq_count)]
        block_ids = jnp.arange(seq_count, dtype=jnp.int32)
        all_pads = lax.all_gather(live, "seq", axis=0, tiled=True)
        pads = [all_pads[i : i + 1] for i in range(seq_count)]
    blocks = len(buffers)
    pads = jnp.concatenate(pads, axis=0)
    wanted = (
        (block_ids >= 0) & (block_ids <= seq) & (block_ids * toks + toks > my_start[0])
    ).astype(jnp.int32)
    att_scal = jnp.concatenate(
        [
            jnp.full((16,), seq, jnp.int32),
            jnp.pad(block_ids.astype(jnp.int32), (0, 16 - blocks)),
            jnp.pad(wanted, (0, 16 - blocks)),
        ]
    )
    deep = att + 32
    context = call(
        functools.partial(attend_kernel, blocks, att ** (-0.5)),
        sds((att, toks), BF16),
        (att_scal, queries, *buffers, pads, rel),
        smem=(0,),
        scratch=[
            pltpu.VMEM((deep, toks), BF16),
            pltpu.VMEM((deep, toks), BF16),
            pltpu.VMEM((1, toks), F32),
            pltpu.VMEM((1, toks), F32),
            pltpu.VMEM((att, toks), F32),
        ],
        flops=4 * blocks * toks * toks * att,
    )
    full_context = ring_gather(context, "tp", tp_count)
    hidden_out = call(
        functools.partial(last_kernel, len(full_context), att),
        sds((toks, part), BF16),
        (slots, *full_context, w_o_t, mixed),
        smem=(0,),
        scratch=[pltpu.VMEM((tp_count * att, toks), BF16)],
        flops=2 * part * tp_count * att * toks,
    )
    return (hidden_out, kv_cache, tenant_states)


def solution(mesh):
    return jax.shard_map(
        functools.partial(on_device, mesh.shape["tp"], mesh.shape["seq"]),
        mesh=mesh,
        in_specs=(
            P("seq", "tp"),
            P(),
            P(None, "tp", None),
            P(),
            P("tp", None),
            P("tp"),
            P("tp"),
            P(None, "tp"),
            P(),
            P("tp"),
            P("tp"),
            P("tp", None),
            P(),
            P(None, "tp", None),
            P("tp", None),
            P("seq"),
            P("seq"),
            P(),
        ),
        out_specs=(P("seq", "tp"), P(None, "tp", "seq"), P(None, "tp", None, None)),
        check_vma=False,
    )
```

time: 447 us -> 293 us (0.66)
  waiting for transfers between devices: 279 us -> 139 us
  blocking collectives: 44.9 us -> 0 us
  starting transfers between devices: 16 us -> 58.1 us
  matrix products: 38 us -> 0 us
  local copies, waits for them, and re-layouts: 27.5 us -> 47.6 us
  Pallas kernels: 0 us -> 18.2 us
  other arithmetic: 24.2 us -> 14.7 us
    unnamed x7 -> x2, waiting for transfers between devices: 155 us -> 0.03 us
    all_gather x2 -> x1, waiting for transfers between devices: 122 us -> 0.01 us  [on_device(): w_cols = lax.all_gather(swapped, 'seq', axis=0, tiled=False)]
    ppermute x4 -> x39, waiting for transfers between devices: 1.75 us -> 83.9 us  [the longest x12 71.9 us: ring_gather(): one = lax.ppermute(one, axis, ahead)]
    dot_general x13 -> x0, matrix products: 38 us -> none  [the longest x3 14.3 us: times_rows(): lax.dot_general(left, weights, (((1,), (1,)), ((), ())), preferred_elemen...]
    psum x1, waiting for transfers between devices: 0.02 us -> 35.6 us  [on_device(): lax.psum(tenant_part, 'seq').astype(F32)]
    ppermute x4 -> x39, starting transfers between devices: 15.8 us -> 50.7 us  [the longest x12 22.9 us: ring_gather(): one = lax.ppermute(one, axis, ahead)]
    all_gather x3 -> x0, blocking collectives: 26 us -> none  [the longest x1 11.1 us: on_device(): lax.all_gather(key_rows, 'seq', axis=0, tiled=True)]
    all_to_all x0 -> x1, waiting for transfers between devices: none -> 19.4 us  [on_device(): swapped = lax.all_to_all(mine, 'tp', 0, 0, tiled=False)]
  transfers between devices with their start and end apart: 9 -> 42, of which waited for: 6 -> 22; matrix products, arithmetic and copies ran while one was open for 12% -> 12% of each run, Pallas kernels for 0% -> 3%
where the time goes in v1:
time: 293 us; the launch traced here: 292 us
  waiting for transfers between devices  139 us (47%)
  starting transfers between devices  58.1 us (20%)
  local copies, waits for them, and re-layouts  47.6 us (16%)
  Pallas kernels  18.2 us (6%)
  other arithmetic  14.7 us (5%)
  between operations  14.6 us (5%)
    ppermute x12, waiting for transfers between devices, ring_gather(): one = lax.ppermute(one, axis, ahead)  71.9 us
    psum x1, waiting for transfers between devices, on_device(): lax.psum(tenant_part, 'seq').astype(F32)  35.6 us
    unnamed x88, local copies, waits for them, and re-layouts  24.9 us
    ppermute x12, starting transfers between devices, ring_gather(): one = lax.ppermute(one, axis, ahead)  22.9 us
    all_to_all x1, waiting for transfers between devices, on_device(): swapped = lax.all_to_all(mine, 'tp', 0, 0, tiled=False)  19.4 us
    pallas_call x7, Pallas kernels, call(): pl.pallas_call(kernel, out_shape=out_shape, in_specs=specs, out_specs=jax...  18.2 us
    ppermute x3, starting transfers between devices, on_device(): lax.ppermute(pay, 'seq', [(i, i + by) for i in range(seq_count - by)])  8.89 us
    all_to_all x1, starting transfers between devices, on_device(): swapped = lax.all_to_all(mine, 'tp', 0, 0, tiled=False)  7.28 us
  transfers between devices with their start and end apart: 42, of which 22 were waited for; matrix products, arithmetic and copies ran while one was open for 12% of the time, Pallas kernels for 3%

profile of v1, /device:TPU:0, one launch (start us, length us, event | category | flops | bytes accessed | tf_op | source)
XLA Modules:
  0.0 292.0 jit_solution(8598911979801174628)
XLA Ops:
  7.2 1.8 multiply_convert_fusion.1
  10.4 1.2 copy.75
  11.5 7.3 %all-to-all-start = ((bf16[8,104,448]{2,1,0:T(8,128)(2,1)}), bf16[8,104,448]{2,1,0:T(8,128)(2,1)S(1)}, u32[]{:S(2)}, u32[]{:S(2)}) async-start(bf16[8,104,448]{2,1,0:T(8,128)(2,1)} %copy.75), calls=%async_computation | async-start | bytes 1703936 | tf_op jit(solution)/shard_map/all_to_all | solution.py:404
  18.9 2.0 collective-permute-start
  21.0 1.5 copy.70
  22.5 19.4 %all-to-all-done = bf16[8,104,448]{2,1,0:T(8,128)(2,1)S(1)} async-done(((bf16[8,104,448]{2,1,0:T(8,128)(2,1)}), bf16[8,104,448]{2,1,0:T(8,128)(2,1)S(1)}, u32[]{:S(2)}, u32[]{:S(2)}) %all-to-all-start) | async-done | bytes 745504 | tf_op jit(solution)/shard_map/all_to_all | solution.py:404
  42.8 1.9 slice_bitcast_fusion.1
  44.9 2.3 multiply_convert_fusion.refs_10_
  47.2 1.4 collective-permute-start.2
  50.7 7.7 %collective-permute-done.2.refs_4_ = bf16[448,512]{1,0:T(8,128)(2,1)S(1)} collective-permute-done((bf16[448,512]{1,0:T(8,128)(2,1)S(1)}, bf16[448,512]{1,0:T(8,128)(2,1)S(1)}, u32[]{:S(2)}, u32[]{:S(2)}) %collective-permute-start.2) | collective-permute-done | bytes 458784 | tf_op jit(solution)/shard_map/ppermute | solution.py:53
  58.4 2.5 collective-permute-start.4
  62.4 8.7 %collective-permute-done.4.refs_6_ = bf16[448,512]{1,0:T(8,128)(2,1)S(1)} collective-permute-done((bf16[448,512]{1,0:T(8,128)(2,1)S(1)}, bf16[448,512]{1,0:T(8,128)(2,1)S(1)}, u32[]{:S(2)}, u32[]{:S(2)}) %collective-permute-start.4) | collective-permute-done | bytes 458784 | tf_op jit(solution)/shard_map/ppermute | solution.py:53
  71.2 1.3 collective-permute-start.6
  74.0 3.2 %collective-permute-done.6.refs_8_ = bf16[224,512]{1,0:T(8,128)(2,1)S(1)} collective-permute-done((bf16[224,512]{1,0:T(8,128)(2,1)S(1)}, bf16[224,512]{1,0:T(8,128)(2,1)S(1)}, u32[]{:S(2)}, u32[]{:S(2)}) %collective-permute-start.6) | collective-permute-done | bytes 229408 | tf_op jit(solution)/shard_map/ppermute | solution.py:59
  77.2 1.7 collective-permute-done.7.refs_9_
  79.0 2.1 copy-done
  81.0 3.4 %shard_map.202 = (f32[320,512]{1,0:T(8,128)S(1)}, f32[192,512]{1,0:T(8,128)S(1)}, f32[8,512]{1,0:T(8,128)S(1)}, f32[8,320]{1,0:T(8,128)S(1)}) custom-call(s32[8]{0:T(128)S(1)} %fusion.4.refs_0_, bf16[448,512]{1,0:T(8,128)(2,1)S(1)} %bitcast.48, bf16[448,512]{1,0:T(8,128)(2,1)S(1)} %collective-permute-done.refs_2_, ...), custom_call_target="tpu_custom_call" | custom-call | flops 1908408320 | bytes 7397408 | tf_op jit(solution)/shard_map/pallas_call | solution.py:96
  86.1 1.4 collective-permute-start.8
  88.3 1.1 copy-done.24
  89.4 3.2 %shard_map.203 = (f32[192,512]{1,0:T(8,128)S(1)}, bf16[64,512]{1,0:T(8,128)(2,1)S(1)}, f32[8,512]{1,0:T(8,128)S(1)}, bf16[208,128]{1,0:T(8,128)(2,1)S(1)}, f32[768,128]{1,0:T(8,128)S(1)}) custom-call(s32[24]{0:T(128)S(1)} %fusion.5.scal_ref.refs_0_, f32[320,512]{1,0:T(8,128)S(1)} %copy-done.24, f32[8,512]{1,0:T(8,128)S(1)} %get-tuple-element.17.dt_ref, ...), custom_call_target="tpu_custom_call" | custom-call | flops 1000000000 | bytes 862304 | tf_op jit(solution)/shard_map/pallas_call | solution.py:96
  92.5 4.1 %collective-permute-start.9 = (bf16[208,128]{1,0:T(8,128)(2,1)S(1)}, bf16[208,128]{1,0:T(8,128)(2,1)S(1)}, u32[]{:S(2)}, u32[]{:S(2)}) collective-permute-start(bf16[208,128]{1,0:T(8,128)(2,1)S(1)} %get-tuple-element.19), channel_id=1, source_target_pairs={{0,8},{8,16},{16,24},{1,9},{9,17},{17,25},{2,10},{10,18},{18,26},{... | collective-permute-start | bytes 159752 | tf_op jit(solution)/shard_map/ppermute | solution.py:444
  96.7 1.3 collective-permute-start.11
  98.0 3.5 %collective-permute-start.10 = (bf16[208,128]{1,0:T(8,128)(2,1)S(1)}, bf16[208,128]{1,0:T(8,128)(2,1)S(1)}, u32[]{:S(2)}, u32[]{:S(2)}) collective-permute-start(bf16[208,128]{1,0:T(8,128)(2,1)S(1)} %get-tuple-element.19), channel_id=1, source_target_pairs={{0,16},{8,24},{1,17},{9,25},{2,18},{10,26},{3,19},{11,27},{4,20},{... | collective-permute-start | bytes 159752 | tf_op jit(solution)/shard_map/ppermute | solution.py:444
  101.5 1.7 collective-permute-done.10.refs_2_
  103.2 1.6 shard_map.204
  104.8 2.0 collective-permute-start.12
  106.8 3.7 %collective-permute-done.12.refs_2_ = bf16[192,512]{1,0:T(8,128)(2,1)S(1)} collective-permute-done((bf16[192,512]{1,0:T(8,128)(2,1)S(1)}, bf16[192,512]{1,0:T(8,128)(2,1)S(1)}, u32[]{:S(2)}, u32[]{:S(2)}) %collective-permute-start.12) | collective-permute-done | bytes 196640 | tf_op jit(solution)/shard_map/ppermute | solution.py:53
  110.5 2.0 collective-permute-start.14
  112.5 4.4 %collective-permute-done.14.refs_4_ = bf16[192,512]{1,0:T(8,128)(2,1)S(1)} collective-permute-done((bf16[192,512]{1,0:T(8,128)(2,1)S(1)}, bf16[192,512]{1,0:T(8,128)(2,1)S(1)}, u32[]{:S(2)}, u32[]{:S(2)}) %collective-permute-start.14) | collective-permute-done | bytes 196640 | tf_op jit(solution)/shard_map/ppermute | solution.py:53
  117.0 2.0 collective-permute-start.16
  119.0 4.4 %collective-permute-done.16.refs_6_ = bf16[192,512]{1,0:T(8,128)(2,1)S(1)} collective-permute-done((bf16[192,512]{1,0:T(8,128)(2,1)S(1)}, bf16[192,512]{1,0:T(8,128)(2,1)S(1)}, u32[]{:S(2)}, u32[]{:S(2)}) %collective-permute-start.16) | collective-permute-done | bytes 196640 | tf_op jit(solution)/shard_map/ppermute | solution.py:53
  124.1 2.3 collective-permute-start.18
  127.0 4.0 %copy.76 = bf16[8,4,104,448]{3,2,1,0:T(8,128)(2,1)} copy(bf16[8,4,104,448]{3,2,0,1:T(8,128)(2,1)} %bitcast.57) | data formatting | bytes 5963776 | tf_op jit(solution)/shard_map/transpose | solution.py:406
  131.1 2.7 slice.80
  133.8 1.7 copy.77
  138.9 1.7 shard_map.205.refs_1_.refs_11_
  140.7 2.1 collective-permute-start.20
  142.7 10.9 %collective-permute-done.20.refs_2_ = bf16[448,512]{1,0:T(8,128)(2,1)S(1)} collective-permute-done((bf16[448,512]{1,0:T(8,128)(2,1)S(1)}, bf16[448,512]{1,0:T(8,128)(2,1)S(1)}, u32[]{:S(2)}, u32[]{:S(2)}) %collective-permute-start.20) | collective-permute-done | bytes 458784 | tf_op jit(solution)/shard_map/ppermute | solution.py:53
  153.7 2.3 collective-permute-start.22
  156.0 10.6 %collective-permute-done.22.refs_4_ = bf16[448,512]{1,0:T(8,128)(2,1)S(1)} collective-permute-done((bf16[448,512]{1,0:T(8,128)(2,1)S(1)}, bf16[448,512]{1,0:T(8,128)(2,1)S(1)}, u32[]{:S(2)}, u32[]{:S(2)}) %collective-permute-start.22) | collective-permute-done | bytes 458784 | tf_op jit(solution)/shard_map/ppermute | solution.py:53
  166.6 2.0 collective-permute-start.24
  168.8 8.5 %collective-permute-done.24.refs_6_ = bf16[448,512]{1,0:T(8,128)(2,1)S(1)} collective-permute-done((bf16[448,512]{1,0:T(8,128)(2,1)S(1)}, bf16[448,512]{1,0:T(8,128)(2,1)S(1)}, u32[]{:S(2)}, u32[]{:S(2)}) %collective-permute-start.24) | collective-permute-done | bytes 458784 | tf_op jit(solution)/shard_map/ppermute | solution.py:53
  178.0 1.8 collective-permute-start.26
  180.7 5.4 %fusion.refs_10_ = bf16[672,3584]{1,0:T(8,128)(2,1)} fusion(bf16[3,224,3584]{2,1,0:T(8,128)(2,1)} %param.32, f32[3584]{0:T(1024)S(1)} %copy-done.34), kind=kLoop, calls=%fused_computation.1 | loop fusion | flops 7225344 | bytes 9648128 | tf_op jit(solution)/shard_map/convert_element_type | solution.py:398
  186.9 2.4 copy-done.1
  189.2 1.0 copy-done.27
  190.2 4.7 %shard_map.206 = (bf16[224,512]{1,0:T(8,128)(2,1)S(1)}, bf16[448,512]{1,0:T(8,128)(2,1)}) custom-call(s32[8]{0:T(128)S(1)} %fusion.4.refs_0_, bf16[448,512]{1,0:T(8,128)(2,1)S(1)} %shard_map.205.refs_1_.refs_11_, bf16[448,512]{1,0:T(8,128)(2,1)S(1)} %collective-permute-done.20.refs_2_, bf16[448,512]{1,0:T(8,128)(2,1)S(1)} %collective-permute-done.21.refs_3_, ...), custom_call_target="tpu_custom_call" | custom-call | flops 2466250752 | bytes 8486944 | tf_op jit(solution)/shard_map/pallas_call | solution.py:96
  195.6 4.2 %collective-permute-start.29 = (bf16[448,512]{1,0:T(8,128)(2,1)}, bf16[448,512]{1,0:T(8,128)(2,1)S(1)}, u32[]{:S(2)}, u32[]{:S(2)}) collective-permute-start(bf16[448,512]{1,0:T(8,128)(2,1)} %get-tuple-element.27.refs_2_), channel_id=1, source_target_pairs={{0,16},{8,24},{1,17},{9,25},{2,18},{10,26},{3,19},{11,27},{4,20},{... | collective-permute-start | bytes 1376264 | tf_op jit(solution)/shard_map/ppermute | solution.py:484
  201.3 1.3 collective-permute-start.28
  202.6 3.5 %collective-permute-done.29.refs_4_ = bf16[448,512]{1,0:T(8,128)(2,1)S(1)} collective-permute-done((bf16[448,512]{1,0:T(8,128)(2,1)}, bf16[448,512]{1,0:T(8,128)(2,1)S(1)}, u32[]{:S(2)}, u32[]{:S(2)}) %collective-permute-start.29) | collective-permute-done | bytes 458784 | tf_op jit(solution)/shard_map/ppermute | solution.py:484
  206.9 1.0 copy-done.25
  208.9 1.5 shard_map.207.refs_1_
  210.4 1.6 collective-permute-start.31
  212.4 4.0 %collective-permute-done.31.refs_2_ = bf16[224,512]{1,0:T(8,128)(2,1)S(1)} collective-permute-done((bf16[224,512]{1,0:T(8,128)(2,1)S(1)}, bf16[224,512]{1,0:T(8,128)(2,1)S(1)}, u32[]{:S(2)}, u32[]{:S(2)}) %collective-permute-start.31) | collective-permute-done | bytes 229408 | tf_op jit(solution)/shard_map/ppermute | solution.py:53
  216.4 1.5 collective-permute-start.33
  219.2 4.4 %collective-permute-done.33.refs_4_ = bf16[224,512]{1,0:T(8,128)(2,1)S(1)} collective-permute-done((bf16[224,512]{1,0:T(8,128)(2,1)S(1)}, bf16[224,512]{1,0:T(8,128)(2,1)S(1)}, u32[]{:S(2)}, u32[]{:S(2)}) %collective-permute-start.33) | collective-permute-done | bytes 229408 | tf_op jit(solution)/shard_map/ppermute | solution.py:53
  223.6 1.5 collective-permute-start.35
  226.3 4.5 %collective-permute-done.35.refs_6_ = bf16[224,512]{1,0:T(8,128)(2,1)S(1)} collective-permute-done((bf16[224,512]{1,0:T(8,128)(2,1)S(1)}, bf16[224,512]{1,0:T(8,128)(2,1)S(1)}, u32[]{:S(2)}, u32[]{:S(2)}) %collective-permute-start.35) | collective-permute-done | bytes 229408 | tf_op jit(solution)/shard_map/ppermute | solution.py:53
  230.8 1.6 collective-permute-start.37
  233.2 35.6 %all-reduce.11.cloned.1.call-done = bf16[4,3,64,64]{3,2,1,0:T(8,128)(2,1)} async-done(((bf16[4,3,64,64]{3,2,1,0:T(8,128)(2,1)}), bf16[4,3,64,64]{3,2,1,0:T(8,128)(2,1)}) %all-reduce.11.cloned.1.call-update) | async-done | bytes 98320 | tf_op jit(solution)/shard_map/psum | solution.py:455
  268.9 1.7 reshape.117
  270.6 2.9 slice.88
  273.4 2.8 copy.80
  282.2 2.1 shard_map.208
  (165 shorter events, 31.9 us)
Async XLA Ops:
  7.2 1.8 copy-start.31
  9.3 9.5 %copy-start.2 = (bf16[512,448]{0,1:T(8,128)(2,1)S(1)}, bf16[512,448]{0,1:T(8,128)(2,1)}, u32[]{:S(2)}) copy-start(bf16[512,448]{0,1:T(8,128)(2,1)} %param.19) | copy-start | bytes 1376260
  11.5 30.3 %all-to-all-start = ((bf16[8,104,448]{2,1,0:T(8,128)(2,1)}), bf16[8,104,448]{2,1,0:T(8,128)(2,1)S(1)}, u32[]{:S(2)}, u32[]{:S(2)}) async-start(bf16[8,104,448]{2,1,0:T(8,128)(2,1)} %copy.75), calls=%async_computation | async-start | bytes 1703936 | tf_op jit(solution)/shard_map/all_to_all | solution.py:404
  18.8 108.2 %all-gather.3.cloned.1.call-start = ((), (), s32[]{:S(2)}) async-start(), calls=%async_computation.2 | async-start | bytes 4259840 | tf_op jit(solution)/shard_map/all_gather | solution.py:405
  18.9 28.3 %collective-permute-start = (bf16[448,512]{1,0:T(8,128)(2,1)S(1)}, bf16[448,512]{1,0:T(8,128)(2,1)S(1)}, u32[]{:S(2)}, u32[]{:S(2)}) collective-permute-start(bf16[448,512]{1,0:T(8,128)(2,1)S(1)} %bitcast.46), channel_id=1, source_target_pairs={{0,2},{2,4},{4,6},{6,7},{7,5},{5,3},{3,1},{1,0},{8,10},{10,12},{12... | collective-permute-start | bytes 1376264 | tf_op jit(solution)/shard_map/ppermute | solution.py:53
  20.9 27.7 %collective-permute-start.1 = (bf16[448,512]{1,0:T(8,128)(2,1)S(1)}, bf16[448,512]{1,0:T(8,128)(2,1)S(1)}, u32[]{:S(2)}, u32[]{:S(2)}) collective-permute-start(bf16[448,512]{1,0:T(8,128)(2,1)S(1)} %bitcast.47), channel_id=1, source_target_pairs={{0,1},{2,0},{4,2},{6,4},{7,6},{5,7},{3,5},{1,3},{8,9},{10,8},{12,1... | collective-permute-start | bytes 1376264 | tf_op jit(solution)/shard_map/ppermute | solution.py:54
  22.4 22.4 %copy-start.32 = (bf16[3,3584]{1,0:T(4,128)(2,1)S(1)}, bf16[3,3584]{1,0:T(4,128)(2,1)}, u32[]{:S(2)}) copy-start(bf16[3,3584]{1,0:T(4,128)(2,1)} %param.23) | copy-start | bytes 64516
  22.4 22.4 %copy-start.33 = (f32[3584]{0:T(1024)S(1)}, f32[3584]{0:T(1024)}, u32[]{:S(2)}) copy-start(f32[3584]{0:T(1024)} %param.20) | copy-start | bytes 43012
  42.8 226.1 %all-reduce.11.cloned.1.call-start = ((), (), s32[]{:S(2)}) async-start(), calls=%async_computation.1 | async-start | bytes 393216 | tf_op jit(solution)/shard_map/psum | solution.py:455
  44.8 2.4 copy-start.36
  44.8 4.5 %copy-start.38 = (s32[512]{0:T(512)S(1)}, s32[512]{0:T(512)}, u32[]{:S(2)}) copy-start(s32[512]{0:T(512)} %param.34) | copy-start | bytes 6148
  44.8 17.1 %copy-start.40 = (f32[3]{0:T(128)S(1)}, f32[3]{0:T(128)}, u32[]{:S(2)}) copy-start(f32[3]{0:T(128)} %param.24) | copy-start | bytes 40
  44.8 17.2 %copy-start.41 = (f32[3]{0:T(128)S(1)}, f32[3]{0:T(128)}, u32[]{:S(2)}) copy-start(f32[3]{0:T(128)} %param.25) | copy-start | bytes 40
  44.9 17.3 %copy-start.42 = (f32[3]{0:T(128)S(1)}, f32[3]{0:T(128)}, u32[]{:S(2)}) copy-start(f32[3]{0:T(128)} %param.28) | copy-start | bytes 40
  44.9 17.4 %copy-start.35 = (f32[4,192]{1,0:T(4,128)S(1)}, f32[4,192]{1,0:T(4,128)}, u32[]{:S(2)}) copy-start(f32[4,192]{1,0:T(4,128)} %param.26) | copy-start | bytes 9220
  44.9 17.4 %copy-start.39 = (f32[4,128]{1,0:T(4,128)S(1)}, f32[4,128]{1,0:T(4,128)}, u32[]{:S(2)}) copy-start(f32[4,128]{1,0:T(4,128)} %param.27) | copy-start | bytes 6148
  44.9 29.1 %copy-start.37 = (s32[512]{0:T(512)S(1)}, s32[512]{0:T(512)}, u32[]{:S(2)}) copy-start(s32[512]{0:T(512)} %param.35) | copy-start | bytes 6148
  47.2 11.2 %collective-permute-start.2 = (bf16[448,512]{1,0:T(8,128)(2,1)S(1)}, bf16[448,512]{1,0:T(8,128)(2,1)S(1)}, u32[]{:S(2)}, u32[]{:S(2)}) collective-permute-start(bf16[448,512]{1,0:T(8,128)(2,1)S(1)} %collective-permute-done.refs_2_), channel_id=1, source_target_pairs={{0,2},{2,4},{4,6},{6,7},{7,5},{5,3},{3,1},{1,0},{8,10},{10,12},{12... | collective-permute-start | bytes 1376264 | tf_op jit(solution)/shard_map/ppermute | solution.py:53
  48.6 12.7 %collective-permute-start.3 = (bf16[448,512]{1,0:T(8,128)(2,1)S(1)}, bf16[448,512]{1,0:T(8,128)(2,1)S(1)}, u32[]{:S(2)}, u32[]{:S(2)}) collective-permute-start(bf16[448,512]{1,0:T(8,128)(2,1)S(1)} %collective-permute-done.1.refs_3_), channel_id=1, source_target_pairs={{0,1},{2,0},{4,2},{6,4},{7,6},{5,7},{3,5},{1,3},{8,9},{10,8},{12,1... | collective-permute-start | bytes 1376264 | tf_op jit(solution)/shard_map/ppermute | solution.py:54
  58.4 12.8 %collective-permute-start.4 = (bf16[448,512]{1,0:T(8,128)(2,1)S(1)}, bf16[448,512]{1,0:T(8,128)(2,1)S(1)}, u32[]{:S(2)}, u32[]{:S(2)}) collective-permute-start(bf16[448,512]{1,0:T(8,128)(2,1)S(1)} %collective-permute-done.2.refs_4_), channel_id=1, source_target_pairs={{0,2},{2,4},{4,6},{6,7},{7,5},{5,3},{3,1},{1,0},{8,10},{10,12},{12... | collective-permute-start | bytes 1376264 | tf_op jit(solution)/shard_map/ppermute | solution.py:53
  61.3 11.5 %collective-permute-start.5 = (bf16[448,512]{1,0:T(8,128)(2,1)S(1)}, bf16[448,512]{1,0:T(8,128)(2,1)S(1)}, u32[]{:S(2)}, u32[]{:S(2)}) collective-permute-start(bf16[448,512]{1,0:T(8,128)(2,1)S(1)} %collective-permute-done.3.refs_5_), channel_id=1, source_target_pairs={{0,1},{2,0},{4,2},{6,4},{7,6},{5,7},{3,5},{1,3},{8,9},{10,8},{12,1... | collective-permute-start | bytes 1376264 | tf_op jit(solution)/shard_map/ppermute | solution.py:54
  71.2 6.1 %collective-permute-start.6 = (bf16[224,512]{1,0:T(8,128)(2,1)S(1)}, bf16[224,512]{1,0:T(8,128)(2,1)S(1)}, u32[]{:S(2)}, u32[]{:S(2)}) collective-permute-start(bf16[224,512]{1,0:T(8,128)(2,1)S(1)} %slice.76), channel_id=1, source_target_pairs={{0,2},{2,4},{4,6},{6,7},{7,5},{5,3},{3,1},{1,0},{8,10},{10,12},{12... | collective-permute-start | bytes 688136 | tf_op jit(solution)/shard_map/ppermute | solution.py:59
  72.8 6.1 %collective-permute-start.7 = (bf16[224,512]{1,0:T(8,128)(2,1)S(1)}, bf16[224,512]{1,0:T(8,128)(2,1)S(1)}, u32[]{:S(2)}, u32[]{:S(2)}) collective-permute-start(bf16[224,512]{1,0:T(8,128)(2,1)S(1)} %slice.77), channel_id=1, source_target_pairs={{0,1},{2,0},{4,2},{6,4},{7,6},{5,7},{3,5},{1,3},{8,9},{10,8},{12,1... | collective-permute-start | bytes 688136 | tf_op jit(solution)/shard_map/ppermute | solution.py:60
  79.0 2.1 copy-start
  86.0 17.2 %copy-start.4 = (f32[192,512]{1,0:T(8,128)S(1)}, f32[192,512]{1,0:T(8,128)}, u32[]{:S(2)}) copy-start(f32[192,512]{1,0:T(8,128)} %copy-done.3) | copy-start | bytes 1179652
  86.1 2.2 collective-permute-start.8
  92.5 8.9 %collective-permute-start.9 = (bf16[208,128]{1,0:T(8,128)(2,1)S(1)}, bf16[208,128]{1,0:T(8,128)(2,1)S(1)}, u32[]{:S(2)}, u32[]{:S(2)}) collective-permute-start(bf16[208,128]{1,0:T(8,128)(2,1)S(1)} %get-tuple-element.19), channel_id=1, source_target_pairs={{0,8},{8,16},{16,24},{1,9},{9,17},{17,25},{2,10},{10,18},{18,26},{... | collective-permute-start | bytes 159752 | tf_op jit(solution)/shard_map/ppermute | solution.py:444
  96.7 4.8 %collective-permute-start.11 = (bf16[208,128]{1,0:T(8,128)(2,1)S(1)}, bf16[208,128]{1,0:T(8,128)(2,1)S(1)}, u32[]{:S(2)}, u32[]{:S(2)}) collective-permute-start(bf16[208,128]{1,0:T(8,128)(2,1)S(1)} %get-tuple-element.19), channel_id=1, source_target_pairs={{0,24},{1,25},{2,26},{3,27},{4,28},{5,29},{6,30},{7,31}} | collective-permute-start | bytes 159752 | tf_op jit(solution)/shard_map/ppermute | solution.py:444
  98.0 5.2 %collective-permute-start.10 = (bf16[208,128]{1,0:T(8,128)(2,1)S(1)}, bf16[208,128]{1,0:T(8,128)(2,1)S(1)}, u32[]{:S(2)}, u32[]{:S(2)}) collective-permute-start(bf16[208,128]{1,0:T(8,128)(2,1)S(1)} %get-tuple-element.19), channel_id=1, source_target_pairs={{0,16},{8,24},{1,17},{9,25},{2,18},{10,26},{3,19},{11,27},{4,20},{... | collective-permute-start | bytes 159752 | tf_op jit(solution)/shard_map/ppermute | solution.py:444
  101.5 24.9 %copy-start.21 = (bf16[208,128]{1,0:T(8,128)(2,1)}, bf16[208,128]{1,0:T(8,128)(2,1)S(1)}, u32[]{:S(2)}) copy-start(bf16[208,128]{1,0:T(8,128)(2,1)S(1)} %collective-permute-done.9.refs_1_) | copy-start | bytes 159748
  101.5 25.5 %copy-start.22 = (bf16[208,128]{1,0:T(8,128)(2,1)}, bf16[208,128]{1,0:T(8,128)(2,1)S(1)}, u32[]{:S(2)}) copy-start(bf16[208,128]{1,0:T(8,128)(2,1)S(1)} %collective-permute-done.11.refs_3_) | copy-start | bytes 159748
  104.8 5.7 %collective-permute-start.12 = (bf16[192,512]{1,0:T(8,128)(2,1)S(1)}, bf16[192,512]{1,0:T(8,128)(2,1)S(1)}, u32[]{:S(2)}, u32[]{:S(2)}) collective-permute-start(bf16[192,512]{1,0:T(8,128)(2,1)S(1)} %get-tuple-element.25.refs_1_), channel_id=1, source_target_pairs={{0,2},{2,4},{4,6},{6,7},{7,5},{5,3},{3,1},{1,0},{8,10},{10,12},{12... | collective-permute-start | bytes 589832 | tf_op jit(solution)/shard_map/ppermute | solution.py:53
  106.8 5.7 %collective-permute-start.13 = (bf16[192,512]{1,0:T(8,128)(2,1)S(1)}, bf16[192,512]{1,0:T(8,128)(2,1)S(1)}, u32[]{:S(2)}, u32[]{:S(2)}) collective-permute-start(bf16[192,512]{1,0:T(8,128)(2,1)S(1)} %get-tuple-element.25.refs_1_), channel_id=1, source_target_pairs={{0,1},{2,0},{4,2},{6,4},{7,6},{5,7},{3,5},{1,3},{8,9},{10,8},{12,1... | collective-permute-start | bytes 589832 | tf_op jit(solution)/shard_map/ppermute | solution.py:54
  110.5 6.5 %collective-permute-start.14 = (bf16[192,512]{1,0:T(8,128)(2,1)S(1)}, bf16[192,512]{1,0:T(8,128)(2,1)S(1)}, u32[]{:S(2)}, u32[]{:S(2)}) collective-permute-start(bf16[192,512]{1,0:T(8,128)(2,1)S(1)} %collective-permute-done.12.refs_2_), channel_id=1, source_target_pairs={{0,2},{2,4},{4,6},{6,7},{7,5},{5,3},{3,1},{1,0},{8,10},{10,12},{12... | collective-permute-start | bytes 589832 | tf_op jit(solution)/shard_map/ppermute | solution.py:53
  112.5 6.5 %collective-permute-start.15 = (bf16[192,512]{1,0:T(8,128)(2,1)S(1)}, bf16[192,512]{1,0:T(8,128)(2,1)S(1)}, u32[]{:S(2)}, u32[]{:S(2)}) collective-permute-start(bf16[192,512]{1,0:T(8,128)(2,1)S(1)} %collective-permute-done.13.refs_3_), channel_id=1, source_target_pairs={{0,1},{2,0},{4,2},{6,4},{7,6},{5,7},{3,5},{1,3},{8,9},{10,8},{12,1... | collective-permute-start | bytes 589832 | tf_op jit(solution)/shard_map/ppermute | solution.py:54
  117.0 14.1 %copy-start.11 = (bf16[192,512]{1,0:T(8,128)(2,1)}, bf16[192,512]{1,0:T(8,128)(2,1)S(1)}, u32[]{:S(2)}) copy-start(bf16[192,512]{1,0:T(8,128)(2,1)S(1)} %collective-permute-done.14.refs_4_) | copy-start | bytes 589828
  117.0 6.4 %collective-permute-start.16 = (bf16[192,512]{1,0:T(8,128)(2,1)S(1)}, bf16[192,512]{1,0:T(8,128)(2,1)S(1)}, u32[]{:S(2)}, u32[]{:S(2)}) collective-permute-start(bf16[192,512]{1,0:T(8,128)(2,1)S(1)} %collective-permute-done.14.refs_4_), channel_id=1, source_target_pairs={{0,2},{2,4},{4,6},{6,7},{7,5},{5,3},{3,1},{1,0},{8,10},{10,12},{12... | collective-permute-start | bytes 589832 | tf_op jit(solution)/shard_map/ppermute | solution.py:53
  119.0 12.1 %copy-start.13 = (bf16[192,512]{1,0:T(8,128)(2,1)}, bf16[192,512]{1,0:T(8,128)(2,1)S(1)}, u32[]{:S(2)}) copy-start(bf16[192,512]{1,0:T(8,128)(2,1)S(1)} %collective-permute-done.15.refs_5_) | copy-start | bytes 589828
  119.0 7.4 %collective-permute-start.17 = (bf16[192,512]{1,0:T(8,128)(2,1)S(1)}, bf16[192,512]{1,0:T(8,128)(2,1)S(1)}, u32[]{:S(2)}, u32[]{:S(2)}) collective-permute-start(bf16[192,512]{1,0:T(8,128)(2,1)S(1)} %collective-permute-done.15.refs_5_), channel_id=1, source_target_pairs={{0,1},{2,0},{4,2},{6,4},{7,6},{5,7},{3,5},{1,3},{8,9},{10,8},{12,1... | collective-permute-start | bytes 589832 | tf_op jit(solution)/shard_map/ppermute | solution.py:54
  124.1 11.4 %collective-permute-start.18 = (bf16[96,512]{1,0:T(8,128)(2,1)}, bf16[96,512]{1,0:T(8,128)(2,1)S(1)}, u32[]{:S(2)}, u32[]{:S(2)}) collective-permute-start(bf16[96,512]{1,0:T(8,128)(2,1)} %slice.78), channel_id=1, source_target_pairs={{0,2},{2,4},{4,6},{6,7},{7,5},{5,3},{3,1},{1,0},{8,10},{10,12},{12... | collective-permute-start | bytes 294920 | tf_op jit(solution)/shard_map/ppermute | solution.py:59
  127.0 8.5 %collective-permute-start.19 = (bf16[96,512]{1,0:T(8,128)(2,1)}, bf16[96,512]{1,0:T(8,128)(2,1)S(1)}, u32[]{:S(2)}, u32[]{:S(2)}) collective-permute-start(bf16[96,512]{1,0:T(8,128)(2,1)} %slice.79), channel_id=1, source_target_pairs={{0,1},{2,0},{4,2},{6,4},{7,6},{5,7},{3,5},{1,3},{8,9},{10,8},{12,1... | collective-permute-start | bytes 294920 | tf_op jit(solution)/shard_map/ppermute | solution.py:60
  133.8 46.9 %copy-start.34 = (f32[3584]{0:T(1024)S(1)}, f32[3584]{0:T(1024)}, u32[]{:S(2)}) copy-start(f32[3584]{0:T(1024)} %param.31) | copy-start | bytes 43012
  140.7 13.0 %collective-permute-start.20 = (bf16[448,512]{1,0:T(8,128)(2,1)S(1)}, bf16[448,512]{1,0:T(8,128)(2,1)S(1)}, u32[]{:S(2)}, u32[]{:S(2)}) collective-permute-start(bf16[448,512]{1,0:T(8,128)(2,1)S(1)} %shard_map.205.refs_1_.refs_11_), channel_id=1, source_target_pairs={{0,2},{2,4},{4,6},{6,7},{7,5},{5,3},{3,1},{1,0},{8,10},{10,12},{12... | collective-permute-start | bytes 1376264 | tf_op jit(solution)/shard_map/ppermute | solution.py:53
  142.7 13.3 %collective-permute-start.21 = (bf16[448,512]{1,0:T(8,128)(2,1)S(1)}, bf16[448,512]{1,0:T(8,128)(2,1)S(1)}, u32[]{:S(2)}, u32[]{:S(2)}) collective-permute-start(bf16[448,512]{1,0:T(8,128)(2,1)S(1)} %shard_map.205.refs_1_.refs_11_), channel_id=1, source_target_pairs={{0,1},{2,0},{4,2},{6,4},{7,6},{5,7},{3,5},{1,3},{8,9},{10,8},{12,1... | collective-permute-start | bytes 1376264 | tf_op jit(solution)/shard_map/ppermute | solution.py:54
  153.7 13.0 %collective-permute-start.22 = (bf16[448,512]{1,0:T(8,128)(2,1)S(1)}, bf16[448,512]{1,0:T(8,128)(2,1)S(1)}, u32[]{:S(2)}, u32[]{:S(2)}) collective-permute-start(bf16[448,512]{1,0:T(8,128)(2,1)S(1)} %collective-permute-done.20.refs_2_), channel_id=1, source_target_pairs={{0,2},{2,4},{4,6},{6,7},{7,5},{5,3},{3,1},{1,0},{8,10},{10,12},{12... | collective-permute-start | bytes 1376264 | tf_op jit(solution)/shard_map/ppermute | solution.py:53
  156.0 12.6 %collective-permute-start.23 = (bf16[448,512]{1,0:T(8,128)(2,1)S(1)}, bf16[448,512]{1,0:T(8,128)(2,1)S(1)}, u32[]{:S(2)}, u32[]{:S(2)}) collective-permute-start(bf16[448,512]{1,0:T(8,128)(2,1)S(1)} %collective-permute-done.21.refs_3_), channel_id=1, source_target_pairs={{0,1},{2,0},{4,2},{6,4},{7,6},{5,7},{3,5},{1,3},{8,9},{10,8},{12,1... | collective-permute-start | bytes 1376264 | tf_op jit(solution)/shard_map/ppermute | solution.py:54
  166.6 10.7 %collective-permute-start.24 = (bf16[448,512]{1,0:T(8,128)(2,1)S(1)}, bf16[448,512]{1,0:T(8,128)(2,1)S(1)}, u32[]{:S(2)}, u32[]{:S(2)}) collective-permute-start(bf16[448,512]{1,0:T(8,128)(2,1)S(1)} %collective-permute-done.22.refs_4_), channel_id=1, source_target_pairs={{0,2},{2,4},{4,6},{6,7},{7,5},{5,3},{3,1},{1,0},{8,10},{10,12},{12... | collective-permute-start | bytes 1376264 | tf_op jit(solution)/shard_map/ppermute | solution.py:53
  168.7 11.1 %copy-start.26 = (bf16[448,512]{1,0:T(8,128)(2,1)}, bf16[448,512]{1,0:T(8,128)(2,1)S(1)}, u32[]{:S(2)}) copy-start(bf16[448,512]{1,0:T(8,128)(2,1)S(1)} %collective-permute-done.23.refs_5_) | copy-start | bytes 1376260
  168.7 11.1 %collective-permute-start.25 = (bf16[448,512]{1,0:T(8,128)(2,1)S(1)}, bf16[448,512]{1,0:T(8,128)(2,1)S(1)}, u32[]{:S(2)}, u32[]{:S(2)}) collective-permute-start(bf16[448,512]{1,0:T(8,128)(2,1)S(1)} %collective-permute-done.23.refs_5_), channel_id=1, source_target_pairs={{0,1},{2,0},{4,2},{6,4},{7,6},{5,7},{3,5},{1,3},{8,9},{10,8},{12,1... | collective-permute-start | bytes 1376264 | tf_op jit(solution)/shard_map/ppermute | solution.py:54
  178.0 8.8 %collective-permute-start.26 = (bf16[224,512]{1,0:T(8,128)(2,1)}, bf16[224,512]{1,0:T(8,128)(2,1)S(1)}, u32[]{:S(2)}, u32[]{:S(2)}) collective-permute-start(bf16[224,512]{1,0:T(8,128)(2,1)} %slice.81), channel_id=1, source_target_pairs={{0,2},{2,4},{4,6},{6,7},{7,5},{5,3},{3,1},{1,0},{8,10},{10,12},{12... | collective-permute-start | bytes 688136 | tf_op jit(solution)/shard_map/ppermute | solution.py:59
  180.5 6.4 %collective-permute-start.27 = (bf16[224,512]{1,0:T(8,128)(2,1)}, bf16[224,512]{1,0:T(8,128)(2,1)S(1)}, u32[]{:S(2)}, u32[]{:S(2)}) collective-permute-start(bf16[224,512]{1,0:T(8,128)(2,1)} %slice.82), channel_id=1, source_target_pairs={{0,1},{2,0},{4,2},{6,4},{7,6},{5,7},{3,5},{1,3},{8,9},{10,8},{12,1... | collective-permute-start | bytes 688136 | tf_op jit(solution)/shard_map/ppermute | solution.py:60
  186.8 2.4 copy-start.1
  195.6 10.5 %collective-permute-start.29 = (bf16[448,512]{1,0:T(8,128)(2,1)}, bf16[448,512]{1,0:T(8,128)(2,1)S(1)}, u32[]{:S(2)}, u32[]{:S(2)}) collective-permute-start(bf16[448,512]{1,0:T(8,128)(2,1)} %get-tuple-element.27.refs_2_), channel_id=1, source_target_pairs={{0,16},{8,24},{1,17},{9,25},{2,18},{10,26},{3,19},{11,27},{4,20},{... | collective-permute-start | bytes 1376264 | tf_op jit(solution)/shard_map/ppermute | solution.py:484
  201.3 5.6 %collective-permute-start.28 = (bf16[448,512]{1,0:T(8,128)(2,1)}, bf16[448,512]{1,0:T(8,128)(2,1)S(1)}, u32[]{:S(2)}, u32[]{:S(2)}) collective-permute-start(bf16[448,512]{1,0:T(8,128)(2,1)} %get-tuple-element.27.refs_2_), channel_id=1, source_target_pairs={{0,8},{16,24},{1,9},{17,25},{2,10},{18,26},{3,11},{19,27},{4,12},{... | collective-permute-start | bytes 1376264 | tf_op jit(solution)/shard_map/ppermute | solution.py:483
  206.1 0.7 collective-permute-start.30
  210.4 6.1 %collective-permute-start.31 = (bf16[224,512]{1,0:T(8,128)(2,1)S(1)}, bf16[224,512]{1,0:T(8,128)(2,1)S(1)}, u32[]{:S(2)}, u32[]{:S(2)}) collective-permute-start(bf16[224,512]{1,0:T(8,128)(2,1)S(1)} %shard_map.207.refs_1_), channel_id=1, source_target_pairs={{0,2},{2,4},{4,6},{6,7},{7,5},{5,3},{3,1},{1,0},{8,10},{10,12},{12... | collective-permute-start | bytes 688136 | tf_op jit(solution)/shard_map/ppermute | solution.py:53
  211.9 6.1 %collective-permute-start.32 = (bf16[224,512]{1,0:T(8,128)(2,1)S(1)}, bf16[224,512]{1,0:T(8,128)(2,1)S(1)}, u32[]{:S(2)}, u32[]{:S(2)}) collective-permute-start(bf16[224,512]{1,0:T(8,128)(2,1)S(1)} %shard_map.207.refs_1_), channel_id=1, source_target_pairs={{0,1},{2,0},{4,2},{6,4},{7,6},{5,7},{3,5},{1,3},{8,9},{10,8},{12,1... | collective-permute-start | bytes 688136 | tf_op jit(solution)/shard_map/ppermute | solution.py:54
  216.4 7.1 %collective-permute-start.33 = (bf16[224,512]{1,0:T(8,128)(2,1)S(1)}, bf16[224,512]{1,0:T(8,128)(2,1)S(1)}, u32[]{:S(2)}, u32[]{:S(2)}) collective-permute-start(bf16[224,512]{1,0:T(8,128)(2,1)S(1)} %collective-permute-done.31.refs_2_), channel_id=1, source_target_pairs={{0,2},{2,4},{4,6},{6,7},{7,5},{5,3},{3,1},{1,0},{8,10},{10,12},{12... | collective-permute-start | bytes 688136 | tf_op jit(solution)/shard_map/ppermute | solution.py:53
  218.0 7.8 %collective-permute-start.34 = (bf16[224,512]{1,0:T(8,128)(2,1)S(1)}, bf16[224,512]{1,0:T(8,128)(2,1)S(1)}, u32[]{:S(2)}, u32[]{:S(2)}) collective-permute-start(bf16[224,512]{1,0:T(8,128)(2,1)S(1)} %collective-permute-done.32.refs_3_), channel_id=1, source_target_pairs={{0,1},{2,0},{4,2},{6,4},{7,6},{5,7},{3,5},{1,3},{8,9},{10,8},{12,1... | collective-permute-start | bytes 688136 | tf_op jit(solution)/shard_map/ppermute | solution.py:54
  223.6 7.2 %collective-permute-start.35 = (bf16[224,512]{1,0:T(8,128)(2,1)S(1)}, bf16[224,512]{1,0:T(8,128)(2,1)S(1)}, u32[]{:S(2)}, u32[]{:S(2)}) collective-permute-start(bf16[224,512]{1,0:T(8,128)(2,1)S(1)} %collective-permute-done.33.refs_4_), channel_id=1, source_target_pairs={{0,2},{2,4},{4,6},{6,7},{7,5},{5,3},{3,1},{1,0},{8,10},{10,12},{12... | collective-permute-start | bytes 688136 | tf_op jit(solution)/shard_map/ppermute | solution.py:53
  225.8 6.8 %copy-start.9 = (bf16[224,512]{1,0:T(8,128)(2,1)}, bf16[224,512]{1,0:T(8,128)(2,1)S(1)}, u32[]{:S(2)}) copy-start(bf16[224,512]{1,0:T(8,128)(2,1)S(1)} %collective-permute-done.34.refs_5_) | copy-start | bytes 688132
  225.8 6.8 %collective-permute-start.36 = (bf16[224,512]{1,0:T(8,128)(2,1)S(1)}, bf16[224,512]{1,0:T(8,128)(2,1)S(1)}, u32[]{:S(2)}, u32[]{:S(2)}) collective-permute-start(bf16[224,512]{1,0:T(8,128)(2,1)S(1)} %collective-permute-done.34.refs_5_), channel_id=1, source_target_pairs={{0,1},{2,0},{4,2},{6,4},{7,6},{5,7},{3,5},{1,3},{8,9},{10,8},{12,1... | collective-permute-start | bytes 688136 | tf_op jit(solution)/shard_map/ppermute | solution.py:54
  230.8 45.4 %collective-permute-start.37 = (bf16[112,512]{1,0:T(8,128)(2,1)S(1)}, bf16[112,512]{1,0:T(8,128)(2,1)S(1)}, u32[]{:S(2)}, u32[]{:S(2)}) collective-permute-start(bf16[112,512]{1,0:T(8,128)(2,1)S(1)} %slice.86), channel_id=1, source_target_pairs={{0,2},{2,4},{4,6},{6,7},{7,5},{5,3},{3,1},{1,0},{8,10},{10,12},{12... | collective-permute-start | bytes 344072 | tf_op jit(solution)/shard_map/ppermute | solution.py:59
  232.6 44.2 %collective-permute-start.38 = (bf16[112,512]{1,0:T(8,128)(2,1)S(1)}, bf16[112,512]{1,0:T(8,128)(2,1)S(1)}, u32[]{:S(2)}, u32[]{:S(2)}) collective-permute-start(bf16[112,512]{1,0:T(8,128)(2,1)S(1)} %slice.87), channel_id=1, source_target_pairs={{0,1},{2,0},{4,2},{6,4},{7,6},{5,7},{3,5},{1,3},{8,9},{10,8},{12,1... | collective-permute-start | bytes 344072 | tf_op jit(solution)/shard_map/ppermute | solution.py:60
  (21 other events, 17.9 us)
Sparse Core Ops, SparseCore 0:
  42.9 27.7 all-gather.2
  233.3 35.4 all-reduce.10

commit v2 on v1

v2 whole, which is shorter than its diff:
```python
import functools

import jax
import jax.numpy as jnp
import numpy as np
from jax import lax
from jax.experimental import pallas as pl
from jax.experimental.pallas import tpu as pltpu
from jax.sharding import PartitionSpec as P

F32 = jnp.float32
BF16 = jnp.bfloat16
EPS = 1e-05
NEG = -1e30


def ring_order(count):
    columns = {8: 2, 32: 4}.get(count, 0)
    if not columns:
        return list(range(count))
    rows = count // columns
    order = [row * columns for row in range(rows)]
    for row in reversed(range(rows)):
        inner = list(range(1, columns))
        if (rows - 1 - row) % 2:
            inner.reverse()
        order += [row * columns + column for column in inner]
    return order


def sources(count):
    order = ring_order(count)
    place = {device: i for i, device in enumerate(order)}
    table = np.zeros((count, count), np.int32)
    for device in range(count):
        at = place[device]
        slots = [order[at]]
        for hop in range(1, (count - 1) // 2 + 1):
            slots += [order[(at - hop) % count], order[(at + hop) % count]]
        if count % 2 == 0 and count > 1:
            slots.append(order[(at + count // 2) % count])
        table[device] = slots
    return table


def ring_gather(piece, axis, count, split=False, tasks=()):
    order = ring_order(count)
    ahead = [(order[i], order[(i + 1) % count]) for i in range(count)]
    behind = [(order[i], order[(i - 1) % count]) for i in range(count)]
    half = piece.shape[0] // 2
    split = split and half % 16 == 0
    parts = [piece[:half], piece[half:]] if split else [piece]
    far_hop = (count - 1) // 2 + 1
    last_hop = far_hop if count % 2 == 0 else far_hop - 1
    here = {(0, i): (part, part) for i, part in enumerate(parts)}
    results = [None] * len(tasks)
    finished = [(piece,)]
    step = 0
    for hop in range(1, last_hop + 1):
        for i in range(len(parts)):
            one, two = here[hop - 1, i]
            wait = finished[max(0, len(finished) - 3)] if split else finished[-1]
            ends = [t for t, task in enumerate(tasks) if task[1] == step - 1]
            held = [results[t] for t in ends]
            one, two, _, held = lax.optimization_barrier((one, two, wait, held))
            for t, value in zip(ends, held, strict=True):
                results[t] = value
            if hop < far_hop:
                got = (lax.ppermute(one, axis, ahead), lax.ppermute(two, axis, behind))
            elif not split and half % 16 == 0:
                got = (lax.ppermute(one[:half], axis, ahead), lax.ppermute(two[half:], axis, behind))
            elif i == 0:
                got = (lax.ppermute(one, axis, ahead),) * 2
            else:
                got = (lax.ppermute(two, axis, behind),) * 2
            here[hop, i] = got
            for t, task in enumerate(tasks):
                if task[0] == step:
                    recent = finished[max(0, step + 1 - len(parts)) :]
                    results[t] = task[2]([value for pair in recent for value in pair])
            finished.append(got)
            step += 1
    pieces = [piece]
    for hop in range(1, last_hop + 1):
        if hop < far_hop:
            for side in range(2):
                pieces += [here[hop, i][side] for i in range(len(parts))]
        elif not split and half % 16 == 0:
            pieces += list(here[hop, 0])
        else:
            pieces += [here[hop, i][0] for i in range(len(parts))]
    return pieces, results


def sum_pairs(value, axis, count):
    by = 1
    while by < count:
        value = value + lax.ppermute(value, axis, [(i, i ^ by) for i in range(count)])
        by *= 2
    return value


def lay_out(slots_ref, piece_refs, rows, full_ref):
    columns = full_ref.shape[1]
    total = jnp.zeros((8, columns), F32)
    slot = 0
    done = 0
    for piece in piece_refs:
        count = piece.shape[0]
        strip = next(s for s in (64, 32, 16, 8) if count % s == 0)
        start = slots_ref[lax.axis_index("tp"), slot] * rows + done

        def body(i, carry, piece=piece, strip=strip, start=start):
            part = piece[pl.ds(pl.multiple_of(i * strip, strip), strip), :]
            full_ref[pl.ds(pl.multiple_of(start + i * strip, 16), strip), :] = part
            wide = part.astype(F32)
            return carry + jnp.sum((wide * wide).reshape(strip // 8, 8, columns), axis=0)

        total = lax.fori_loop(0, count // strip, body, total)
        done += count
        if done == rows:
            slot, done = slot + 1, 0
    return jnp.sum(total, axis=0, keepdims=True)


def call(kernel, out_shape, operands, smem=(), scratch=(), flops=0, vmem=12):
    specs = [
        pl.BlockSpec(
            memory_space=pltpu.SMEM if i in smem else pltpu.VMEM
        )
        for i in range(len(operands))
    ]
    size = sum(o.size * o.dtype.itemsize for o in operands)
    return pl.pallas_call(
        kernel,
        out_shape=out_shape,
        in_specs=specs,
        out_specs=jax.tree.map(lambda _: pl.BlockSpec(memory_space=pltpu.VMEM), out_shape),
        scratch_shapes=list(scratch),
        compiler_params=pltpu.CompilerParams(vmem_limit_bytes=vmem << 20),
        cost_estimate=pl.CostEstimate(flops=flops, bytes_accessed=size, transcendentals=0),
    )(*operands)


def after(values, first):
    return lax.optimization_barrier((*values, first))


def silu(value):
    return value / (1.0 + jnp.exp(-value))


def share_kernel(seq_ref, out_ref, o_ref, gain_ref, mine_ref, mine_o_ref):
    count, part = mine_ref.shape[0], mine_ref.shape[2]
    for d in range(count):
        columns = slice(d * part, (d + 1) * part)
        scaled = out_ref[:, columns].astype(F32) * gain_ref[:, 0:1]
        mine_ref[d, :, :] = scaled.astype(BF16)
        mine_o_ref[d, :, :] = o_ref[:, columns]


def weights_kernel(xz_ref, bc_ref, dt_ref, gain_ref, w_ref):
    inner = xz_ref.shape[1]
    bc = bc_ref.shape[1]
    width = gain_ref.shape[1]
    tile = 512
    for i in range(width // tile):
        at = slice(i * tile, (i + 1) * tile)
        gain = gain_ref[:, at]

        def put(first, value, at=at, gain=gain):
            w_ref[first : first + value.shape[0], at] = (value.astype(F32) * gain).astype(BF16)

        put(0, xz_ref[0, :, at])
        put(inner, bc_ref[at, :].astype(F32).T)
        put(inner + bc, xz_ref[1, :, at])
        heads = dt_ref.shape[0]
        last = jnp.concatenate(
            [dt_ref[:, at].astype(F32), jnp.zeros((16 - heads, tile), F32)], axis=0
        )
        put(2 * inner + bc, last)


def run_starts(seg_ref, bounds_ref):
    seg = seg_ref[...]
    start = jnp.zeros(seg.shape, jnp.int32)
    for t in range(bounds_ref.shape[0]):
        start = jnp.where(seg == t, bounds_ref[t, 0], start)
    return start


def start_at(place, bounds_ref):
    start = jnp.int32(0)
    for t in range(bounds_ref.shape[0]):
        start = jnp.where(place >= bounds_ref[t, 0], bounds_ref[t, 0], start)
    return start


def turn_kernel(cols_ref, out_ref):
    rows = cols_ref.shape[0]
    tile = 256 if rows % 256 == 0 else rows
    for i in range(rows // tile):
        at = slice(i * tile, (i + 1) * tile)
        out_ref[:, at] = cols_ref[at, :].astype(F32).T.astype(BF16)


def in_kernel(pieces, rows, conv_rows, inner, *refs):
    slots_ref = refs[0]
    piece_refs = refs[1 : 1 + pieces]
    w_ref, raw_ref, z_ref, dt_ref, tail_ref, full_ref, acc_ref = refs[1 + pieces :]
    squares = lay_out(slots_ref, piece_refs, rows, full_ref)
    scale = lax.rsqrt(squares / full_ref.shape[0] + EPS)
    acc_ref[...] = jnp.dot(w_ref[...], full_ref[...], preferred_element_type=F32)
    raw_ref[...] = acc_ref[:conv_rows, :] * scale
    z_ref[...] = acc_ref[conv_rows : conv_rows + inner, :] * scale
    dt_ref[...] = acc_ref[conv_rows + inner : conv_rows + inner + 8, :] * scale
    last = raw_ref.shape[1] - 128
    tail_ref[...] = raw_ref[:, last:].T[120:, :]


def mix_kernel(
    tenants,
    heads,
    bounds_ref,
    bias_ref,
    rate_ref,
    skip_ref,
    raw_ref,
    dt_ref,
    halo_ref,
    conv_x_ref,
    conv_bc_ref,
    seg_ref,
    live_ref,
    y_ref,
    c_ref,
    entry_ref,
    pay_ref,
    local_ref,
    ext_ref,
    x_ref,
    xdt_ref,
    taps_ref,
):
    conv_rows, toks = raw_ref.shape
    inner = y_ref.shape[0]
    hd = inner // heads
    lane = lax.broadcasted_iota(jnp.int32, (1, toks), 1)
    base = lax.axis_index("seq") * toks
    rel = base + lane - run_starts(seg_ref, bounds_ref)
    live = live_ref[...].astype(F32)
    count = conv_x_ref.shape[0]
    both = jnp.concatenate([conv_x_ref[...], conv_bc_ref[...]], axis=1)
    taps_ref[...] = jnp.concatenate([both, jnp.zeros((128 - count, conv_rows), F32)], axis=0).T
    head = lax.broadcasted_iota(jnp.int32, (8, 1), 0)
    bias = rate = jnp.zeros((8, 1), F32)
    for h in range(heads):
        bias = jnp.where(head == h, bias_ref[h], bias)
        rate = jnp.where(head == h, rate_ref[h], rate)
    before = jnp.concatenate([jnp.zeros((120, conv_rows), F32), halo_ref[...]], axis=0).T
    ext_ref[:, :128] = before
    ext_ref[:, 128:] = raw_ref[...]
    strip = 64
    keep = [(rel >= shift).astype(F32) for shift in range(4)]
    for i in range(conv_rows // strip):
        rows = pl.ds(i * strip, strip)
        ext = ext_ref[rows, :]
        taps = taps_ref[rows, :]
        total = taps[:, 3:4] * ext[:, 128:]
        for shift in range(1, 4):
            moved = pltpu.roll(ext, shift, 1)[:, 128:]
            total = total + taps[:, 3 - shift : 4 - shift] * moved * keep[shift]
        x_ref[rows, :] = silu(total)
    step = dt_ref[...] + bias
    step = (jnp.maximum(step, 0.0) + jnp.log1p(jnp.exp(-jnp.abs(step)))) * live
    logs = -step * rate
    shift = 1
    while shift < toks:
        logs = logs + jnp.where(lane >= shift, pltpu.roll(logs, shift, 1), 0.0)
        shift *= 2
    start = lane - rel
    entry_ref[...] = jnp.exp(logs) * (start < 0).astype(F32)
    for h in range(heads):
        xdt_ref[h * hd : (h + 1) * hd, :] = x_ref[h * hd : (h + 1) * hd, :] * step[h : h + 1, :]
    input_b = x_ref[inner : inner + 64, :]
    output_c = x_ref[inner + 64 : inner + 128, :].astype(BF16)
    c_ref[...] = output_c
    bc_tok = x_ref[inner : inner + 128, :].T
    b_tok = bc_tok[:, :64].astype(BF16)
    columns = [
        jnp.broadcast_to(logs[h : h + 1, :], (128, toks)).T for h in range(heads)
    ]
    for block in range(toks // 128):
        here = slice(block * 128, (block + 1) * 128)
        upto = (block + 1) * 128
        key = lax.broadcasted_iota(jnp.int32, (upto, 128), 0)
        seen = (key <= lane[:, here]) & (key >= start[:, here])
        bias = jnp.where(seen, 0.0, NEG)
        c_dot_b = jnp.dot(b_tok[:upto, :], output_c[:, here], preferred_element_type=F32)
        for h in range(heads):
            gap = logs[h : h + 1, here] - columns[h][:upto, :]
            mixing = (jnp.exp(jnp.minimum(gap, 0.0) + bias) * c_dot_b).astype(BF16)
            rows = slice(h * hd, (h + 1) * hd)
            y_ref[rows, here] = (
                jnp.dot(
                    xdt_ref[rows, :upto].astype(BF16), mixing, preferred_element_type=F32
                )
                + skip_ref[h] * x_ref[rows, here]
            )
    wide_b = bc_tok.astype(BF16)
    tok = lax.broadcasted_iota(jnp.int32, (inner, 128), 1)
    for k in range(tenants + 1):
        if k < tenants:
            pick = jnp.clip(bounds_ref[k, 1] - 1 - base, 0, toks - 1)
            first = bounds_ref[k, 0] - base
        else:
            pick = toks - 1
            first = start_at(base + toks - 1, bounds_ref) - base
        at = jnp.sum(jnp.where(lane == pick, logs, 0.0), axis=1, keepdims=True)
        inside = (lane <= pick) & (lane >= first)
        toward = jnp.exp(jnp.minimum(at - logs, 0.0) + jnp.where(inside, 0.0, NEG))
        carried = jnp.exp(at) * jnp.where(first < 0, 1.0, 0.0)
        lhs = jnp.concatenate(
            [
                (xdt_ref[h * hd : (h + 1) * hd, :] * toward[h : h + 1, :]).astype(BF16)
                for h in range(heads)
            ],
            axis=0,
        )
        state = jnp.dot(lhs, wide_b, preferred_element_type=F32)
        factor = jnp.concatenate(
            [jnp.broadcast_to(carried[h : h + 1, :], (hd, 128)) for h in range(heads)], axis=0
        )
        if k < tenants:
            local_ref[k * inner : (k + 1) * inner, :] = jnp.where(tok < 64, state, factor)
        else:
            high = factor.astype(BF16).astype(F32)
            packed = jnp.where(tok < 64, state, jnp.where(tok < 96, high, factor - high))
            pay_ref[:inner, :] = packed.astype(BF16)
    rows = [live[:, i * 128 : (i + 1) * 128] for i in range(toks // 128)]
    rows.append(jnp.zeros((16 - toks // 128, 128), F32))
    pay_ref[inner:, :] = jnp.concatenate(rows, axis=0).astype(BF16)


def gate_kernel(
    tenants,
    heads,
    bounds_ref,
    pay_ref,
    y_ref,
    z_ref,
    c_ref,
    entry_ref,
    local_ref,
    g_ref,
    tenant_ref,
):
    inner = y_ref.shape[0]
    hd = inner // heads
    incoming = jnp.zeros((inner, 64), F32)
    for block in range(pay_ref.shape[0] - 1):
        wide = pay_ref[block, :inner, :].astype(F32)
        passed = (wide[:, 64:65] + wide[:, 96:97]) * incoming + wide[:, :64]
        incoming = jnp.where(block < lax.axis_index("seq"), passed, incoming)
    for h in range(heads):
        rows = slice(h * hd, (h + 1) * hd)
        carry = jnp.dot(incoming[rows, :].astype(BF16), c_ref[...], preferred_element_type=F32)
        y_full = y_ref[rows, :] + carry * entry_ref[h : h + 1, :]
        g_ref[rows, :] = (y_full * silu(z_ref[rows, :])).astype(BF16)
    for k in range(tenants):
        rows = slice(k * inner, (k + 1) * inner)
        last = bounds_ref[k, 1] - 1 - lax.axis_index("seq") * y_ref.shape[1]
        owned = jnp.where((last >= 0) & (last < y_ref.shape[1]), 1.0, 0.0)
        local = local_ref[rows, :]
        tenant_ref[rows, :] = ((local[:, 64:65] * incoming + local[:, :64]) * owned).astype(BF16)


def mixed_kernel(pieces, rows, *refs):
    slots_ref = refs[0]
    piece_refs = refs[1 : 1 + pieces]
    w_ref, hidden_ref, out_ref, full_ref = refs[1 + pieces :]
    squares = lay_out(slots_ref, piece_refs, rows, full_ref)
    scale = lax.rsqrt(squares / full_ref.shape[0] + EPS)
    product = jnp.dot(w_ref[...], full_ref[...], preferred_element_type=F32)
    out_ref[...] = (hidden_ref[...].astype(F32) + product * scale).astype(BF16)


def qkv_kernel(pieces, rows, *refs):
    slots_ref = refs[0]
    piece_refs = refs[1 : 1 + pieces]
    w_ref, q_ref, k_ref, v_ref, kv_ref, full_ref = refs[1 + pieces :]
    squares = lay_out(slots_ref, piece_refs, rows, full_ref)
    scale = lax.rsqrt(squares / full_ref.shape[0] + EPS)
    product = jnp.dot(w_ref[...], full_ref[...], preferred_element_type=F32)
    att = q_ref.shape[0]
    q_ref[...] = (product[:att] * scale).astype(BF16)
    keys = (product[att : 2 * att] * scale).astype(BF16)
    values = (product[2 * att :] * scale).astype(BF16)
    k_ref[...] = keys
    v_ref[...] = values
    kv_ref[:att, :] = keys
    kv_ref[att:, :] = values


def attend_kernel(blocks, block_of, score_scale, *refs):
    bounds_ref, q_ref = refs[:2]
    k_refs = refs[2 : 2 + blocks]
    v_refs = refs[2 + blocks : 2 + 2 * blocks]
    pay_ref, seg_ref, ctx_ref, q_aug, k_aug, peak_ref, total_ref, sum_ref = refs[2 + 2 * blocks :]
    inner = pay_ref.shape[1] - 16
    seq = lax.axis_index("seq")
    att, toks = q_ref.shape
    extra = q_aug.shape[0] - att
    row = lax.broadcasted_iota(jnp.int32, (extra, toks), 0)
    q_aug[:att, :] = q_ref[...]
    q_aug[att:, :] = jnp.where(row == 0, 1.0, 0.0).astype(BF16)
    place = seq * toks + lax.broadcasted_iota(jnp.int32, (1, toks), 1)
    start = run_starts(seg_ref, bounds_ref)
    first_start = start_at(seq * toks, bounds_ref)
    peak_ref[...] = jnp.full(peak_ref.shape, NEG, F32)
    total_ref[...] = jnp.zeros(total_ref.shape, F32)
    sum_ref[...] = jnp.zeros(sum_ref.shape, F32)
    for b in range(blocks):
        block = block_of(b, seq)

        @pl.when((block >= 0) & (block <= seq) & (block * toks + toks > first_start))
        def _(b=b, block=block):
            count = k_refs[b].shape[1]
            k_aug[:att, :] = k_refs[b][...]
            pads = pay_ref[block, inner:, :].astype(F32)
            pads = jnp.concatenate([pads[i : i + 1, :] for i in range(count // 128)], axis=1)
            bias = (pads - 1.0) * 1e30
            k_aug[att:, :] = jnp.where(row == 0, bias, 0.0).astype(BF16)
            scores = (
                lax.dot_general(
                    k_aug[...], q_aug[...], (((0,), (0,)), ((), ())), preferred_element_type=F32
                )
                * score_scale
            )
            key = block * count + lax.broadcasted_iota(jnp.int32, (count, toks), 0)
            scores = jnp.where((key <= place) & (key >= start), scores, NEG)
            peak = jnp.maximum(peak_ref[...], jnp.max(scores, axis=0, keepdims=True))
            weights = jnp.exp(scores - peak)
            keep = jnp.exp(peak_ref[...] - peak)
            peak_ref[...] = peak
            total_ref[...] = total_ref[...] * keep + jnp.sum(weights, axis=0, keepdims=True)
            sum_ref[...] = sum_ref[...] * keep + jnp.dot(
                v_refs[b][...], weights.astype(BF16), preferred_element_type=F32
            )

    ctx_ref[...] = (sum_ref[...] / total_ref[...]).astype(BF16)


def last_kernel(pieces, rows, *refs):
    slots_ref = refs[0]
    piece_refs = refs[1 : 1 + pieces]
    w_ref, mixed_ref, out_ref, full_ref = refs[1 + pieces :]
    lay_out(slots_ref, piece_refs, rows, full_ref)
    product = jnp.dot(w_ref[...], full_ref[...], preferred_element_type=F32)
    out_ref[...] = (mixed_ref[...].astype(F32) + product).T.astype(BF16)


def on_device(
    tp_count,
    seq_count,
    hidden_in,
    mamba_gain,
    w_xz,
    w_bc,
    w_dt,
    dt_bias,
    decay_rate,
    conv_x,
    conv_bc,
    skip_gain,
    inner_gain,
    w_out,
    attn_gain,
    w_qkv,
    w_o,
    seg_ids,
    pad_mask,
    tenant_bounds,
):
    toks, part = hidden_in.shape
    width = mamba_gain.shape[0]
    inner = w_xz.shape[1]
    heads = decay_rate.shape[0]
    att = w_qkv.shape[1]
    tenants = tenant_bounds.shape[0]
    bc = w_bc.shape[1]
    conv_rows = inner + bc
    seq = lax.axis_index("seq")
    sds = jax.ShapeDtypeStruct

    hidden_t = hidden_in.T
    slots = jnp.asarray(sources(tp_count))
    seg_row, pad_row = seg_ids[None, :], pad_mask[None, :]

    out_share, o_share = inner // seq_count, att // seq_count

    def shares(first):
        out_rows, o_rows, _ = after((w_out, w_o), first)
        if out_share % 8 or o_share % 8:
            scaled = (out_rows.astype(F32) * inner_gain[:, None]).astype(BF16)
            cut = [
                lax.dynamic_slice_in_dim(rows, seq * count, count)
                for rows, count in ((scaled, out_share), (o_rows, o_share))
            ]
            return tuple(c.reshape(c.shape[0], tp_count, part).transpose(1, 0, 2) for c in cut)
        return pl.pallas_call(
            share_kernel,
            out_shape=(
                sds((tp_count, out_share, part), BF16),
                sds((tp_count, o_share, part), BF16),
            ),
            grid_spec=pltpu.PrefetchScalarGridSpec(
                num_scalar_prefetch=1,
                grid=(1,),
                in_specs=[
                    pl.BlockSpec((out_share, width), lambda i, at: (at[0], 0)),
                    pl.BlockSpec((o_share, width), lambda i, at: (at[0], 0)),
                    pl.BlockSpec((out_share, 128), lambda i, at: (at[0], 0)),
                ],
                out_specs=(
                    pl.BlockSpec((tp_count, out_share, part), lambda i, at: (0, 0, 0)),
                    pl.BlockSpec((tp_count, o_share, part), lambda i, at: (0, 0, 0)),
                ),
            ),
            compiler_params=pltpu.CompilerParams(vmem_limit_bytes=16 << 20),
        )(
            jnp.full((1,), seq, jnp.int32),
            out_rows,
            o_rows,
            jnp.broadcast_to(inner_gain[:, None], (inner, 128)),
        )

    in_rows = conv_rows + inner + 16

    def in_weights(first):
        xz, narrow, dt, _ = after((w_xz, w_bc, w_dt), first)
        return call(
            weights_kernel,
            sds((in_rows, width), BF16),
            (xz, narrow, dt, mamba_gain[None, :]),
            vmem=16,
            flops=10**7,
        )

    def exchange(share, first):
        value, _ = after((share,), first)
        return lax.all_to_all(value, "tp", 0, 0, tiled=False)

    def spread(columns, first):
        value, _ = after((columns,), first)
        return lax.all_gather(value, "seq", axis=1, tiled=True)

    full_in, ((out_shares, o_shares), w_in) = ring_gather(
        hidden_t, "tp", tp_count, True, ((1, 3, shares), (3, 5, in_weights))
    )
    pieces = len(full_in)

    raw, z, dt_raw, tail = call(
        functools.partial(in_kernel, pieces, part, conv_rows, inner),
        (
            sds((conv_rows, toks), F32),
            sds((inner, toks), F32),
            sds((8, toks), F32),
            sds((8, conv_rows), F32),
        ),
        (slots, *full_in, w_in),
        smem=(0,),
        scratch=[
            pltpu.VMEM((width, toks), BF16),
            pltpu.VMEM((in_rows, toks), F32),
        ],
        flops=2 * in_rows * width * toks,
    )
    w_out_cols = spread(exchange(out_shares, tail), tail)
    halo = lax.ppermute(tail, "seq", [(i, i + 1) for i in range(seq_count - 1)])
    y, c_rows, entry, pay, local = call(
        functools.partial(mix_kernel, tenants, heads),
        (
            sds((inner, toks), F32),
            sds((bc // 2, toks), BF16),
            sds((8, toks), F32),
            sds((inner + 16, 128), BF16),
            sds((tenants * inner, 128), F32),
        ),
        (tenant_bounds, dt_bias, decay_rate, skip_gain, raw, dt_raw, halo, conv_x, conv_bc, seg_row, pad_row),
        smem=(0, 1, 2, 3),
        scratch=[
            pltpu.VMEM((conv_rows, toks + 128), F32),
            pltpu.VMEM((conv_rows, toks), F32),
            pltpu.VMEM((inner, toks), F32),
            pltpu.VMEM((conv_rows, 128), F32),
        ],
        flops=10**9,
    )
    all_pays = lax.all_gather(pay, "seq", axis=0, tiled=False)
    gated, tenant_part = call(
        functools.partial(gate_kernel, tenants, heads),
        (sds((inner, toks), BF16), sds((tenants * inner, bc // 2), BF16)),
        (tenant_bounds, all_pays, y, z, c_rows, entry, local),
        smem=(0,),
        flops=10**8,
    )
    tenant_states = (
        sum_pairs(tenant_part, "seq", seq_count)
        .astype(F32)
        .reshape(tenants, heads, inner // heads, bc // 2)
    )
    def turned(cols, rows):
        def task(first):
            value, _ = after((cols,), first)
            return call(
                turn_kernel,
                sds((part, tp_count * rows), BF16),
                (value.reshape(tp_count * rows, part),),
            )

        return task

    full_gated, (w_out_t,) = ring_gather(
        gated, "tp", tp_count, False, ((3, -1, turned(w_out_cols, inner)),)
    )
    mixed = call(
        functools.partial(mixed_kernel, len(full_gated), inner),
        sds((part, toks), BF16),
        (slots, *full_gated, w_out_t, hidden_t),
        smem=(0,),
        scratch=[
            pltpu.VMEM((tp_count * inner, toks), BF16),
        ],
        flops=2 * part * tp_count * inner * toks,
    )
    def att_weights(first):
        value, _ = after((w_qkv,), first)
        return (value.reshape(3 * att, width).astype(F32) * attn_gain).astype(BF16)

    full_mixed, (w_att,) = ring_gather(mixed, "tp", tp_count, True, ((4, 5, att_weights),))
    queries, keys, values, kv = call(
        functools.partial(qkv_kernel, len(full_mixed), part),
        (
            sds((att, toks), BF16),
            sds((att, toks), BF16),
            sds((att, toks), BF16),
            sds((2 * att, toks), BF16),
        ),
        (slots, *full_mixed, w_att),
        smem=(0,),
        scratch=[
            pltpu.VMEM((width, toks), BF16),
        ],
        flops=6 * att * width * toks,
    )
    kv_cache = kv.reshape(2, att, toks)

    if seq_count == 4:

        def near(value):
            return lax.ppermute(value, "seq", [(0, 1), (2, 3)])

        def far(value):
            return lax.ppermute(value, "seq", [(0, 2), (1, 3)])

        def swap(value):
            return lax.ppermute(value, "seq", [(2, 3), (3, 2)])

        far_keys, far_values = far(keys), far(values)
        near_keys, near_values = near(keys), near(values)
        o_columns = exchange(o_shares, (near_keys, near_values))
        swap_keys, swap_values = swap(far_keys), swap(far_values)
        w_o_cols = spread(o_columns, (swap_keys, swap_values))
        key_blocks = [keys, near_keys, far_keys, swap_keys]
        value_blocks = [values, near_values, far_values, swap_values]


        def block_of(b, at):
            return (at, at ^ 1, at - 2, (at ^ 1) - 2)[b]

    else:
        all_keys = lax.all_gather(keys, "seq", axis=0, tiled=False)
        all_values = lax.all_gather(values, "seq", axis=0, tiled=False)
        w_o_cols = spread(exchange(o_shares, keys), keys)
        key_blocks = [all_keys[i] for i in range(seq_count)]
        value_blocks = [all_values[i] for i in range(seq_count)]

        def block_of(b, at):
            return jnp.int32(b)

    blocks = len(key_blocks)
    deep = att + 32
    context = call(
        functools.partial(attend_kernel, blocks, block_of, att ** (-0.5)),
        sds((att, toks), BF16),
        (tenant_bounds, queries, *key_blocks, *value_blocks, all_pays, seg_row),
        smem=(0,),
        scratch=[
            pltpu.VMEM((deep, toks), BF16),
            pltpu.VMEM((deep, toks), BF16),
            pltpu.VMEM((1, toks), F32),
            pltpu.VMEM((1, toks), F32),
            pltpu.VMEM((att, toks), F32),
        ],
        flops=4 * blocks * toks * toks * att,
    )
    full_context, (w_o_t,) = ring_gather(
        context, "tp", tp_count, False, ((1, 2, turned(w_o_cols, att)),)
    )
    hidden_out = call(
        functools.partial(last_kernel, len(full_context), att),
        sds((toks, part), BF16),
        (slots, *full_context, w_o_t, mixed),
        smem=(0,),
        scratch=[
            pltpu.VMEM((tp_count * att, toks), BF16),
        ],
        flops=2 * part * tp_count * att * toks,
    )
    return (hidden_out, kv_cache, tenant_states)


def solution(mesh):
    return jax.shard_map(
        functools.partial(on_device, mesh.shape["tp"], mesh.shape["seq"]),
        mesh=mesh,
        in_specs=(
            P("seq", "tp"),
            P(),
            P(None, "tp", None),
            P(),
            P("tp", None),
            P("tp"),
            P("tp"),
            P(None, "tp"),
            P(),
            P("tp"),
            P("tp"),
            P("tp", None),
            P(),
            P(None, "tp", None),
            P("tp", None),
            P("seq"),
            P("seq"),
            P(),
        ),
        out_specs=(P("seq", "tp"), P(None, "tp", "seq"), P(None, "tp", None, None)),
        check_vma=False,
    )
```

time: 293 us -> 235 us (0.80)
  waiting for transfers between devices: 139 us -> 90.4 us
  local copies, waits for them, and re-layouts: 47.6 us -> 12.9 us
  blocking collectives: 0 us -> 24.9 us
  other arithmetic: 14.7 us -> 4.09 us
  starting transfers between devices: 58.1 us -> 64.9 us
  Pallas kernels: 18.2 us -> 21.7 us
    psum x1 -> x0, waiting for transfers between devices: 35.6 us -> none  [on_device(): lax.psum(tenant_part, 'seq').astype(F32)]
    all_to_all x1, waiting for transfers between devices: 19.4 us -> 0.01 us  [exchange(): return lax.all_to_all(value, 'tp', 0, 0, tiled=False)]
    all_to_all x0 -> x1, blocking collectives: none -> 15.2 us  [exchange(): return lax.all_to_all(value, 'tp', 0, 0, tiled=False)]
    unnamed x88 -> x46, local copies, waits for them, and re-layouts: 24.9 us -> 10.1 us
    ppermute x38 -> x52, starting transfers between devices: 49.3 us -> 59.4 us  [the longest x36 37 us: ring_gather(): got = (lax.ppermute(one, axis, ahead), lax.ppermute(two, axis, behind))]
    all_gather x0 -> x1, blocking collectives: none -> 9.63 us  [on_device(): all_pays = lax.all_gather(pay, 'seq', axis=0, tiled=False)]
    slice x11 -> x6, local copies, waits for them, and re-layouts: 8.93 us -> 1.22 us  [the longest x2 1.19 us: ring_gather(): parts = [piece[:half], piece[half:]] if split else [piece]]
    convert_element_type x4 -> x1, other arithmetic: 9.44 us -> 3.2 us  [att_weights(): return (value.reshape(3 * att, width).astype(F32) * attn_gain).astype(BF16)]
  transfers between devices with their start and end apart: 42 -> 56, of which waited for: 22 -> 39; matrix products, arithmetic and copies ran while one was open for 12% -> 3% of each run, Pallas kernels for 3% -> 4%
where the time goes in v2:
time: 235 us; the launch traced here: 233 us
  waiting for transfers between devices  90.4 us (38%)
  starting transfers between devices  64.9 us (28%)
  blocking collectives  24.9 us (11%)
  Pallas kernels  21.7 us (9%)
  between operations  14.4 us (6%)
  local copies, waits for them, and re-layouts  12.9 us (5%)
  other arithmetic  4.09 us (2%)
    ppermute x36, waiting for transfers between devices, ring_gather(): got = (lax.ppermute(one, axis, ahead), lax.ppermute(two, axis, behind))  59.9 us
    ppermute x36, starting transfers between devices, ring_gather(): got = (lax.ppermute(one, axis, ahead), lax.ppermute(two, axis, behind))  37 us
    pallas_call x10, Pallas kernels, call(): pl.pallas_call(kernel, out_shape=out_shape, in_specs=specs, out_specs=jax...  20.6 us
    all_to_all x1, blocking collectives, exchange(): return lax.all_to_all(value, 'tp', 0, 0, tiled=False)  15.2 us
    unnamed x46, local copies, waits for them, and re-layouts  10.1 us
    all_gather x1, blocking collectives, on_device(): all_pays = lax.all_gather(pay, 'seq', axis=0, tiled=False)  9.63 us
    ppermute x2, waiting for transfers between devices, far(): return lax.ppermute(value, 'seq', [(0, 2), (1, 3)])  8.29 us
    ppermute x2, waiting for transfers between devices, ring_gather(): got = (lax.ppermute(two, axis, behind),) * 2  5.87 us
  transfers between devices with their start and end apart: 56, of which 39 were waited for; matrix products, arithmetic and copies ran while one was open for 3% of the time, Pallas kernels for 4%

profile of v2, /device:TPU:0, one launch (start us, length us, event | category | flops | bytes accessed | tf_op | source)
XLA Modules:
  0.0 233.3 jit_solution(8951214331056371613)
XLA Ops:
  7.2 1.2 fusion.2
  8.4 3.1 %collective-permute-start = (bf16[224,512]{1,0:T(8,128)(2,1)S(1)}, bf16[224,512]{1,0:T(8,128)(2,1)S(1)}, u32[]{:S(2)}, u32[]{:S(2)}) collective-permute-start(bf16[224,512]{1,0:T(8,128)(2,1)S(1)} %get-tuple-element.83), channel_id=1, source_target_pairs={{0,2},{2,4},{4,6},{6,7},{7,5},{5,3},{3,1},{1,0},{8,10},{10,12},{12... | collective-permute-start | bytes 688136 | tf_op jit(solution)/shard_map/ppermute | solution.py:69
  11.5 2.0 collective-permute-start.1
  13.5 4.3 %collective-permute-done.refs_2_ = bf16[224,512]{1,0:T(8,128)(2,1)S(1)} collective-permute-done((bf16[224,512]{1,0:T(8,128)(2,1)S(1)}, bf16[224,512]{1,0:T(8,128)(2,1)S(1)}, u32[]{:S(2)}, u32[]{:S(2)}) %collective-permute-start) | collective-permute-done | bytes 229408 | tf_op jit(solution)/shard_map/ppermute | solution.py:69
  17.8 2.2 collective-permute-done.2.refs_4_
  20.0 1.6 collective-permute-start.4
  22.7 2.2 collective-permute-done.3.refs_5_
  24.9 1.6 collective-permute-start.5
  27.9 1.4 copy-done.3
  29.3 1.3 copy-done.5
  31.7 1.6 collective-permute-start.8
  34.2 1.6 collective-permute-start.9
  38.5 1.3 collective-permute-done.8.refs_10_
  40.6 1.6 collective-permute-start.12
  42.2 1.8 collective-permute-done.9.refs_11_
  44.0 1.2 collective-permute-start.13
  45.2 1.4 collective-permute-done.12.refs_14_
  46.7 3.4 %collective-permute-done.13.refs_15_ = bf16[224,512]{1,0:T(8,128)(2,1)S(1)} collective-permute-done((bf16[224,512]{1,0:T(8,128)(2,1)S(1)}, bf16[224,512]{1,0:T(8,128)(2,1)S(1)}, u32[]{:S(2)}, u32[]{:S(2)}) %collective-permute-start.13) | collective-permute-done | bytes 229408 | tf_op jit(solution)/shard_map/ppermute | solution.py:75
  51.0 3.9 %shard_map.204 = (f32[320,512]{1,0:T(8,128)S(1)}, f32[192,512]{1,0:T(8,128)S(1)}, f32[8,512]{1,0:T(8,128)S(1)}, f32[8,320]{1,0:T(8,128)S(1)}) custom-call(s32[8,8]{1,0:T(8,128)S(1)} %copy-done.9, bf16[448,512]{1,0:T(8,128)(2,1)S(1)} %bitcast.14, bf16[224,512]{1,0:T(8,128)(2,1)S(1)} %collective-permute-done.refs_2_, ...), custom_call_target="tpu_custom_call" | custom-call | flops 1937768448 | bytes 7454976 | tf_op jit(solution)/shard_map/pallas_call | solution.py:134
  54.9 15.2 %all_to_all.10 = bf16[8,48,448]{2,1,0:T(8,128)(2,1)} all-to-all(bf16[8,48,448]{2,1,0:T(8,128)(2,1)S(1)} %get-tuple-element.122), channel_id=1, replica_groups=mesh['seq'=4,'tp'=8] {'tp'}, dimensions={0} | all-to-all | bytes 688128 | tf_op jit(solution)/shard_map/all_to_all | solution.py:552
  70.2 1.3 collective-permute-start.14
  72.3 3.3 %shard_map.205 = (f32[192,512]{1,0:T(8,128)S(1)}, bf16[64,512]{1,0:T(8,128)(2,1)S(1)}, f32[8,512]{1,0:T(8,128)S(1)}, bf16[208,128]{1,0:T(8,128)(2,1)S(1)}, f32[768,128]{1,0:T(8,128)S(1)}) custom-call(s32[4,2]{1,0:T(4,128)S(1)} %copy.24.bounds_ref.refs_0_, f32[3]{0:T(128)S(1)} %copy-done.15, f32[3]{0:T(128)S(1)} %copy-done.16, f32[3]{0:T(128)S(1)} %copy-done.17, ...), custom_call_target="tpu_custom_call" | custom-call | flops 1000000000 | bytes 691268 | tf_op jit(solution)/shard_map/pallas_call | solution.py:134
  75.6 9.6 %all-gather = bf16[832,128]{1,0:T(8,128)(2,1)S(1)} all-gather(bf16[208,128]{1,0:T(8,128)(2,1)S(1)} %get-tuple-element.106), channel_id=2, replica_groups=mesh['seq'=4,'tp'=8] {'seq'}, dimensions={0}, use_global_device_ids=true | all-gather | bytes 266240 | tf_op jit(solution)/shard_map/all_gather | solution.py:600
  86.7 1.7 collective-permute-start.16
  88.4 5.1 %collective-permute-done.15.refs_2_ = bf16[192,512]{1,0:T(8,128)(2,1)S(1)} collective-permute-done((bf16[192,512]{1,0:T(8,128)(2,1)S(1)}, bf16[192,512]{1,0:T(8,128)(2,1)S(1)}, u32[]{:S(2)}, u32[]{:S(2)}) %collective-permute-start.15) | collective-permute-done | bytes 196640 | tf_op jit(solution)/shard_map/ppermute | solution.py:69
  95.6 4.3 %collective-permute-done.17.refs_4_ = bf16[192,512]{1,0:T(8,128)(2,1)S(1)} collective-permute-done((bf16[192,512]{1,0:T(8,128)(2,1)S(1)}, bf16[192,512]{1,0:T(8,128)(2,1)S(1)}, u32[]{:S(2)}, u32[]{:S(2)}) %collective-permute-start.17) | collective-permute-done | bytes 196640 | tf_op jit(solution)/shard_map/ppermute | solution.py:69
  102.3 3.6 %collective-permute-done.19.refs_6_ = bf16[192,512]{1,0:T(8,128)(2,1)S(1)} collective-permute-done((bf16[192,512]{1,0:T(8,128)(2,1)S(1)}, bf16[192,512]{1,0:T(8,128)(2,1)S(1)}, u32[]{:S(2)}, u32[]{:S(2)}) %collective-permute-start.19) | collective-permute-done | bytes 196640 | tf_op jit(solution)/shard_map/ppermute | solution.py:69
  109.0 1.4 copy-done.4
  112.6 1.8 shard_map.208.refs_1_.refs_11_
  115.2 1.3 collective-permute-start.25
  117.3 1.3 collective-permute-start.26
  118.5 4.4 %collective-permute-done.23.refs_2_ = bf16[224,512]{1,0:T(8,128)(2,1)S(1)} collective-permute-done((bf16[224,512]{1,0:T(8,128)(2,1)S(1)}, bf16[224,512]{1,0:T(8,128)(2,1)S(1)}, u32[]{:S(2)}, u32[]{:S(2)}) %collective-permute-start.23) | collective-permute-done | bytes 229408 | tf_op jit(solution)/shard_map/ppermute | solution.py:69
  123.5 1.3 collective-permute-start.27
  125.5 2.4 %collective-permute-done.24.refs_3_ = bf16[224,512]{1,0:T(8,128)(2,1)S(1)} collective-permute-done((bf16[224,512]{1,0:T(8,128)(2,1)S(1)}, bf16[224,512]{1,0:T(8,128)(2,1)S(1)}, u32[]{:S(2)}, u32[]{:S(2)}) %collective-permute-start.24) | collective-permute-done | bytes 229408 | tf_op jit(solution)/shard_map/ppermute | solution.py:69
  128.4 1.3 collective-permute-start.28
  130.4 2.4 %collective-permute-done.27.refs_6_ = bf16[224,512]{1,0:T(8,128)(2,1)S(1)} collective-permute-done((bf16[224,512]{1,0:T(8,128)(2,1)S(1)}, bf16[224,512]{1,0:T(8,128)(2,1)S(1)}, u32[]{:S(2)}, u32[]{:S(2)}) %collective-permute-start.27) | collective-permute-done | bytes 229408 | tf_op jit(solution)/shard_map/ppermute | solution.py:69
  133.4 4.2 %collective-permute-done.28.refs_7_ = bf16[224,512]{1,0:T(8,128)(2,1)S(1)} collective-permute-done((bf16[224,512]{1,0:T(8,128)(2,1)S(1)}, bf16[224,512]{1,0:T(8,128)(2,1)S(1)}, u32[]{:S(2)}, u32[]{:S(2)}) %collective-permute-start.28) | collective-permute-done | bytes 229408 | tf_op jit(solution)/shard_map/ppermute | solution.py:69
  138.2 2.0 collective-permute-start.32
  140.9 3.2 %fusion.refs_16_ = bf16[672,3584]{1,0:T(8,128)(2,1)S(1)} fusion(bf16[3,224,3584]{2,1,0:T(8,128)(2,1)} %param.32, f32[3584]{0:T(1024)S(1)} %copy-done.20), kind=kLoop, calls=%fused_computation.1 | loop fusion | flops 7225344 | bytes 9648128 | tf_op jit(solution)/shard_map/convert_element_type | solution.py:639
  144.1 3.4 %collective-permute-done.33.refs_12_ = bf16[224,512]{1,0:T(8,128)(2,1)S(1)} collective-permute-done((bf16[224,512]{1,0:T(8,128)(2,1)S(1)}, bf16[224,512]{1,0:T(8,128)(2,1)S(1)}, u32[]{:S(2)}, u32[]{:S(2)}) %collective-permute-start.33) | collective-permute-done | bytes 229408 | tf_op jit(solution)/shard_map/ppermute | solution.py:69
  147.5 1.5 collective-permute-start.35
  150.8 2.7 %collective-permute-done.35.refs_14_ = bf16[224,512]{1,0:T(8,128)(2,1)S(1)} collective-permute-done((bf16[224,512]{1,0:T(8,128)(2,1)S(1)}, bf16[224,512]{1,0:T(8,128)(2,1)S(1)}, u32[]{:S(2)}, u32[]{:S(2)}) %collective-permute-start.35) | collective-permute-done | bytes 229408 | tf_op jit(solution)/shard_map/ppermute | solution.py:73
  153.5 2.5 %collective-permute-done.36.refs_15_ = bf16[224,512]{1,0:T(8,128)(2,1)S(1)} collective-permute-done((bf16[224,512]{1,0:T(8,128)(2,1)S(1)}, bf16[224,512]{1,0:T(8,128)(2,1)S(1)}, u32[]{:S(2)}, u32[]{:S(2)}) %collective-permute-start.36) | collective-permute-done | bytes 229408 | tf_op jit(solution)/shard_map/ppermute | solution.py:75
  156.0 5.2 %shard_map.209 = (bf16[224,512]{1,0:T(8,128)(2,1)S(1)}, bf16[224,512]{1,0:T(8,128)(2,1)S(1)}, bf16[224,512]{1,0:T(8,128)(2,1)S(1)}, bf16[448,512]{1,0:T(8,128)(2,1)}) custom-call(s32[8,8]{1,0:T(8,128)S(1)} %copy-done.9, bf16[448,512]{1,0:T(8,128)(2,1)S(1)} %shard_map.208.refs_1_.refs_11_, bf16[224,512]{1,0:T(8,128)(2,1)S(1)} %collective-permute-done.23.refs_2_, ...), custom_call_target="tpu_custom_call" | custom-call | flops 2466250752 | bytes 8487168 | tf_op jit(solution)/shard_map/pallas_call | solution.py:134
  161.8 1.3 collective-permute-start.37
  163.1 1.3 collective-permute-start.40
  165.5 4.1 %all-to-all-start.1 = ((bf16[8,56,448]{2,1,0:T(8,128)(2,1)}), bf16[8,56,448]{2,1,0:T(8,128)(2,1)}, u32[]{:S(2)}, u32[]{:S(2)}) async-start(bf16[8,56,448]{2,1,0:T(8,128)(2,1)} %get-tuple-element.151), calls=%async_computation.1 | async-start | bytes 917504 | tf_op jit(solution)/shard_map/all_to_all | solution.py:552
  169.7 3.5 %collective-permute-start.38 = (bf16[224,512]{1,0:T(8,128)(2,1)S(1)}, bf16[224,512]{1,0:T(8,128)(2,1)S(1)}, u32[]{:S(2)}, u32[]{:S(2)}) collective-permute-start(bf16[224,512]{1,0:T(8,128)(2,1)S(1)} %get-tuple-element.142.refs_2_), channel_id=1, source_target_pairs={{0,16},{8,24},{1,17},{9,25},{2,18},{10,26},{3,19},{11,27},{4,20},{... | collective-permute-start | bytes 688136 | tf_op jit(solution)/shard_map/ppermute | solution.py:665
  173.2 1.3 collective-permute-start.41
  174.5 4.6 %collective-permute-done.38.refs_4_ = bf16[224,512]{1,0:T(8,128)(2,1)S(1)} collective-permute-done((bf16[224,512]{1,0:T(8,128)(2,1)S(1)}, bf16[224,512]{1,0:T(8,128)(2,1)S(1)}, u32[]{:S(2)}, u32[]{:S(2)}) %collective-permute-start.38) | collective-permute-done | bytes 229408 | tf_op jit(solution)/shard_map/ppermute | solution.py:665
  179.8 3.7 %collective-permute-done.41.refs_8_ = bf16[224,512]{1,0:T(8,128)(2,1)S(1)} collective-permute-done((bf16[224,512]{1,0:T(8,128)(2,1)S(1)}, bf16[224,512]{1,0:T(8,128)(2,1)S(1)}, u32[]{:S(2)}, u32[]{:S(2)}) %collective-permute-start.41) | collective-permute-done | bytes 229408 | tf_op jit(solution)/shard_map/ppermute | solution.py:665
  185.1 1.5 shard_map.210.refs_1_
  186.6 1.6 collective-permute-start.43
  188.7 5.8 %collective-permute-done.43.refs_2_ = bf16[224,512]{1,0:T(8,128)(2,1)S(1)} collective-permute-done((bf16[224,512]{1,0:T(8,128)(2,1)S(1)}, bf16[224,512]{1,0:T(8,128)(2,1)S(1)}, u32[]{:S(2)}, u32[]{:S(2)}) %collective-permute-start.43) | collective-permute-done | bytes 229408 | tf_op jit(solution)/shard_map/ppermute | solution.py:69
  195.5 1.5 collective-permute-start.45
  197.5 4.4 %collective-permute-done.45.refs_4_ = bf16[224,512]{1,0:T(8,128)(2,1)S(1)} collective-permute-done((bf16[224,512]{1,0:T(8,128)(2,1)S(1)}, bf16[224,512]{1,0:T(8,128)(2,1)S(1)}, u32[]{:S(2)}, u32[]{:S(2)}) %collective-permute-start.45) | collective-permute-done | bytes 229408 | tf_op jit(solution)/shard_map/ppermute | solution.py:69
  201.9 1.2 collective-permute-done.46.refs_5_
  203.1 1.5 collective-permute-start.47
  205.1 5.0 %all-gather.6.cloned.1.call-done = bf16[8,224,448]{2,1,0:T(8,128)(2,1)} async-done(((bf16[8,56,448]{2,1,0:T(8,128)(2,1)}), bf16[8,224,448]{2,1,0:T(8,128)(2,1)}) %all-gather.6.cloned.1.call-update) | async-done | bytes 1605648 | tf_op jit(solution)/shard_map/all_gather | solution.py:556
  210.1 1.5 copy-done.2
  212.2 1.5 collective-permute-start.49
  214.4 4.5 %collective-permute-start.52 = (bf16[768,64]{1,0:T(8,128)(2,1)S(1)}, bf16[768,64]{1,0:T(8,128)(2,1)S(1)}, u32[]{:S(2)}, u32[]{:S(2)}) collective-permute-start(bf16[768,64]{1,0:T(8,128)(2,1)S(1)} %add.6), channel_id=1, source_target_pairs={{0,16},{8,24},{16,0},{24,8},{1,17},{9,25},{17,1},{25,9},{2,18},{10... | collective-permute-start | bytes 294920 | tf_op jit(solution)/shard_map/ppermute | solution.py:98
  218.8 3.6 %collective-permute-done.52 = bf16[768,64]{1,0:T(8,128)(2,1)S(1)} collective-permute-done((bf16[768,64]{1,0:T(8,128)(2,1)S(1)}, bf16[768,64]{1,0:T(8,128)(2,1)S(1)}, u32[]{:S(2)}, u32[]{:S(2)}) %collective-permute-start.52) | collective-permute-done | bytes 98336 | tf_op jit(solution)/shard_map/ppermute | solution.py:98
  223.3 2.2 shard_map.212
  (121 shorter events, 38.5 us)
Async XLA Ops:
  7.2 101.9 %all-gather.4.cloned.1.call-start = ((), (), s32[]{:S(2)}) async-start(), calls=%async_computation.2 | async-start | bytes 1966080 | tf_op jit(solution)/shard_map/all_gather | solution.py:556
  8.4 9.5 %collective-permute-start = (bf16[224,512]{1,0:T(8,128)(2,1)S(1)}, bf16[224,512]{1,0:T(8,128)(2,1)S(1)}, u32[]{:S(2)}, u32[]{:S(2)}) collective-permute-start(bf16[224,512]{1,0:T(8,128)(2,1)S(1)} %get-tuple-element.83), channel_id=1, source_target_pairs={{0,2},{2,4},{4,6},{6,7},{7,5},{5,3},{3,1},{1,0},{8,10},{10,12},{12... | collective-permute-start | bytes 688136 | tf_op jit(solution)/shard_map/ppermute | solution.py:69
  11.5 8.5 %collective-permute-start.2 = (bf16[224,512]{1,0:T(8,128)(2,1)S(1)}, bf16[224,512]{1,0:T(8,128)(2,1)S(1)}, u32[]{:S(2)}, u32[]{:S(2)}) collective-permute-start(bf16[224,512]{1,0:T(8,128)(2,1)S(1)} %get-tuple-element.83), channel_id=1, source_target_pairs={{0,1},{2,0},{4,2},{6,4},{7,6},{5,7},{3,5},{1,3},{8,9},{10,8},{12,1... | collective-permute-start | bytes 688136 | tf_op jit(solution)/shard_map/ppermute | solution.py:69
  11.5 11.3 %collective-permute-start.1 = (bf16[224,512]{1,0:T(8,128)(2,1)S(1)}, bf16[224,512]{1,0:T(8,128)(2,1)S(1)}, u32[]{:S(2)}, u32[]{:S(2)}) collective-permute-start(bf16[224,512]{1,0:T(8,128)(2,1)S(1)} %get-tuple-element.84), channel_id=1, source_target_pairs={{0,2},{2,4},{4,6},{6,7},{7,5},{5,3},{3,1},{1,0},{8,10},{10,12},{12... | collective-permute-start | bytes 688136 | tf_op jit(solution)/shard_map/ppermute | solution.py:69
  13.5 11.4 %collective-permute-start.3 = (bf16[224,512]{1,0:T(8,128)(2,1)S(1)}, bf16[224,512]{1,0:T(8,128)(2,1)S(1)}, u32[]{:S(2)}, u32[]{:S(2)}) collective-permute-start(bf16[224,512]{1,0:T(8,128)(2,1)S(1)} %get-tuple-element.84), channel_id=1, source_target_pairs={{0,1},{2,0},{4,2},{6,4},{7,6},{5,7},{3,5},{1,3},{8,9},{10,8},{12,1... | collective-permute-start | bytes 688136 | tf_op jit(solution)/shard_map/ppermute | solution.py:69
  20.0 11.7 %collective-permute-start.4 = (bf16[224,512]{1,0:T(8,128)(2,1)S(1)}, bf16[224,512]{1,0:T(8,128)(2,1)S(1)}, u32[]{:S(2)}, u32[]{:S(2)}) collective-permute-start(bf16[224,512]{1,0:T(8,128)(2,1)S(1)} %collective-permute-done.refs_2_), channel_id=1, source_target_pairs={{0,2},{2,4},{4,6},{6,7},{7,5},{5,3},{3,1},{1,0},{8,10},{10,12},{12... | collective-permute-start | bytes 688136 | tf_op jit(solution)/shard_map/ppermute | solution.py:69
  21.6 10.1 %collective-permute-start.6 = (bf16[224,512]{1,0:T(8,128)(2,1)S(1)}, bf16[224,512]{1,0:T(8,128)(2,1)S(1)}, u32[]{:S(2)}, u32[]{:S(2)}) collective-permute-start(bf16[224,512]{1,0:T(8,128)(2,1)S(1)} %collective-permute-done.2.refs_4_), channel_id=1, source_target_pairs={{0,1},{2,0},{4,2},{6,4},{7,6},{5,7},{3,5},{1,3},{8,9},{10,8},{12,1... | collective-permute-start | bytes 688136 | tf_op jit(solution)/shard_map/ppermute | solution.py:69
  24.9 8.9 %collective-permute-start.5 = (bf16[224,512]{1,0:T(8,128)(2,1)S(1)}, bf16[224,512]{1,0:T(8,128)(2,1)S(1)}, u32[]{:S(2)}, u32[]{:S(2)}) collective-permute-start(bf16[224,512]{1,0:T(8,128)(2,1)S(1)} %collective-permute-done.1.refs_3_), channel_id=1, source_target_pairs={{0,2},{2,4},{4,6},{6,7},{7,5},{5,3},{3,1},{1,0},{8,10},{10,12},{12... | collective-permute-start | bytes 688136 | tf_op jit(solution)/shard_map/ppermute | solution.py:69
  26.5 7.7 %collective-permute-start.7 = (bf16[224,512]{1,0:T(8,128)(2,1)S(1)}, bf16[224,512]{1,0:T(8,128)(2,1)S(1)}, u32[]{:S(2)}, u32[]{:S(2)}) collective-permute-start(bf16[224,512]{1,0:T(8,128)(2,1)S(1)} %collective-permute-done.3.refs_5_), channel_id=1, source_target_pairs={{0,1},{2,0},{4,2},{6,4},{7,6},{5,7},{3,5},{1,3},{8,9},{10,8},{12,1... | collective-permute-start | bytes 688136 | tf_op jit(solution)/shard_map/ppermute | solution.py:69
  31.7 8.1 %collective-permute-start.8 = (bf16[224,512]{1,0:T(8,128)(2,1)S(1)}, bf16[224,512]{1,0:T(8,128)(2,1)S(1)}, u32[]{:S(2)}, u32[]{:S(2)}) collective-permute-start(bf16[224,512]{1,0:T(8,128)(2,1)S(1)} %collective-permute-done.4.refs_6_), channel_id=1, source_target_pairs={{0,2},{2,4},{4,6},{6,7},{7,5},{5,3},{3,1},{1,0},{8,10},{10,12},{12... | collective-permute-start | bytes 688136 | tf_op jit(solution)/shard_map/ppermute | solution.py:69
  33.3 7.3 %collective-permute-start.10 = (bf16[224,512]{1,0:T(8,128)(2,1)S(1)}, bf16[224,512]{1,0:T(8,128)(2,1)S(1)}, u32[]{:S(2)}, u32[]{:S(2)}) collective-permute-start(bf16[224,512]{1,0:T(8,128)(2,1)S(1)} %collective-permute-done.6.refs_8_), channel_id=1, source_target_pairs={{0,1},{2,0},{4,2},{6,4},{7,6},{5,7},{3,5},{1,3},{8,9},{10,8},{12,1... | collective-permute-start | bytes 688136 | tf_op jit(solution)/shard_map/ppermute | solution.py:69
  34.2 9.9 %collective-permute-start.9 = (bf16[224,512]{1,0:T(8,128)(2,1)S(1)}, bf16[224,512]{1,0:T(8,128)(2,1)S(1)}, u32[]{:S(2)}, u32[]{:S(2)}) collective-permute-start(bf16[224,512]{1,0:T(8,128)(2,1)S(1)} %collective-permute-done.5.refs_7_), channel_id=1, source_target_pairs={{0,2},{2,4},{4,6},{6,7},{7,5},{5,3},{3,1},{1,0},{8,10},{10,12},{12... | collective-permute-start | bytes 688136 | tf_op jit(solution)/shard_map/ppermute | solution.py:69
  35.8 8.3 %collective-permute-start.11 = (bf16[224,512]{1,0:T(8,128)(2,1)S(1)}, bf16[224,512]{1,0:T(8,128)(2,1)S(1)}, u32[]{:S(2)}, u32[]{:S(2)}) collective-permute-start(bf16[224,512]{1,0:T(8,128)(2,1)S(1)} %collective-permute-done.7.refs_9_), channel_id=1, source_target_pairs={{0,1},{2,0},{4,2},{6,4},{7,6},{5,7},{3,5},{1,3},{8,9},{10,8},{12,1... | collective-permute-start | bytes 688136 | tf_op jit(solution)/shard_map/ppermute | solution.py:69
  37.7 33.7 %copy-start.21 = (s32[4,2]{0,1:T(2,128)S(1)}, s32[4,2]{0,1:T(2,128)}, u32[]{:S(2)}) copy-start(s32[4,2]{0,1:T(2,128)} %param.36) | copy-start | bytes 100
  37.7 34.6 %copy-start.11 = (f32[4,192]{1,0:T(4,128)S(1)}, f32[4,192]{1,0:T(4,128)}, u32[]{:S(2)}) copy-start(f32[4,192]{1,0:T(4,128)} %conv_x_ref.1) | copy-start | bytes 9220
  37.7 34.6 %copy-start.12 = (f32[4,128]{1,0:T(4,128)S(1)}, f32[4,128]{1,0:T(4,128)}, u32[]{:S(2)}) copy-start(f32[4,128]{1,0:T(4,128)} %conv_bc_ref.1) | copy-start | bytes 6148
  37.7 34.6 %copy-start.13 = (s32[512]{0:T(512)S(1)}, s32[512]{0:T(512)}, u32[]{:S(2)}) copy-start(s32[512]{0:T(512)} %param.35) | copy-start | bytes 6148
  37.7 34.6 %copy-start.14 = (s32[512]{0:T(512)S(1)}, s32[512]{0:T(512)}, u32[]{:S(2)}) copy-start(s32[512]{0:T(512)} %param.34) | copy-start | bytes 6148
  37.7 34.6 %copy-start.15 = (f32[3]{0:T(128)S(1)}, f32[3]{0:T(128)}, u32[]{:S(2)}) copy-start(f32[3]{0:T(128)} %bias_ref.1) | copy-start | bytes 40
  37.8 34.5 %copy-start.16 = (f32[3]{0:T(128)S(1)}, f32[3]{0:T(128)}, u32[]{:S(2)}) copy-start(f32[3]{0:T(128)} %rate_ref.1) | copy-start | bytes 40
  37.8 34.5 %copy-start.17 = (f32[3]{0:T(128)S(1)}, f32[3]{0:T(128)}, u32[]{:S(2)}) copy-start(f32[3]{0:T(128)} %skip_ref.1) | copy-start | bytes 40
  40.6 6.0 %collective-permute-start.12 = (bf16[224,512]{1,0:T(8,128)(2,1)S(1)}, bf16[224,512]{1,0:T(8,128)(2,1)S(1)}, u32[]{:S(2)}, u32[]{:S(2)}) collective-permute-start(bf16[224,512]{1,0:T(8,128)(2,1)S(1)} %collective-permute-done.8.refs_10_), channel_id=1, source_target_pairs={{0,2},{2,4},{4,6},{6,7},{7,5},{5,3},{3,1},{1,0},{8,10},{10,12},{12... | collective-permute-start | bytes 688136 | tf_op jit(solution)/shard_map/ppermute | solution.py:73
  44.0 6.0 %collective-permute-start.13 = (bf16[224,512]{1,0:T(8,128)(2,1)S(1)}, bf16[224,512]{1,0:T(8,128)(2,1)S(1)}, u32[]{:S(2)}, u32[]{:S(2)}) collective-permute-start(bf16[224,512]{1,0:T(8,128)(2,1)S(1)} %collective-permute-done.11.refs_13_), channel_id=1, source_target_pairs={{0,1},{2,0},{4,2},{6,4},{7,6},{5,7},{3,5},{1,3},{8,9},{10,8},{12,1... | collective-permute-start | bytes 688136 | tf_op jit(solution)/shard_map/ppermute | solution.py:75
  70.2 2.1 collective-permute-start.14
  86.3 7.2 %collective-permute-start.15 = (bf16[192,512]{1,0:T(8,128)(2,1)S(1)}, bf16[192,512]{1,0:T(8,128)(2,1)S(1)}, u32[]{:S(2)}, u32[]{:S(2)}) collective-permute-start(bf16[192,512]{1,0:T(8,128)(2,1)S(1)} %get-tuple-element.114.refs_1_), channel_id=1, source_target_pairs={{0,2},{2,4},{4,6},{6,7},{7,5},{5,3},{3,1},{1,0},{8,10},{10,12},{12... | collective-permute-start | bytes 589832 | tf_op jit(solution)/shard_map/ppermute | solution.py:69
  86.7 6.9 %collective-permute-start.16 = (bf16[192,512]{1,0:T(8,128)(2,1)S(1)}, bf16[192,512]{1,0:T(8,128)(2,1)S(1)}, u32[]{:S(2)}, u32[]{:S(2)}) collective-permute-start(bf16[192,512]{1,0:T(8,128)(2,1)S(1)} %get-tuple-element.114.refs_1_), channel_id=1, source_target_pairs={{0,1},{2,0},{4,2},{6,4},{7,6},{5,7},{3,5},{1,3},{8,9},{10,8},{12,1... | collective-permute-start | bytes 589832 | tf_op jit(solution)/shard_map/ppermute | solution.py:69
  93.6 6.3 %collective-permute-start.17 = (bf16[192,512]{1,0:T(8,128)(2,1)S(1)}, bf16[192,512]{1,0:T(8,128)(2,1)S(1)}, u32[]{:S(2)}, u32[]{:S(2)}) collective-permute-start(bf16[192,512]{1,0:T(8,128)(2,1)S(1)} %collective-permute-done.15.refs_2_), channel_id=1, source_target_pairs={{0,2},{2,4},{4,6},{6,7},{7,5},{5,3},{3,1},{1,0},{8,10},{10,12},{12... | collective-permute-start | bytes 589832 | tf_op jit(solution)/shard_map/ppermute | solution.py:69
  94.5 5.7 %collective-permute-start.18 = (bf16[192,512]{1,0:T(8,128)(2,1)S(1)}, bf16[192,512]{1,0:T(8,128)(2,1)S(1)}, u32[]{:S(2)}, u32[]{:S(2)}) collective-permute-start(bf16[192,512]{1,0:T(8,128)(2,1)S(1)} %collective-permute-done.16.refs_3_), channel_id=1, source_target_pairs={{0,1},{2,0},{4,2},{6,4},{7,6},{5,7},{3,5},{1,3},{8,9},{10,8},{12,1... | collective-permute-start | bytes 589832 | tf_op jit(solution)/shard_map/ppermute | solution.py:69
  100.3 5.7 %collective-permute-start.19 = (bf16[192,512]{1,0:T(8,128)(2,1)S(1)}, bf16[192,512]{1,0:T(8,128)(2,1)S(1)}, u32[]{:S(2)}, u32[]{:S(2)}) collective-permute-start(bf16[192,512]{1,0:T(8,128)(2,1)S(1)} %collective-permute-done.17.refs_4_), channel_id=1, source_target_pairs={{0,2},{2,4},{4,6},{6,7},{7,5},{5,3},{3,1},{1,0},{8,10},{10,12},{12... | collective-permute-start | bytes 589832 | tf_op jit(solution)/shard_map/ppermute | solution.py:69
  101.2 5.7 %collective-permute-start.20 = (bf16[192,512]{1,0:T(8,128)(2,1)S(1)}, bf16[192,512]{1,0:T(8,128)(2,1)S(1)}, u32[]{:S(2)}, u32[]{:S(2)}) collective-permute-start(bf16[192,512]{1,0:T(8,128)(2,1)S(1)} %collective-permute-done.18.refs_5_), channel_id=1, source_target_pairs={{0,1},{2,0},{4,2},{6,4},{7,6},{5,7},{3,5},{1,3},{8,9},{10,8},{12,1... | collective-permute-start | bytes 589832 | tf_op jit(solution)/shard_map/ppermute | solution.py:69
  106.9 4.7 %collective-permute-start.21 = (bf16[96,512]{1,0:T(8,128)(2,1)S(1)}, bf16[96,512]{1,0:T(8,128)(2,1)S(1)}, u32[]{:S(2)}, u32[]{:S(2)}) collective-permute-start(bf16[96,512]{1,0:T(8,128)(2,1)S(1)} %slice.26), channel_id=1, source_target_pairs={{0,2},{2,4},{4,6},{6,7},{7,5},{5,3},{3,1},{1,0},{8,10},{10,12},{12... | collective-permute-start | bytes 294920 | tf_op jit(solution)/shard_map/ppermute | solution.py:71
  107.9 4.7 %collective-permute-start.22 = (bf16[96,512]{1,0:T(8,128)(2,1)S(1)}, bf16[96,512]{1,0:T(8,128)(2,1)S(1)}, u32[]{:S(2)}, u32[]{:S(2)}) collective-permute-start(bf16[96,512]{1,0:T(8,128)(2,1)S(1)} %slice.27), channel_id=1, source_target_pairs={{0,1},{2,0},{4,2},{6,4},{7,6},{5,7},{3,5},{1,3},{8,9},{10,8},{12,1... | collective-permute-start | bytes 294920 | tf_op jit(solution)/shard_map/ppermute | solution.py:71
  114.4 8.5 %collective-permute-start.23 = (bf16[224,512]{1,0:T(8,128)(2,1)S(1)}, bf16[224,512]{1,0:T(8,128)(2,1)S(1)}, u32[]{:S(2)}, u32[]{:S(2)}) collective-permute-start(bf16[224,512]{1,0:T(8,128)(2,1)S(1)} %get-tuple-element.127), channel_id=1, source_target_pairs={{0,2},{2,4},{4,6},{6,7},{7,5},{5,3},{3,1},{1,0},{8,10},{10,12},{12... | collective-permute-start | bytes 688136 | tf_op jit(solution)/shard_map/ppermute | solution.py:69
  115.2 8.2 %collective-permute-start.25 = (bf16[224,512]{1,0:T(8,128)(2,1)S(1)}, bf16[224,512]{1,0:T(8,128)(2,1)S(1)}, u32[]{:S(2)}, u32[]{:S(2)}) collective-permute-start(bf16[224,512]{1,0:T(8,128)(2,1)S(1)} %get-tuple-element.127), channel_id=1, source_target_pairs={{0,1},{2,0},{4,2},{6,4},{7,6},{5,7},{3,5},{1,3},{8,9},{10,8},{12,1... | collective-permute-start | bytes 688136 | tf_op jit(solution)/shard_map/ppermute | solution.py:69
  116.5 11.4 %collective-permute-start.24 = (bf16[224,512]{1,0:T(8,128)(2,1)S(1)}, bf16[224,512]{1,0:T(8,128)(2,1)S(1)}, u32[]{:S(2)}, u32[]{:S(2)}) collective-permute-start(bf16[224,512]{1,0:T(8,128)(2,1)S(1)} %get-tuple-element.128), channel_id=1, source_target_pairs={{0,2},{2,4},{4,6},{6,7},{7,5},{5,3},{3,1},{1,0},{8,10},{10,12},{12... | collective-permute-start | bytes 688136 | tf_op jit(solution)/shard_map/ppermute | solution.py:69
  117.3 11.1 %collective-permute-start.26 = (bf16[224,512]{1,0:T(8,128)(2,1)S(1)}, bf16[224,512]{1,0:T(8,128)(2,1)S(1)}, u32[]{:S(2)}, u32[]{:S(2)}) collective-permute-start(bf16[224,512]{1,0:T(8,128)(2,1)S(1)} %get-tuple-element.128), channel_id=1, source_target_pairs={{0,1},{2,0},{4,2},{6,4},{7,6},{5,7},{3,5},{1,3},{8,9},{10,8},{12,1... | collective-permute-start | bytes 688136 | tf_op jit(solution)/shard_map/ppermute | solution.py:69
  123.5 9.3 %collective-permute-start.27 = (bf16[224,512]{1,0:T(8,128)(2,1)S(1)}, bf16[224,512]{1,0:T(8,128)(2,1)S(1)}, u32[]{:S(2)}, u32[]{:S(2)}) collective-permute-start(bf16[224,512]{1,0:T(8,128)(2,1)S(1)} %collective-permute-done.23.refs_2_), channel_id=1, source_target_pairs={{0,2},{2,4},{4,6},{6,7},{7,5},{5,3},{3,1},{1,0},{8,10},{10,12},{12... | collective-permute-start | bytes 688136 | tf_op jit(solution)/shard_map/ppermute | solution.py:69
  124.8 8.0 %collective-permute-start.29 = (bf16[224,512]{1,0:T(8,128)(2,1)S(1)}, bf16[224,512]{1,0:T(8,128)(2,1)S(1)}, u32[]{:S(2)}, u32[]{:S(2)}) collective-permute-start(bf16[224,512]{1,0:T(8,128)(2,1)S(1)} %collective-permute-done.25.refs_4_), channel_id=1, source_target_pairs={{0,1},{2,0},{4,2},{6,4},{7,6},{5,7},{3,5},{1,3},{8,9},{10,8},{12,1... | collective-permute-start | bytes 688136 | tf_op jit(solution)/shard_map/ppermute | solution.py:69
  128.4 9.2 %collective-permute-start.28 = (bf16[224,512]{1,0:T(8,128)(2,1)S(1)}, bf16[224,512]{1,0:T(8,128)(2,1)S(1)}, u32[]{:S(2)}, u32[]{:S(2)}) collective-permute-start(bf16[224,512]{1,0:T(8,128)(2,1)S(1)} %collective-permute-done.24.refs_3_), channel_id=1, source_target_pairs={{0,2},{2,4},{4,6},{6,7},{7,5},{5,3},{3,1},{1,0},{8,10},{10,12},{12... | collective-permute-start | bytes 688136 | tf_op jit(solution)/shard_map/ppermute | solution.py:69
  129.7 8.4 %collective-permute-start.30 = (bf16[224,512]{1,0:T(8,128)(2,1)S(1)}, bf16[224,512]{1,0:T(8,128)(2,1)S(1)}, u32[]{:S(2)}, u32[]{:S(2)}) collective-permute-start(bf16[224,512]{1,0:T(8,128)(2,1)S(1)} %collective-permute-done.26.refs_5_), channel_id=1, source_target_pairs={{0,1},{2,0},{4,2},{6,4},{7,6},{5,7},{3,5},{1,3},{8,9},{10,8},{12,1... | collective-permute-start | bytes 688136 | tf_op jit(solution)/shard_map/ppermute | solution.py:69
  132.8 11.3 %collective-permute-start.31 = (bf16[224,512]{1,0:T(8,128)(2,1)S(1)}, bf16[224,512]{1,0:T(8,128)(2,1)S(1)}, u32[]{:S(2)}, u32[]{:S(2)}) collective-permute-start(bf16[224,512]{1,0:T(8,128)(2,1)S(1)} %collective-permute-done.27.refs_6_), channel_id=1, source_target_pairs={{0,2},{2,4},{4,6},{6,7},{7,5},{5,3},{3,1},{1,0},{8,10},{10,12},{12... | collective-permute-start | bytes 688136 | tf_op jit(solution)/shard_map/ppermute | solution.py:69
  138.2 10.8 %collective-permute-start.32 = (bf16[224,512]{1,0:T(8,128)(2,1)S(1)}, bf16[224,512]{1,0:T(8,128)(2,1)S(1)}, u32[]{:S(2)}, u32[]{:S(2)}) collective-permute-start(bf16[224,512]{1,0:T(8,128)(2,1)S(1)} %collective-permute-done.28.refs_7_), channel_id=1, source_target_pairs={{0,2},{2,4},{4,6},{6,7},{7,5},{5,3},{3,1},{1,0},{8,10},{10,12},{12... | collective-permute-start | bytes 688136 | tf_op jit(solution)/shard_map/ppermute | solution.py:69
  140.1 7.4 %collective-permute-start.33 = (bf16[224,512]{1,0:T(8,128)(2,1)S(1)}, bf16[224,512]{1,0:T(8,128)(2,1)S(1)}, u32[]{:S(2)}, u32[]{:S(2)}) collective-permute-start(bf16[224,512]{1,0:T(8,128)(2,1)S(1)} %collective-permute-done.29.refs_8_), channel_id=1, source_target_pairs={{0,1},{2,0},{4,2},{6,4},{7,6},{5,7},{3,5},{1,3},{8,9},{10,8},{12,1... | collective-permute-start | bytes 688136 | tf_op jit(solution)/shard_map/ppermute | solution.py:69
  140.2 9.8 %collective-permute-start.34 = (bf16[224,512]{1,0:T(8,128)(2,1)S(1)}, bf16[224,512]{1,0:T(8,128)(2,1)S(1)}, u32[]{:S(2)}, u32[]{:S(2)}) collective-permute-start(bf16[224,512]{1,0:T(8,128)(2,1)S(1)} %collective-permute-done.30.refs_9_), channel_id=1, source_target_pairs={{0,1},{2,0},{4,2},{6,4},{7,6},{5,7},{3,5},{1,3},{8,9},{10,8},{12,1... | collective-permute-start | bytes 688136 | tf_op jit(solution)/shard_map/ppermute | solution.py:69
  147.5 6.0 %collective-permute-start.35 = (bf16[224,512]{1,0:T(8,128)(2,1)S(1)}, bf16[224,512]{1,0:T(8,128)(2,1)S(1)}, u32[]{:S(2)}, u32[]{:S(2)}) collective-permute-start(bf16[224,512]{1,0:T(8,128)(2,1)S(1)} %collective-permute-done.31.refs_10_), channel_id=1, source_target_pairs={{0,2},{2,4},{4,6},{6,7},{7,5},{5,3},{3,1},{1,0},{8,10},{10,12},{12... | collective-permute-start | bytes 688136 | tf_op jit(solution)/shard_map/ppermute | solution.py:73
  149.9 6.0 %collective-permute-start.36 = (bf16[224,512]{1,0:T(8,128)(2,1)S(1)}, bf16[224,512]{1,0:T(8,128)(2,1)S(1)}, u32[]{:S(2)}, u32[]{:S(2)}) collective-permute-start(bf16[224,512]{1,0:T(8,128)(2,1)S(1)} %collective-permute-done.34.refs_13_), channel_id=1, source_target_pairs={{0,1},{2,0},{4,2},{6,4},{7,6},{5,7},{3,5},{1,3},{8,9},{10,8},{12,1... | collective-permute-start | bytes 688136 | tf_op jit(solution)/shard_map/ppermute | solution.py:75
  161.8 2.6 %collective-permute-start.37 = (bf16[224,512]{1,0:T(8,128)(2,1)S(1)}, bf16[224,512]{1,0:T(8,128)(2,1)S(1)}, u32[]{:S(2)}, u32[]{:S(2)}) collective-permute-start(bf16[224,512]{1,0:T(8,128)(2,1)S(1)} %get-tuple-element.142.refs_2_), channel_id=1, source_target_pairs={{0,8},{16,24},{1,9},{17,25},{2,10},{18,26},{3,11},{19,27},{4,12},{... | collective-permute-start | bytes 688136 | tf_op jit(solution)/shard_map/ppermute | solution.py:662
  163.1 2.4 %collective-permute-start.40 = (bf16[224,512]{1,0:T(8,128)(2,1)S(1)}, bf16[224,512]{1,0:T(8,128)(2,1)S(1)}, u32[]{:S(2)}, u32[]{:S(2)}) collective-permute-start(bf16[224,512]{1,0:T(8,128)(2,1)S(1)} %get-tuple-element.143.refs_6_), channel_id=1, source_target_pairs={{0,8},{16,24},{1,9},{17,25},{2,10},{18,26},{3,11},{19,27},{4,12},{... | collective-permute-start | bytes 688136 | tf_op jit(solution)/shard_map/ppermute | solution.py:662
  165.5 18.6 %all-to-all-start.1 = ((bf16[8,56,448]{2,1,0:T(8,128)(2,1)}), bf16[8,56,448]{2,1,0:T(8,128)(2,1)}, u32[]{:S(2)}, u32[]{:S(2)}) async-start(bf16[8,56,448]{2,1,0:T(8,128)(2,1)} %get-tuple-element.151), calls=%async_computation.1 | async-start | bytes 917504 | tf_op jit(solution)/shard_map/all_to_all | solution.py:552
  169.6 40.5 %all-gather.6.cloned.1.call-start = ((), (), s32[]{:S(2)}) async-start(), calls=%async_computation.3 | async-start | bytes 2293760 | tf_op jit(solution)/shard_map/all_gather | solution.py:556
  169.7 9.4 %collective-permute-start.38 = (bf16[224,512]{1,0:T(8,128)(2,1)S(1)}, bf16[224,512]{1,0:T(8,128)(2,1)S(1)}, u32[]{:S(2)}, u32[]{:S(2)}) collective-permute-start(bf16[224,512]{1,0:T(8,128)(2,1)S(1)} %get-tuple-element.142.refs_2_), channel_id=1, source_target_pairs={{0,16},{8,24},{1,17},{9,25},{2,18},{10,26},{3,19},{11,27},{4,20},{... | collective-permute-start | bytes 688136 | tf_op jit(solution)/shard_map/ppermute | solution.py:665
  173.2 10.3 %collective-permute-start.41 = (bf16[224,512]{1,0:T(8,128)(2,1)S(1)}, bf16[224,512]{1,0:T(8,128)(2,1)S(1)}, u32[]{:S(2)}, u32[]{:S(2)}) collective-permute-start(bf16[224,512]{1,0:T(8,128)(2,1)S(1)} %get-tuple-element.143.refs_6_), channel_id=1, source_target_pairs={{0,16},{8,24},{1,17},{9,25},{2,18},{10,26},{3,19},{11,27},{4,20},{... | collective-permute-start | bytes 688136 | tf_op jit(solution)/shard_map/ppermute | solution.py:665
  179.1 5.0 %collective-permute-start.39 = (bf16[224,512]{1,0:T(8,128)(2,1)S(1)}, bf16[224,512]{1,0:T(8,128)(2,1)S(1)}, u32[]{:S(2)}, u32[]{:S(2)}) collective-permute-start(bf16[224,512]{1,0:T(8,128)(2,1)S(1)} %collective-permute-done.38.refs_4_), channel_id=1, source_target_pairs={{16,24},{24,16},{17,25},{25,17},{18,26},{26,18},{19,27},{27,19},{2... | collective-permute-start | bytes 688136 | tf_op jit(solution)/shard_map/ppermute | solution.py:668
  183.4 0.7 collective-permute-start.42
  186.6 7.9 %collective-permute-start.43 = (bf16[224,512]{1,0:T(8,128)(2,1)S(1)}, bf16[224,512]{1,0:T(8,128)(2,1)S(1)}, u32[]{:S(2)}, u32[]{:S(2)}) collective-permute-start(bf16[224,512]{1,0:T(8,128)(2,1)S(1)} %shard_map.210.refs_1_), channel_id=1, source_target_pairs={{0,2},{2,4},{4,6},{6,7},{7,5},{5,3},{3,1},{1,0},{8,10},{10,12},{12... | collective-permute-start | bytes 688136 | tf_op jit(solution)/shard_map/ppermute | solution.py:69
  188.2 7.3 %collective-permute-start.44 = (bf16[224,512]{1,0:T(8,128)(2,1)S(1)}, bf16[224,512]{1,0:T(8,128)(2,1)S(1)}, u32[]{:S(2)}, u32[]{:S(2)}) collective-permute-start(bf16[224,512]{1,0:T(8,128)(2,1)S(1)} %shard_map.210.refs_1_), channel_id=1, source_target_pairs={{0,1},{2,0},{4,2},{6,4},{7,6},{5,7},{3,5},{1,3},{8,9},{10,8},{12,1... | collective-permute-start | bytes 688136 | tf_op jit(solution)/shard_map/ppermute | solution.py:69
  195.5 6.4 %collective-permute-start.45 = (bf16[224,512]{1,0:T(8,128)(2,1)S(1)}, bf16[224,512]{1,0:T(8,128)(2,1)S(1)}, u32[]{:S(2)}, u32[]{:S(2)}) collective-permute-start(bf16[224,512]{1,0:T(8,128)(2,1)S(1)} %collective-permute-done.43.refs_2_), channel_id=1, source_target_pairs={{0,2},{2,4},{4,6},{6,7},{7,5},{5,3},{3,1},{1,0},{8,10},{10,12},{12... | collective-permute-start | bytes 688136 | tf_op jit(solution)/shard_map/ppermute | solution.py:69
  197.0 6.1 %collective-permute-start.46 = (bf16[224,512]{1,0:T(8,128)(2,1)S(1)}, bf16[224,512]{1,0:T(8,128)(2,1)S(1)}, u32[]{:S(2)}, u32[]{:S(2)}) collective-permute-start(bf16[224,512]{1,0:T(8,128)(2,1)S(1)} %collective-permute-done.44.refs_3_), channel_id=1, source_target_pairs={{0,1},{2,0},{4,2},{6,4},{7,6},{5,7},{3,5},{1,3},{8,9},{10,8},{12,1... | collective-permute-start | bytes 688136 | tf_op jit(solution)/shard_map/ppermute | solution.py:69
  203.1 9.0 %collective-permute-start.47 = (bf16[224,512]{1,0:T(8,128)(2,1)S(1)}, bf16[224,512]{1,0:T(8,128)(2,1)S(1)}, u32[]{:S(2)}, u32[]{:S(2)}) collective-permute-start(bf16[224,512]{1,0:T(8,128)(2,1)S(1)} %collective-permute-done.45.refs_4_), channel_id=1, source_target_pairs={{0,2},{2,4},{4,6},{6,7},{7,5},{5,3},{3,1},{1,0},{8,10},{10,12},{12... | collective-permute-start | bytes 688136 | tf_op jit(solution)/shard_map/ppermute | solution.py:69
  204.6 7.6 %collective-permute-start.48 = (bf16[224,512]{1,0:T(8,128)(2,1)S(1)}, bf16[224,512]{1,0:T(8,128)(2,1)S(1)}, u32[]{:S(2)}, u32[]{:S(2)}) collective-permute-start(bf16[224,512]{1,0:T(8,128)(2,1)S(1)} %collective-permute-done.46.refs_5_), channel_id=1, source_target_pairs={{0,1},{2,0},{4,2},{6,4},{7,6},{5,7},{3,5},{1,3},{8,9},{10,8},{12,1... | collective-permute-start | bytes 688136 | tf_op jit(solution)/shard_map/ppermute | solution.py:69
  205.1 9.2 %collective-permute-start.51 = (bf16[768,64]{1,0:T(8,128)(2,1)S(1)}, bf16[768,64]{1,0:T(8,128)(2,1)S(1)}, u32[]{:S(2)}, u32[]{:S(2)}) collective-permute-start(bf16[768,64]{1,0:T(8,128)(2,1)S(1)} %get-tuple-element.158), channel_id=1, source_target_pairs={{0,8},{8,0},{16,24},{24,16},{1,9},{9,1},{17,25},{25,17},{2,10},{10... | collective-permute-start | bytes 294920 | tf_op jit(solution)/shard_map/ppermute | solution.py:98
  212.2 11.2 %collective-permute-start.49 = (bf16[112,512]{1,0:T(8,128)(2,1)S(1)}, bf16[112,512]{1,0:T(8,128)(2,1)S(1)}, u32[]{:S(2)}, u32[]{:S(2)}) collective-permute-start(bf16[112,512]{1,0:T(8,128)(2,1)S(1)} %slice.30), channel_id=1, source_target_pairs={{0,2},{2,4},{4,6},{6,7},{7,5},{5,3},{3,1},{1,0},{8,10},{10,12},{12... | collective-permute-start | bytes 344072 | tf_op jit(solution)/shard_map/ppermute | solution.py:71
  213.7 9.6 %collective-permute-start.50 = (bf16[112,512]{1,0:T(8,128)(2,1)S(1)}, bf16[112,512]{1,0:T(8,128)(2,1)S(1)}, u32[]{:S(2)}, u32[]{:S(2)}) collective-permute-start(bf16[112,512]{1,0:T(8,128)(2,1)S(1)} %slice.31), channel_id=1, source_target_pairs={{0,1},{2,0},{4,2},{6,4},{7,6},{5,7},{3,5},{1,3},{8,9},{10,8},{12,1... | collective-permute-start | bytes 344072 | tf_op jit(solution)/shard_map/ppermute | solution.py:71
  214.4 8.1 %collective-permute-start.52 = (bf16[768,64]{1,0:T(8,128)(2,1)S(1)}, bf16[768,64]{1,0:T(8,128)(2,1)S(1)}, u32[]{:S(2)}, u32[]{:S(2)}) collective-permute-start(bf16[768,64]{1,0:T(8,128)(2,1)S(1)} %add.6), channel_id=1, source_target_pairs={{0,16},{8,24},{16,0},{24,8},{1,17},{9,25},{17,1},{25,9},{2,18},{10... | collective-permute-start | bytes 294920 | tf_op jit(solution)/shard_map/ppermute | solution.py:98
  (14 other events, 128.5 us)
Sparse Core Ops, SparseCore 0:
  70.3 19.2 all-gather.3
  184.3 25.7 all-gather.5

commit v3 on v2

--- a/solution.py
+++ b/solution.py
@@ -43,18 +43,17 @@
     return table
 
 
-def ring_gather(piece, axis, count, split=False, tasks=()):
+def ring_gather(parts, axis, count, tasks=()):
     order = ring_order(count)
     ahead = [(order[i], order[(i + 1) % count]) for i in range(count)]
     behind = [(order[i], order[(i - 1) % count]) for i in range(count)]
-    half = piece.shape[0] // 2
-    split = split and half % 16 == 0
-    parts = [piece[:half], piece[half:]] if split else [piece]
+    half = parts[0].shape[0] // 2
+    split = len(parts) > 1
     far_hop = (count - 1) // 2 + 1
     last_hop = far_hop if count % 2 == 0 else far_hop - 1
     here = {(0, i): (part, part) for i, part in enumerate(parts)}
     results = [None] * len(tasks)
-    finished = [(piece,)]
+    finished = [tuple(parts)]
     step = 0
     for hop in range(1, last_hop + 1):
         for i in range(len(parts)):
@@ -80,15 +79,13 @@
                     results[t] = task[2]([value for pair in recent for value in pair])
             finished.append(got)
             step += 1
-    pieces = [piece]
+    pieces = [[part] for part in parts]
     for hop in range(1, last_hop + 1):
-        if hop < far_hop:
-            for side in range(2):
-                pieces += [here[hop, i][side] for i in range(len(parts))]
-        elif not split and half % 16 == 0:
-            pieces += list(here[hop, 0])
-        else:
-            pieces += [here[hop, i][0] for i in range(len(parts))]
+        for i in range(len(parts)):
+            if hop < far_hop or (not split and half % 16 == 0):
+                pieces[i] += list(here[hop, i])
+            else:
+                pieces[i].append(here[hop, i][0])
     return pieces, results
 
 
@@ -125,12 +122,12 @@
 
 def call(kernel, out_shape, operands, smem=(), scratch=(), flops=0, vmem=12):
     specs = [
-        pl.BlockSpec(
-            memory_space=pltpu.SMEM if i in smem else pltpu.VMEM
+        jax.tree.map(
+            lambda _, i=i: pl.BlockSpec(memory_space=pltpu.SMEM if i in smem else pltpu.VMEM), o
         )
-        for i in range(len(operands))
+        for i, o in enumerate(operands)
     ]
-    size = sum(o.size * o.dtype.itemsize for o in operands)
+    size = sum(o.size * o.dtype.itemsize for o in jax.tree.leaves(operands))
     return pl.pallas_call(
         kernel,
         out_shape=out_shape,
@@ -225,8 +222,8 @@
     bias_ref,
     rate_ref,
     skip_ref,
-    raw_ref,
-    dt_ref,
+    raw_refs,
+    dt_refs,
     halo_ref,
     conv_x_ref,
     conv_bc_ref,
@@ -242,7 +239,8 @@
     xdt_ref,
     taps_ref,
 ):
-    conv_rows, toks = raw_ref.shape
+    conv_rows, half = raw_refs[0].shape
+    toks = half * len(raw_refs)
     inner = y_ref.shape[0]
     hd = inner // heads
     lane = lax.broadcasted_iota(jnp.int32, (1, toks), 1)
@@ -259,7 +257,8 @@
         rate = jnp.where(head == h, rate_ref[h], rate)
     before = jnp.concatenate([jnp.zeros((120, conv_rows), F32), halo_ref[...]], axis=0).T
     ext_ref[:, :128] = before
-    ext_ref[:, 128:] = raw_ref[...]
+    for i, raw_ref in enumerate(raw_refs):
+        ext_ref[:, 128 + i * half : 128 + (i + 1) * half] = raw_ref[...]
     strip = 64
     keep = [(rel >= shift).astype(F32) for shift in range(4)]
     for i in range(conv_rows // strip):
@@ -271,7 +270,7 @@
             moved = pltpu.roll(ext, shift, 1)[:, 128:]
             total = total + taps[:, 3 - shift : 4 - shift] * moved * keep[shift]
         x_ref[rows, :] = silu(total)
-    step = dt_ref[...] + bias
+    step = jnp.concatenate([dt_ref[...] for dt_ref in dt_refs], axis=1) + bias
     step = (jnp.maximum(step, 0.0) + jnp.log1p(jnp.exp(-jnp.abs(step)))) * live
     logs = -step * rate
     shift = 1
@@ -348,7 +347,7 @@
     bounds_ref,
     pay_ref,
     y_ref,
-    z_ref,
+    z_refs,
     c_ref,
     entry_ref,
     local_ref,
@@ -356,6 +355,7 @@
     tenant_ref,
 ):
     inner = y_ref.shape[0]
+    half = z_refs[0].shape[1]
     hd = inner // heads
     incoming = jnp.zeros((inner, 64), F32)
     for block in range(pay_ref.shape[0] - 1):
@@ -366,7 +366,9 @@
         rows = slice(h * hd, (h + 1) * hd)
         carry = jnp.dot(incoming[rows, :].astype(BF16), c_ref[...], preferred_element_type=F32)
         y_full = y_ref[rows, :] + carry * entry_ref[h : h + 1, :]
-        g_ref[rows, :] = (y_full * silu(z_ref[rows, :])).astype(BF16)
+        for i, z_ref in enumerate(z_refs):
+            here = slice(i * half, (i + 1) * half)
+            g_ref[rows, here] = (y_full[:, here] * silu(z_ref[rows, :])).astype(BF16)
     for k in range(tenants):
         rows = slice(k * inner, (k + 1) * inner)
         last = bounds_ref[k, 1] - 1 - lax.axis_index("seq") * y_ref.shape[1]
@@ -378,41 +380,39 @@
 def mixed_kernel(pieces, rows, *refs):
     slots_ref = refs[0]
     piece_refs = refs[1 : 1 + pieces]
-    w_ref, hidden_ref, out_ref, full_ref = refs[1 + pieces :]
+    w_ref, hidden_refs, *out_refs, full_ref = refs[1 + pieces :]
+    squares = lay_out(slots_ref, piece_refs, rows, full_ref)
+    scale = lax.rsqrt(squares / full_ref.shape[0] + EPS)
+    product = jnp.dot(w_ref[...], full_ref[...], preferred_element_type=F32) * scale
+    half = out_refs[0].shape[1]
+    for i, (hidden_ref, out_ref) in enumerate(zip(hidden_refs, out_refs, strict=True)):
+        here = slice(i * half, (i + 1) * half)
+        out_ref[...] = (hidden_ref[...].astype(F32) + product[:, here]).astype(BF16)
+
+
+def qkv_kernel(rows, slots_ref, piece_refs, w_ref, first_refs, q_ref, kv_ref, all_refs, full_ref):
     squares = lay_out(slots_ref, piece_refs, rows, full_ref)
     scale = lax.rsqrt(squares / full_ref.shape[0] + EPS)
     product = jnp.dot(w_ref[...], full_ref[...], preferred_element_type=F32)
-    out_ref[...] = (hidden_ref[...].astype(F32) + product * scale).astype(BF16)
-
-
-def qkv_kernel(pieces, rows, *refs):
-    slots_ref = refs[0]
-    piece_refs = refs[1 : 1 + pieces]
-    w_ref, q_ref, k_ref, v_ref, kv_ref, full_ref = refs[1 + pieces :]
-    squares = lay_out(slots_ref, piece_refs, rows, full_ref)
-    scale = lax.rsqrt(squares / full_ref.shape[0] + EPS)
-    product = jnp.dot(w_ref[...], full_ref[...], preferred_element_type=F32)
-    att = q_ref.shape[0]
+    att, half = q_ref.shape
     q_ref[...] = (product[:att] * scale).astype(BF16)
-    keys = (product[att : 2 * att] * scale).astype(BF16)
-    values = (product[2 * att :] * scale).astype(BF16)
-    k_ref[...] = keys
-    v_ref[...] = values
-    kv_ref[:att, :] = keys
-    kv_ref[att:, :] = values
+    kv_ref[...] = (product[att:] * scale).astype(BF16)
+    for first_ref, all_ref in zip(first_refs, all_refs, strict=True):
+        all_ref[:, :half] = first_ref[...]
+        all_ref[:, half:] = kv_ref[...]
 
 
 def attend_kernel(blocks, block_of, score_scale, *refs):
-    bounds_ref, q_ref = refs[:2]
-    k_refs = refs[2 : 2 + blocks]
-    v_refs = refs[2 + blocks : 2 + 2 * blocks]
-    pay_ref, seg_ref, ctx_ref, q_aug, k_aug, peak_ref, total_ref, sum_ref = refs[2 + 2 * blocks :]
+    bounds_ref, q_refs, kv_refs, pay_ref, seg_ref = refs[:5]
+    ctx_ref, q_aug, k_aug, v_all, peak_ref, total_ref, sum_ref = refs[5:]
     inner = pay_ref.shape[1] - 16
     seq = lax.axis_index("seq")
-    att, toks = q_ref.shape
+    att, toks = ctx_ref.shape
+    half = q_refs[0].shape[1]
     extra = q_aug.shape[0] - att
     row = lax.broadcasted_iota(jnp.int32, (extra, toks), 0)
-    q_aug[:att, :] = q_ref[...]
+    for i, q_ref in enumerate(q_refs):
+        q_aug[:att, i * half : (i + 1) * half] = q_ref[...]
     q_aug[att:, :] = jnp.where(row == 0, 1.0, 0.0).astype(BF16)
     place = seq * toks + lax.broadcasted_iota(jnp.int32, (1, toks), 1)
     start = run_starts(seg_ref, bounds_ref)
@@ -425,8 +425,10 @@
 
         @pl.when((block >= 0) & (block <= seq) & (block * toks + toks > first_start))
         def _(b=b, block=block):
-            count = k_refs[b].shape[1]
-            k_aug[:att, :] = k_refs[b][...]
+            count = toks
+            for i, kv_ref in enumerate(kv_refs[b]):
+                k_aug[:att, i * half : (i + 1) * half] = kv_ref[:att, :]
+                v_all[:, i * half : (i + 1) * half] = kv_ref[att:, :]
             pads = pay_ref[block, inner:, :].astype(F32)
             pads = jnp.concatenate([pads[i : i + 1, :] for i in range(count // 128)], axis=1)
             bias = (pads - 1.0) * 1e30
@@ -445,7 +447,7 @@
             peak_ref[...] = peak
             total_ref[...] = total_ref[...] * keep + jnp.sum(weights, axis=0, keepdims=True)
             sum_ref[...] = sum_ref[...] * keep + jnp.dot(
-                v_refs[b][...], weights.astype(BF16), preferred_element_type=F32
+                v_all[...], weights.astype(BF16), preferred_element_type=F32
             )
 
     ctx_ref[...] = (sum_ref[...] / total_ref[...]).astype(BF16)
@@ -454,10 +456,13 @@
 def last_kernel(pieces, rows, *refs):
     slots_ref = refs[0]
     piece_refs = refs[1 : 1 + pieces]
-    w_ref, mixed_ref, out_ref, full_ref = refs[1 + pieces :]
+    w_ref, mixed_refs, out_ref, full_ref = refs[1 + pieces :]
     lay_out(slots_ref, piece_refs, rows, full_ref)
     product = jnp.dot(w_ref[...], full_ref[...], preferred_element_type=F32)
-    out_ref[...] = (mixed_ref[...].astype(F32) + product).T.astype(BF16)
+    half = mixed_refs[0].shape[1]
+    for i, mixed_ref in enumerate(mixed_refs):
+        here = slice(i * half, (i + 1) * half)
+        out_ref[here, :] = (mixed_ref[...].astype(F32) + product[:, here]).T.astype(BF16)
 
 
 def on_device(
@@ -493,7 +498,9 @@
     seq = lax.axis_index("seq")
     sds = jax.ShapeDtypeStruct
 
-    hidden_t = hidden_in.T
+    halves = 2
+    half = toks // halves
+    hidden_t = [hidden_in[i * half : (i + 1) * half].T for i in range(halves)]
     slots = jnp.asarray(sources(tp_count))
     seg_row, pad_row = seg_ids[None, :], pad_mask[None, :]
 
@@ -556,27 +563,31 @@
         return lax.all_gather(value, "seq", axis=1, tiled=True)
 
     full_in, ((out_shares, o_shares), w_in) = ring_gather(
-        hidden_t, "tp", tp_count, True, ((1, 3, shares), (3, 5, in_weights))
-    )
-    pieces = len(full_in)
-
-    raw, z, dt_raw, tail = call(
-        functools.partial(in_kernel, pieces, part, conv_rows, inner),
-        (
-            sds((conv_rows, toks), F32),
-            sds((inner, toks), F32),
-            sds((8, toks), F32),
-            sds((8, conv_rows), F32),
+        hidden_t, "tp", tp_count, ((1, 3, shares), (3, 5, in_weights))
+    )
+    pieces = len(full_in[0])
+
+    raws, zs, dts, tails = zip(
+        *(
+            call(
+                functools.partial(in_kernel, pieces, part, conv_rows, inner),
+                (
+                    sds((conv_rows, half), F32),
+                    sds((inner, half), F32),
+                    sds((8, half), F32),
+                    sds((8, conv_rows), F32),
+                ),
+                (slots, *full, w_in),
+                smem=(0,),
+                scratch=[pltpu.VMEM((width, half), BF16), pltpu.VMEM((in_rows, half), F32)],
+                flops=2 * in_rows * width * half,
+            )
+            for full in full_in
         ),
-        (slots, *full_in, w_in),
-        smem=(0,),
-        scratch=[
-            pltpu.VMEM((width, toks), BF16),
-            pltpu.VMEM((in_rows, toks), F32),
-        ],
-        flops=2 * in_rows * width * toks,
-    )
-    w_out_cols = spread(exchange(out_shares, tail), tail)
+        strict=True,
+    )
+    tail = tails[-1]
+    out_columns = exchange(out_shares, tails)
     halo = lax.ppermute(tail, "seq", [(i, i + 1) for i in range(seq_count - 1)])
     y, c_rows, entry, pay, local = call(
         functools.partial(mix_kernel, tenants, heads),
@@ -587,7 +598,7 @@
             sds((inner + 16, 128), BF16),
             sds((tenants * inner, 128), F32),
         ),
-        (tenant_bounds, dt_bias, decay_rate, skip_gain, raw, dt_raw, halo, conv_x, conv_bc, seg_row, pad_row),
+        (tenant_bounds, dt_bias, decay_rate, skip_gain, raws, dts, halo, conv_x, conv_bc, seg_row, pad_row),
         smem=(0, 1, 2, 3),
         scratch=[
             pltpu.VMEM((conv_rows, toks + 128), F32),
@@ -597,19 +608,22 @@
         ],
         flops=10**9,
     )
+    w_out_cols = spread(out_columns, pay)
     all_pays = lax.all_gather(pay, "seq", axis=0, tiled=False)
     gated, tenant_part = call(
         functools.partial(gate_kernel, tenants, heads),
-        (sds((inner, toks), BF16), sds((tenants * inner, bc // 2), BF16)),
-        (tenant_bounds, all_pays, y, z, c_rows, entry, local),
+        (
+            sds((inner, toks), BF16),
+            sds((tenants * inner, bc // 2), BF16),
+        ),
+        (tenant_bounds, all_pays, y, zs, c_rows, entry, local),
         smem=(0,),
         flops=10**8,
     )
-    tenant_states = (
-        sum_pairs(tenant_part, "seq", seq_count)
-        .astype(F32)
-        .reshape(tenants, heads, inner // heads, bc // 2)
-    )
+    def tenant_sums(first):
+        value, _ = after((tenant_part,), first)
+        return sum_pairs(value, "seq", seq_count)
+
     def turned(cols, rows):
         def task(first):
             value, _ = after((cols,), first)
@@ -621,40 +635,42 @@
 
         return task
 
-    full_gated, (w_out_t,) = ring_gather(
-        gated, "tp", tp_count, False, ((3, -1, turned(w_out_cols, inner)),)
-    )
+    (full_gated,), (tenant_sum, w_out_t) = ring_gather(
+        [gated], "tp", tp_count, ((0, 2, tenant_sums), (3, -1, turned(w_out_cols, inner)))
+    )
+    tenant_states = tenant_sum.astype(F32).reshape(tenants, heads, inner // heads, bc // 2)
     mixed = call(
         functools.partial(mixed_kernel, len(full_gated), inner),
-        sds((part, toks), BF16),
+        [sds((part, half), BF16) for _ in range(halves)],
         (slots, *full_gated, w_out_t, hidden_t),
         smem=(0,),
-        scratch=[
-            pltpu.VMEM((tp_count * inner, toks), BF16),
-        ],
+        scratch=[pltpu.VMEM((tp_count * inner, toks), BF16)],
         flops=2 * part * tp_count * inner * toks,
     )
+
     def att_weights(first):
         value, _ = after((w_qkv,), first)
         return (value.reshape(3 * att, width).astype(F32) * attn_gain).astype(BF16)
 
-    full_mixed, (w_att,) = ring_gather(mixed, "tp", tp_count, True, ((4, 5, att_weights),))
-    queries, keys, values, kv = call(
-        functools.partial(qkv_kernel, len(full_mixed), part),
-        (
-            sds((att, toks), BF16),
-            sds((att, toks), BF16),
-            sds((att, toks), BF16),
-            sds((2 * att, toks), BF16),
-        ),
-        (slots, *full_mixed, w_att),
-        smem=(0,),
-        scratch=[
-            pltpu.VMEM((width, toks), BF16),
-        ],
-        flops=6 * att * width * toks,
-    )
-    kv_cache = kv.reshape(2, att, toks)
+    full_mixed, (w_att,) = ring_gather(mixed, "tp", tp_count, ((4, 5, att_weights),))
+    queries, kvs = [], []
+    for i, full in enumerate(full_mixed):
+        last = i == halves - 1
+        q_half, kv_half, whole = call(
+            functools.partial(qkv_kernel, part),
+            (
+                sds((att, half), BF16),
+                sds((2 * att, half), BF16),
+                [sds((2 * att, toks), BF16)] if last else [],
+            ),
+            (slots, full, w_att, kvs if last else []),
+            smem=(0,),
+            scratch=[pltpu.VMEM((width, half), BF16)],
+            flops=6 * att * width * half,
+        )
+        queries.append(q_half)
+        kvs.append(kv_half)
+    kv_cache = whole[0].reshape(2, att, toks)
 
     if seq_count == 4:
 
@@ -667,46 +683,43 @@
         def swap(value):
             return lax.ppermute(value, "seq", [(2, 3), (3, 2)])
 
-        far_keys, far_values = far(keys), far(values)
-        near_keys, near_values = near(keys), near(values)
-        o_columns = exchange(o_shares, (near_keys, near_values))
-        swap_keys, swap_values = swap(far_keys), swap(far_values)
-        w_o_cols = spread(o_columns, (swap_keys, swap_values))
-        key_blocks = [keys, near_keys, far_keys, swap_keys]
-        value_blocks = [values, near_values, far_values, swap_values]
-
+        fars = [far(kv) for kv in kvs]
+        nears = [near(kv) for kv in kvs]
+        o_columns = exchange(o_shares, (fars, nears))
+        swaps = [swap(kv) for kv in fars]
+        w_o_cols = spread(o_columns, swaps)
+        kv_blocks = [kvs, nears, fars, swaps]
 
         def block_of(b, at):
             return (at, at ^ 1, at - 2, (at ^ 1) - 2)[b]
 
     else:
-        all_keys = lax.all_gather(keys, "seq", axis=0, tiled=False)
-        all_values = lax.all_gather(values, "seq", axis=0, tiled=False)
-        w_o_cols = spread(exchange(o_shares, keys), keys)
-        key_blocks = [all_keys[i] for i in range(seq_count)]
-        value_blocks = [all_values[i] for i in range(seq_count)]
+        all_kv = [lax.all_gather(kv, "seq", axis=0, tiled=False) for kv in kvs]
+        w_o_cols = spread(exchange(o_shares, kvs), kvs)
+        kv_blocks = [[kv[i] for kv in all_kv] for i in range(seq_count)]
 
         def block_of(b, at):
             return jnp.int32(b)
 
-    blocks = len(key_blocks)
+    blocks = len(kv_blocks)
     deep = att + 32
     context = call(
         functools.partial(attend_kernel, blocks, block_of, att ** (-0.5)),
         sds((att, toks), BF16),
-        (tenant_bounds, queries, *key_blocks, *value_blocks, all_pays, seg_row),
+        (tenant_bounds, queries, kv_blocks, all_pays, seg_row),
         smem=(0,),
         scratch=[
             pltpu.VMEM((deep, toks), BF16),
             pltpu.VMEM((deep, toks), BF16),
+            pltpu.VMEM((att, toks), BF16),
             pltpu.VMEM((1, toks), F32),
             pltpu.VMEM((1, toks), F32),
             pltpu.VMEM((att, toks), F32),
         ],
         flops=4 * blocks * toks * toks * att,
     )
-    full_context, (w_o_t,) = ring_gather(
-        context, "tp", tp_count, False, ((1, 2, turned(w_o_cols, att)),)
+    (full_context,), (w_o_t,) = ring_gather(
+        [context], "tp", tp_count, ((1, 2, turned(w_o_cols, att)),)
     )
     hidden_out = call(
         functools.partial(last_kernel, len(full_context), att),

time: 235 us -> 228 us (0.970)
  blocking collectives: 24.9 us -> 5.65 us
  Pallas kernels: 21.7 us -> 25.7 us
  local copies, waits for them, and re-layouts: 12.9 us -> 16.8 us
  starting transfers between devices: 64.9 us -> 67.9 us
    all_to_all x1 -> x0, blocking collectives: 15.2 us -> none  [exchange(): return lax.all_to_all(value, 'tp', 0, 0, tiled=False)]
    all_to_all x1 -> x2, waiting for transfers between devices: 0.01 us -> 10.4 us  [exchange(): return lax.all_to_all(value, 'tp', 0, 0, tiled=False)]
    ppermute x36, waiting for transfers between devices: 59.9 us -> 55.6 us  [ring_gather(): got = (lax.ppermute(one, axis, ahead), lax.ppermute(two, axis, behind))]
    all_to_all x1 -> x2, starting transfers between devices: 4.12 us -> 8.43 us  [exchange(): return lax.all_to_all(value, 'tp', 0, 0, tiled=False)]
    all_gather x1, blocking collectives: 9.63 us -> 5.65 us  [on_device(): all_pays = lax.all_gather(pay, 'seq', axis=0, tiled=False)]
    unnamed x46 -> x48, local copies, waits for them, and re-layouts: 10.1 us -> 14.1 us
    pallas_call x10 -> x12, Pallas kernels: 20.6 us -> 24.5 us  [call(): pl.pallas_call(kernel, out_shape=out_shape, in_specs=specs, out_specs=jax...]
    ppermute x2, waiting for transfers between devices: 8.29 us -> 4.63 us  [far(): return lax.ppermute(value, 'seq', [(0, 2), (1, 3)])]
  transfers between devices with their start and end apart: 56 -> 57, of which waited for: 39 -> 41; matrix products, arithmetic and copies ran while one was open for 3% -> 2% of each run, Pallas kernels for 4% -> 8%
where the time goes in v3:
time: 228 us; the launch traced here: 224 us
  waiting for transfers between devices  91.7 us (40%)
  starting transfers between devices  67.9 us (30%)
  Pallas kernels  25.7 us (11%)
  local copies, waits for them, and re-layouts  16.8 us (7%)
  between operations  14.5 us (6%)
  blocking collectives  5.65 us (2%)
    ppermute x36, waiting for transfers between devices, ring_gather(): got = (lax.ppermute(one, axis, ahead), lax.ppermute(two, axis, behind))  55.6 us
    ppermute x36, starting transfers between devices, ring_gather(): got = (lax.ppermute(one, axis, ahead), lax.ppermute(two, axis, behind))  39.6 us
    pallas_call x12, Pallas kernels, call(): pl.pallas_call(kernel, out_shape=out_shape, in_specs=specs, out_specs=jax...  24.5 us
    unnamed x48, local copies, waits for them, and re-layouts  14.1 us
    all_to_all x2, waiting for transfers between devices, exchange(): return lax.all_to_all(value, 'tp', 0, 0, tiled=False)  10.4 us
    all_to_all x2, starting transfers between devices, exchange(): return lax.all_to_all(value, 'tp', 0, 0, tiled=False)  8.43 us
    ppermute x2, waiting for transfers between devices, ring_gather(): got = (lax.ppermute(one, axis, ahead),) * 2  5.9 us
    all_gather x1, blocking collectives, on_device(): all_pays = lax.all_gather(pay, 'seq', axis=0, tiled=False)  5.65 us
  transfers between devices with their start and end apart: 57, of which 41 were waited for; matrix products, arithmetic and copies ran while one was open for 2% of the time, Pallas kernels for 8%

profile of v3, /device:TPU:0, one launch (start us, length us, event | category | flops | bytes accessed | tf_op | source)
XLA Modules:
  0.0 224.3 jit_solution(16679199638655319045)
XLA Ops:
  8.4 3.1 %collective-permute-start = (bf16[448,256]{1,0:T(8,128)(2,1)S(1)}, bf16[448,256]{1,0:T(8,128)(2,1)S(1)}, u32[]{:S(2)}, u32[]{:S(2)}) collective-permute-start(bf16[448,256]{1,0:T(8,128)(2,1)S(1)} %get-tuple-element.90.refs_1_.refs_11__0_), channel_id=1, source_target_pairs={{0,2},{2,4},{4,6},{6,7},{7,5},{5,3},{3,1},{1,0},{8,10},{10,12},{12... | collective-permute-start | bytes 688136 | tf_op jit(solution)/shard_map/ppermute | solution.py:68
  11.5 2.0 collective-permute-start.4
  13.5 4.3 %collective-permute-done.refs_2_ = bf16[448,256]{1,0:T(8,128)(2,1)S(1)} collective-permute-done((bf16[448,256]{1,0:T(8,128)(2,1)S(1)}, bf16[448,256]{1,0:T(8,128)(2,1)S(1)}, u32[]{:S(2)}, u32[]{:S(2)}) %collective-permute-start) | collective-permute-done | bytes 229408 | tf_op jit(solution)/shard_map/ppermute | solution.py:68
  17.9 2.3 %collective-permute-done.1.refs_3_ = bf16[448,256]{1,0:T(8,128)(2,1)} collective-permute-done((bf16[448,256]{1,0:T(8,128)(2,1)S(1)}, bf16[448,256]{1,0:T(8,128)(2,1)}, u32[]{:S(2)}, u32[]{:S(2)}) %collective-permute-start.1) | collective-permute-done | bytes 229408 | tf_op jit(solution)/shard_map/ppermute | solution.py:68
  20.1 1.6 collective-permute-start.2
  22.9 2.2 collective-permute-done.5.refs_3_
  25.0 1.6 collective-permute-start.8
  27.8 1.4 copy-done.4
  31.9 1.6 collective-permute-start.6
  34.0 1.6 collective-permute-start.11
  36.0 3.2 %collective-permute-done.6.refs_6_ = bf16[448,256]{1,0:T(8,128)(2,1)} collective-permute-done((bf16[448,256]{1,0:T(8,128)(2,1)}, bf16[448,256]{1,0:T(8,128)(2,1)}, u32[]{:S(2)}, u32[]{:S(2)}) %collective-permute-start.6) | collective-permute-done | bytes 229408 | tf_op jit(solution)/shard_map/ppermute | solution.py:68
  39.3 1.4 collective-permute-done.7.refs_7_
  41.6 2.6 %collective-permute-done.12.refs_7_ = bf16[448,256]{1,0:T(8,128)(2,1)S(1)} collective-permute-done((bf16[448,256]{1,0:T(8,128)(2,1)}, bf16[448,256]{1,0:T(8,128)(2,1)S(1)}, u32[]{:S(2)}, u32[]{:S(2)}) %collective-permute-start.12) | collective-permute-done | bytes 229408 | tf_op jit(solution)/shard_map/ppermute | solution.py:68
  47.6 2.6 %collective-permute-done.13.refs_8_ = bf16[448,256]{1,0:T(8,128)(2,1)S(1)} collective-permute-done((bf16[448,256]{1,0:T(8,128)(2,1)S(1)}, bf16[448,256]{1,0:T(8,128)(2,1)S(1)}, u32[]{:S(2)}, u32[]{:S(2)}) %collective-permute-start.13) | collective-permute-done | bytes 229408 | tf_op jit(solution)/shard_map/ppermute | solution.py:74
  50.2 3.1 %shard_map.205 = (f32[320,256]{1,0:T(8,128)S(1)}, f32[192,256]{1,0:T(8,128)S(1)}, f32[8,256]{1,0:T(8,128)S(1)}, f32[8,320]{1,0:T(8,128)S(1)}) custom-call(s32[8,8]{1,0:T(8,128)S(1)} %copy-done.10, bf16[448,256]{1,0:T(8,128)(2,1)S(1)} %get-tuple-element.94.refs_1_.refs_11__1_, bf16[448,256]{1,0:T(8,128)(2,1)} %collective-permute-done.4.refs_2_, ...), custom_call_target="tpu_custom_call" | custom-call | flops 968884224 | bytes 5619968 | tf_op jit(solution)/shard_map/pallas_call | solution.py:131
  53.3 1.9 copy-done
  55.2 4.1 %all-to-all-start = ((bf16[8,48,448]{2,1,0:T(8,128)(2,1)}), bf16[8,48,448]{2,1,0:T(8,128)(2,1)S(1)}, u32[]{:S(2)}, u32[]{:S(2)}) async-start(bf16[8,48,448]{2,1,0:T(8,128)(2,1)} %get-tuple-element.135), calls=%async_computation | async-start | bytes 786432 | tf_op jit(solution)/shard_map/all_to_all | solution.py:559
  59.3 2.0 collective-permute-start.10
  62.6 4.8 %collective-permute-done.10.refs_8_ = bf16[448,256]{1,0:T(8,128)(2,1)S(1)} collective-permute-done((bf16[448,256]{1,0:T(8,128)(2,1)}, bf16[448,256]{1,0:T(8,128)(2,1)S(1)}, u32[]{:S(2)}, u32[]{:S(2)}) %collective-permute-start.10) | collective-permute-done | bytes 229408 | tf_op jit(solution)/shard_map/ppermute | solution.py:72
  67.4 2.1 copy-done.1
  69.5 3.7 %shard_map.204 = (f32[320,256]{1,0:T(8,128)S(1)}, f32[192,256]{1,0:T(8,128)S(1)}, f32[8,256]{1,0:T(8,128)S(1)}, f32[8,320]{1,0:T(8,128)}) custom-call(s32[8,8]{1,0:T(8,128)S(1)} %copy-done.10, bf16[448,256]{1,0:T(8,128)(2,1)S(1)} %get-tuple-element.90.refs_1_.refs_11__0_, bf16[448,256]{1,0:T(8,128)(2,1)S(1)} %collective-permute-done.refs_2_, ...), custom_call_target="tpu_custom_call" | custom-call | flops 968884224 | bytes 5619968 | tf_op jit(solution)/shard_map/pallas_call | solution.py:131
  73.2 3.3 %shard_map.206 = (f32[192,512]{1,0:T(8,128)S(1)}, bf16[64,512]{1,0:T(8,128)(2,1)S(1)}, f32[8,512]{1,0:T(8,128)S(1)}, bf16[208,128]{1,0:T(8,128)(2,1)S(1)}, f32[768,128]{1,0:T(8,128)S(1)}) custom-call(s32[4,2]{1,0:T(4,128)S(1)} %copy.24.bounds_ref.refs_0_, f32[3]{0:T(128)S(1)} %copy-done.16, f32[3]{0:T(128)S(1)} %copy-done.17, f32[3]{0:T(128)S(1)} %copy-done.18, ...), custom_call_target="tpu_custom_call" | custom-call | flops 1000000000 | bytes 691268 | tf_op jit(solution)/shard_map/pallas_call | solution.py:131
  77.4 5.7 %all-gather = bf16[832,128]{1,0:T(8,128)(2,1)S(1)} all-gather(bf16[208,128]{1,0:T(8,128)(2,1)S(1)} %get-tuple-element.116), channel_id=2, replica_groups=mesh['seq'=4,'tp'=8] {'seq'}, dimensions={0}, use_global_device_ids=true | all-gather | bytes 266240 | tf_op jit(solution)/shard_map/all_gather | solution.py:612
  84.1 3.3 %collective-permute-start.15 = (bf16[192,512]{1,0:T(8,128)(2,1)S(1)}, bf16[192,512]{1,0:T(8,128)(2,1)S(1)}, u32[]{:S(2)}, u32[]{:S(2)}) collective-permute-start(bf16[192,512]{1,0:T(8,128)(2,1)S(1)} %get-tuple-element.125.refs_1_), channel_id=1, source_target_pairs={{0,2},{2,4},{4,6},{6,7},{7,5},{5,3},{3,1},{1,0},{8,10},{10,12},{12... | collective-permute-start | bytes 589832 | tf_op jit(solution)/shard_map/ppermute | solution.py:68
  87.4 4.9 %collective-permute-done.15.refs_2_ = bf16[192,512]{1,0:T(8,128)(2,1)S(1)} collective-permute-done((bf16[192,512]{1,0:T(8,128)(2,1)S(1)}, bf16[192,512]{1,0:T(8,128)(2,1)S(1)}, u32[]{:S(2)}, u32[]{:S(2)}) %collective-permute-start.15) | collective-permute-done | bytes 196640 | tf_op jit(solution)/shard_map/ppermute | solution.py:68
  92.3 2.6 %collective-permute-done.16.refs_3_ = bf16[192,512]{1,0:T(8,128)(2,1)S(1)} collective-permute-done((bf16[192,512]{1,0:T(8,128)(2,1)S(1)}, bf16[192,512]{1,0:T(8,128)(2,1)S(1)}, u32[]{:S(2)}, u32[]{:S(2)}) %collective-permute-start.16) | collective-permute-done | bytes 196640 | tf_op jit(solution)/shard_map/ppermute | solution.py:68
  94.9 1.7 collective-permute-start.17
  96.9 4.4 %collective-permute-done.17.refs_4_ = bf16[192,512]{1,0:T(8,128)(2,1)S(1)} collective-permute-done((bf16[192,512]{1,0:T(8,128)(2,1)S(1)}, bf16[192,512]{1,0:T(8,128)(2,1)S(1)}, u32[]{:S(2)}, u32[]{:S(2)}) %collective-permute-start.17) | collective-permute-done | bytes 196640 | tf_op jit(solution)/shard_map/ppermute | solution.py:68
  103.1 1.4 collective-permute-start.20
  104.6 1.6 collective-permute-start.22
  106.1 4.2 %collective-permute-done.22 = bf16[768,64]{1,0:T(8,128)(2,1)S(1)} collective-permute-done((bf16[768,64]{1,0:T(8,128)(2,1)S(1)}, bf16[768,64]{1,0:T(8,128)(2,1)S(1)}, u32[]{:S(2)}, u32[]{:S(2)}) %collective-permute-start.22) | collective-permute-done | bytes 98336 | tf_op jit(solution)/shard_map/ppermute | solution.py:95
  111.1 1.4 collective-permute-start.24
  112.5 1.4 copy-done.5
  115.8 1.8 shard_map.209
  117.6 1.4 collective-permute-start.25
  119.7 1.4 collective-permute-start.29
  121.7 3.6 %collective-permute-done.25.piece_refs_1_ = bf16[448,256]{1,0:T(8,128)(2,1)S(1)} collective-permute-done((bf16[448,256]{1,0:T(8,128)(2,1)S(1)}, bf16[448,256]{1,0:T(8,128)(2,1)S(1)}, u32[]{:S(2)}, u32[]{:S(2)}) %collective-permute-start.25) | collective-permute-done | bytes 229408 | tf_op jit(solution)/shard_map/ppermute | solution.py:68
  125.3 1.6 collective-permute-done.26.piece_refs_2_
  126.9 2.3 %collective-permute-start.27 = (bf16[448,256]{1,0:T(8,128)(2,1)S(1)}, bf16[448,256]{1,0:T(8,128)(2,1)S(1)}, u32[]{:S(2)}, u32[]{:S(2)}) collective-permute-start(bf16[448,256]{1,0:T(8,128)(2,1)S(1)} %collective-permute-done.25.piece_refs_1_), channel_id=1, source_target_pairs={{0,2},{2,4},{4,6},{6,7},{7,5},{5,3},{3,1},{1,0},{8,10},{10,12},{12... | collective-permute-start | bytes 688136 | tf_op jit(solution)/shard_map/ppermute | solution.py:68
  130.2 1.6 collective-permute-done.30.piece_refs_2_
  131.8 2.3 %collective-permute-start.33 = (bf16[448,256]{1,0:T(8,128)(2,1)S(1)}, bf16[448,256]{1,0:T(8,128)(2,1)S(1)}, u32[]{:S(2)}, u32[]{:S(2)}) collective-permute-start(bf16[448,256]{1,0:T(8,128)(2,1)S(1)} %collective-permute-done.29.piece_refs_1_), channel_id=1, source_target_pairs={{0,2},{2,4},{4,6},{6,7},{7,5},{5,3},{3,1},{1,0},{8,10},{10,12},{12... | collective-permute-start | bytes 688136 | tf_op jit(solution)/shard_map/ppermute | solution.py:68
  135.4 2.3 %collective-permute-done.28.piece_refs_4_ = bf16[448,256]{1,0:T(8,128)(2,1)S(1)} collective-permute-done((bf16[448,256]{1,0:T(8,128)(2,1)S(1)}, bf16[448,256]{1,0:T(8,128)(2,1)S(1)}, u32[]{:S(2)}, u32[]{:S(2)}) %collective-permute-start.28) | collective-permute-done | bytes 229408 | tf_op jit(solution)/shard_map/ppermute | solution.py:68
  137.7 1.4 collective-permute-start.31
  140.3 1.9 collective-permute-done.34.piece_refs_4_
  142.2 1.7 collective-permute-start.36
  145.8 1.4 collective-permute-start.35
  148.3 1.8 collective-permute-done.37.piece_refs_6_
  151.8 2.6 %shard_map.210 = (bf16[224,256]{1,0:T(8,128)(2,1)S(1)}, bf16[448,256]{1,0:T(8,128)(2,1)S(1)}) custom-call(s32[8,8]{1,0:T(8,128)S(1)} %copy-done.10, bf16[448,256]{1,0:T(8,128)(2,1)S(1)} %get-tuple-element.141.piece_refs_0_.refs_11__0_, bf16[448,256]{1,0:T(8,128)(2,1)S(1)} %collective-permute-done.25.piece_refs_1_, ...), custom_call_target="tpu_custom_call" | custom-call | flops 1233125376 | bytes 6652160 | tf_op jit(solution)/shard_map/pallas_call | solution.py:131
  156.1 3.4 %shard_map.211 = (bf16[224,256]{1,0:T(8,128)(2,1)S(1)}, bf16[448,256]{1,0:T(8,128)(2,1)S(1)}, bf16[448,512]{1,0:T(8,128)(2,1)}) custom-call(s32[8,8]{1,0:T(8,128)S(1)} %copy-done.10, bf16[448,256]{1,0:T(8,128)(2,1)S(1)} %get-tuple-element.145.piece_refs_0_.refs_11__1_, bf16[448,256]{1,0:T(8,128)(2,1)S(1)} %collective-permute-done.29.piece_refs_1_, ...), custom_call_target="tpu_custom_call" | custom-call | flops 1233125376 | bytes 6881536 | tf_op jit(solution)/shard_map/pallas_call | solution.py:131
  160.8 3.4 %collective-permute-start.41 = (bf16[448,256]{1,0:T(8,128)(2,1)S(1)}, bf16[448,256]{1,0:T(8,128)(2,1)S(1)}, u32[]{:S(2)}, u32[]{:S(2)}) collective-permute-start(bf16[448,256]{1,0:T(8,128)(2,1)S(1)} %get-tuple-element.157.first_refs_0_.refs_2__0__0_), channel_id=1, source_target_pairs={{0,16},{8,24},{1,17},{9,25},{2,18},{10,26},{3,19},{11,27},{4,20},{... | collective-permute-start | bytes 688136 | tf_op jit(solution)/shard_map/ppermute | solution.py:681
  165.5 2.2 collective-permute-done.41.refs_2__2__0_
  167.7 2.5 %collective-permute-done.42.refs_2__2__1_ = bf16[448,256]{1,0:T(8,128)(2,1)S(1)} collective-permute-done((bf16[448,256]{1,0:T(8,128)(2,1)S(1)}, bf16[448,256]{1,0:T(8,128)(2,1)S(1)}, u32[]{:S(2)}, u32[]{:S(2)}) %collective-permute-start.42) | collective-permute-done | bytes 229408 | tf_op jit(solution)/shard_map/ppermute | solution.py:681
  170.2 4.4 %all-to-all-start.1 = ((bf16[8,56,448]{2,1,0:T(8,128)(2,1)}), bf16[8,56,448]{2,1,0:T(8,128)(2,1)}, u32[]{:S(2)}, u32[]{:S(2)}) async-start(bf16[8,56,448]{2,1,0:T(8,128)(2,1)} %get-tuple-element.167), calls=%async_computation.1 | async-start | bytes 917504 | tf_op jit(solution)/shard_map/all_to_all | solution.py:559
  176.0 10.4 %all-to-all-done.1 = bf16[8,56,448]{2,1,0:T(8,128)(2,1)} async-done(((bf16[8,56,448]{2,1,0:T(8,128)(2,1)}), bf16[8,56,448]{2,1,0:T(8,128)(2,1)}, u32[]{:S(2)}, u32[]{:S(2)}) %all-to-all-start.1) | async-done | bytes 401440 | tf_op jit(solution)/shard_map/all_to_all | solution.py:559
  186.4 1.5 shard_map.212.refs_1_
  188.0 2.0 collective-permute-start.46
  190.0 4.0 %collective-permute-done.45.refs_2_ = bf16[224,512]{1,0:T(8,128)(2,1)S(1)} collective-permute-done((bf16[224,512]{1,0:T(8,128)(2,1)S(1)}, bf16[224,512]{1,0:T(8,128)(2,1)S(1)}, u32[]{:S(2)}, u32[]{:S(2)}) %collective-permute-start.45) | collective-permute-done | bytes 229408 | tf_op jit(solution)/shard_map/ppermute | solution.py:68
  194.5 1.7 collective-permute-start.48
  196.2 4.0 %collective-permute-done.47.refs_4_ = bf16[224,512]{1,0:T(8,128)(2,1)S(1)} collective-permute-done((bf16[224,512]{1,0:T(8,128)(2,1)S(1)}, bf16[224,512]{1,0:T(8,128)(2,1)S(1)}, u32[]{:S(2)}, u32[]{:S(2)}) %collective-permute-start.47) | collective-permute-done | bytes 229408 | tf_op jit(solution)/shard_map/ppermute | solution.py:68
  202.5 3.1 %all-gather.6.cloned.1.call-done = bf16[8,224,448]{2,1,0:T(8,128)(2,1)} async-done(((bf16[8,56,448]{2,1,0:T(8,128)(2,1)}), bf16[8,224,448]{2,1,0:T(8,128)(2,1)}) %all-gather.6.cloned.1.call-update) | async-done | bytes 1605648 | tf_op jit(solution)/shard_map/all_gather | solution.py:563
  205.6 1.5 copy-done.3
  207.7 1.6 collective-permute-start.51
  210.6 2.4 %collective-permute-done.51.refs_8_ = bf16[112,512]{1,0:T(8,128)(2,1)S(1)} collective-permute-done((bf16[112,512]{1,0:T(8,128)(2,1)S(1)}, bf16[112,512]{1,0:T(8,128)(2,1)S(1)}, u32[]{:S(2)}, u32[]{:S(2)}) %collective-permute-start.51) | collective-permute-done | bytes 114720 | tf_op jit(solution)/shard_map/ppermute | solution.py:70
  214.3 2.2 shard_map.214
  (125 shorter events, 41.6 us)
Async XLA Ops:
  7.2 37.7 %copy-start.2 = (bf16[2,192,3584]{2,1,0:T(8,128)(2,1)S(1)}, bf16[2,192,3584]{2,1,0:T(8,128)(2,1)}, u32[]{:S(2)}) copy-start(bf16[2,192,3584]{2,1,0:T(8,128)(2,1)} %xz_ref) | copy-start | bytes 8257540
  8.4 9.5 %collective-permute-start = (bf16[448,256]{1,0:T(8,128)(2,1)S(1)}, bf16[448,256]{1,0:T(8,128)(2,1)S(1)}, u32[]{:S(2)}, u32[]{:S(2)}) collective-permute-start(bf16[448,256]{1,0:T(8,128)(2,1)S(1)} %get-tuple-element.90.refs_1_.refs_11__0_), channel_id=1, source_target_pairs={{0,2},{2,4},{4,6},{6,7},{7,5},{5,3},{3,1},{1,0},{8,10},{10,12},{12... | collective-permute-start | bytes 688136 | tf_op jit(solution)/shard_map/ppermute | solution.py:68
  11.5 8.6 %collective-permute-start.1 = (bf16[448,256]{1,0:T(8,128)(2,1)S(1)}, bf16[448,256]{1,0:T(8,128)(2,1)}, u32[]{:S(2)}, u32[]{:S(2)}) collective-permute-start(bf16[448,256]{1,0:T(8,128)(2,1)S(1)} %get-tuple-element.90.refs_1_.refs_11__0_), channel_id=1, source_target_pairs={{0,1},{2,0},{4,2},{6,4},{7,6},{5,7},{3,5},{1,3},{8,9},{10,8},{12,1... | collective-permute-start | bytes 688136 | tf_op jit(solution)/shard_map/ppermute | solution.py:68
  11.5 11.4 %collective-permute-start.4 = (bf16[448,256]{1,0:T(8,128)(2,1)S(1)}, bf16[448,256]{1,0:T(8,128)(2,1)}, u32[]{:S(2)}, u32[]{:S(2)}) collective-permute-start(bf16[448,256]{1,0:T(8,128)(2,1)S(1)} %get-tuple-element.94.refs_1_.refs_11__1_), channel_id=1, source_target_pairs={{0,2},{2,4},{4,6},{6,7},{7,5},{5,3},{3,1},{1,0},{8,10},{10,12},{12... | collective-permute-start | bytes 688136 | tf_op jit(solution)/shard_map/ppermute | solution.py:68
  13.5 11.5 %collective-permute-start.5 = (bf16[448,256]{1,0:T(8,128)(2,1)S(1)}, bf16[448,256]{1,0:T(8,128)(2,1)}, u32[]{:S(2)}, u32[]{:S(2)}) collective-permute-start(bf16[448,256]{1,0:T(8,128)(2,1)S(1)} %get-tuple-element.94.refs_1_.refs_11__1_), channel_id=1, source_target_pairs={{0,1},{2,0},{4,2},{6,4},{7,6},{5,7},{3,5},{1,3},{8,9},{10,8},{12,1... | collective-permute-start | bytes 688136 | tf_op jit(solution)/shard_map/ppermute | solution.py:68
  20.1 11.7 %collective-permute-start.2 = (bf16[448,256]{1,0:T(8,128)(2,1)S(1)}, bf16[448,256]{1,0:T(8,128)(2,1)}, u32[]{:S(2)}, u32[]{:S(2)}) collective-permute-start(bf16[448,256]{1,0:T(8,128)(2,1)S(1)} %collective-permute-done.refs_2_), channel_id=1, source_target_pairs={{0,2},{2,4},{4,6},{6,7},{7,5},{5,3},{3,1},{1,0},{8,10},{10,12},{12... | collective-permute-start | bytes 688136 | tf_op jit(solution)/shard_map/ppermute | solution.py:68
  21.7 10.2 %collective-permute-start.3 = (bf16[448,256]{1,0:T(8,128)(2,1)}, bf16[448,256]{1,0:T(8,128)(2,1)}, u32[]{:S(2)}, u32[]{:S(2)}) collective-permute-start(bf16[448,256]{1,0:T(8,128)(2,1)} %collective-permute-done.1.refs_3_), channel_id=1, source_target_pairs={{0,1},{2,0},{4,2},{6,4},{7,6},{5,7},{3,5},{1,3},{8,9},{10,8},{12,1... | collective-permute-start | bytes 688136 | tf_op jit(solution)/shard_map/ppermute | solution.py:68
  25.0 8.9 %collective-permute-start.8 = (bf16[448,256]{1,0:T(8,128)(2,1)}, bf16[448,256]{1,0:T(8,128)(2,1)}, u32[]{:S(2)}, u32[]{:S(2)}) collective-permute-start(bf16[448,256]{1,0:T(8,128)(2,1)} %collective-permute-done.4.refs_2_), channel_id=1, source_target_pairs={{0,2},{2,4},{4,6},{6,7},{7,5},{5,3},{3,1},{1,0},{8,10},{10,12},{12... | collective-permute-start | bytes 688136 | tf_op jit(solution)/shard_map/ppermute | solution.py:68
  26.6 7.4 %collective-permute-start.9 = (bf16[448,256]{1,0:T(8,128)(2,1)}, bf16[448,256]{1,0:T(8,128)(2,1)}, u32[]{:S(2)}, u32[]{:S(2)}) collective-permute-start(bf16[448,256]{1,0:T(8,128)(2,1)} %collective-permute-done.5.refs_3_), channel_id=1, source_target_pairs={{0,1},{2,0},{4,2},{6,4},{7,6},{5,7},{3,5},{1,3},{8,9},{10,8},{12,1... | collective-permute-start | bytes 688136 | tf_op jit(solution)/shard_map/ppermute | solution.py:68
  31.8 18.3 %copy-start.10 = (s32[8,8]{1,0:T(8,128)S(1)}, s32[8,8]{1,0:T(8,128)}, u32[]{:S(2)}) copy-start(s32[8,8]{1,0:T(8,128)} %constant.7.clone.refs_0_.slots_ref) | copy-start | bytes 772
  31.9 7.4 %collective-permute-start.6 = (bf16[448,256]{1,0:T(8,128)(2,1)}, bf16[448,256]{1,0:T(8,128)(2,1)}, u32[]{:S(2)}, u32[]{:S(2)}) collective-permute-start(bf16[448,256]{1,0:T(8,128)(2,1)} %collective-permute-done.2.refs_4_), channel_id=1, source_target_pairs={{0,2},{2,4},{4,6},{6,7},{7,5},{5,3},{3,1},{1,0},{8,10},{10,12},{12... | collective-permute-start | bytes 688136 | tf_op jit(solution)/shard_map/ppermute | solution.py:68
  33.5 7.2 %collective-permute-start.7 = (bf16[448,256]{1,0:T(8,128)(2,1)}, bf16[448,256]{1,0:T(8,128)(2,1)S(1)}, u32[]{:S(2)}, u32[]{:S(2)}) collective-permute-start(bf16[448,256]{1,0:T(8,128)(2,1)} %collective-permute-done.3.refs_5_), channel_id=1, source_target_pairs={{0,1},{2,0},{4,2},{6,4},{7,6},{5,7},{3,5},{1,3},{8,9},{10,8},{12,1... | collective-permute-start | bytes 688136 | tf_op jit(solution)/shard_map/ppermute | solution.py:68
  34.0 7.6 %collective-permute-start.11 = (bf16[448,256]{1,0:T(8,128)(2,1)}, bf16[448,256]{1,0:T(8,128)(2,1)S(1)}, u32[]{:S(2)}, u32[]{:S(2)}) collective-permute-start(bf16[448,256]{1,0:T(8,128)(2,1)} %collective-permute-done.8.refs_4_), channel_id=1, source_target_pairs={{0,2},{2,4},{4,6},{6,7},{7,5},{5,3},{3,1},{1,0},{8,10},{10,12},{12... | collective-permute-start | bytes 688136 | tf_op jit(solution)/shard_map/ppermute | solution.py:68
  35.6 8.6 %collective-permute-start.12 = (bf16[448,256]{1,0:T(8,128)(2,1)}, bf16[448,256]{1,0:T(8,128)(2,1)S(1)}, u32[]{:S(2)}, u32[]{:S(2)}) collective-permute-start(bf16[448,256]{1,0:T(8,128)(2,1)} %collective-permute-done.9.refs_5_), channel_id=1, source_target_pairs={{0,1},{2,0},{4,2},{6,4},{7,6},{5,7},{3,5},{1,3},{8,9},{10,8},{12,1... | collective-permute-start | bytes 688136 | tf_op jit(solution)/shard_map/ppermute | solution.py:68
  44.2 6.0 %collective-permute-start.13 = (bf16[448,256]{1,0:T(8,128)(2,1)S(1)}, bf16[448,256]{1,0:T(8,128)(2,1)S(1)}, u32[]{:S(2)}, u32[]{:S(2)}) collective-permute-start(bf16[448,256]{1,0:T(8,128)(2,1)S(1)} %collective-permute-done.12.refs_7_), channel_id=1, source_target_pairs={{0,1},{2,0},{4,2},{6,4},{7,6},{5,7},{3,5},{1,3},{8,9},{10,8},{12,1... | collective-permute-start | bytes 688136 | tf_op jit(solution)/shard_map/ppermute | solution.py:74
  47.6 19.8 %copy-start.9 = (bf16[448,256]{1,0:T(8,128)(2,1)S(1)}, bf16[448,256]{1,0:T(8,128)(2,1)}, u32[]{:S(2)}) copy-start(bf16[448,256]{1,0:T(8,128)(2,1)} %copy-done.8) | copy-start | bytes 688132
  55.1 18.1 %copy-start.16 = (f32[3]{0:T(128)S(1)}, f32[3]{0:T(128)}, u32[]{:S(2)}) copy-start(f32[3]{0:T(128)} %bias_ref.1) | copy-start | bytes 40
  55.2 18.1 %copy-start.17 = (f32[3]{0:T(128)S(1)}, f32[3]{0:T(128)}, u32[]{:S(2)}) copy-start(f32[3]{0:T(128)} %rate_ref.1) | copy-start | bytes 40
  55.2 21.4 %all-to-all-start = ((bf16[8,48,448]{2,1,0:T(8,128)(2,1)}), bf16[8,48,448]{2,1,0:T(8,128)(2,1)S(1)}, u32[]{:S(2)}, u32[]{:S(2)}) async-start(bf16[8,48,448]{2,1,0:T(8,128)(2,1)} %get-tuple-element.135), calls=%async_computation | async-start | bytes 786432 | tf_op jit(solution)/shard_map/all_to_all | solution.py:559
  59.2 53.3 %all-gather.4.cloned.1.call-start = ((), (), s32[]{:S(2)}) async-start(), calls=%async_computation.2 | async-start | bytes 1966080 | tf_op jit(solution)/shard_map/all_gather | solution.py:563
  59.3 8.1 %collective-permute-start.10 = (bf16[448,256]{1,0:T(8,128)(2,1)}, bf16[448,256]{1,0:T(8,128)(2,1)S(1)}, u32[]{:S(2)}, u32[]{:S(2)}) collective-permute-start(bf16[448,256]{1,0:T(8,128)(2,1)} %collective-permute-done.6.refs_6_), channel_id=1, source_target_pairs={{0,2},{2,4},{4,6},{6,7},{7,5},{5,3},{3,1},{1,0},{8,10},{10,12},{12... | collective-permute-start | bytes 688136 | tf_op jit(solution)/shard_map/ppermute | solution.py:72
  61.4 11.8 %collective-permute-start.14 = (f32[8,320]{1,0:T(8,128)S(1)}, f32[8,320]{1,0:T(8,128)S(1)}, u32[]{:S(2)}, u32[]{:S(2)}) collective-permute-start(f32[8,320]{1,0:T(8,128)S(1)} %get-tuple-element.115), channel_id=1, source_target_pairs={{0,8},{8,16},{16,24},{1,9},{9,17},{17,25},{2,10},{10,18},{18,26},{... | collective-permute-start | bytes 30728 | tf_op jit(solution)/shard_map/ppermute | solution.py:591
  84.1 8.2 %collective-permute-start.15 = (bf16[192,512]{1,0:T(8,128)(2,1)S(1)}, bf16[192,512]{1,0:T(8,128)(2,1)S(1)}, u32[]{:S(2)}, u32[]{:S(2)}) collective-permute-start(bf16[192,512]{1,0:T(8,128)(2,1)S(1)} %get-tuple-element.125.refs_1_), channel_id=1, source_target_pairs={{0,2},{2,4},{4,6},{6,7},{7,5},{5,3},{3,1},{1,0},{8,10},{10,12},{12... | collective-permute-start | bytes 589832 | tf_op jit(solution)/shard_map/ppermute | solution.py:68
  87.4 7.5 %collective-permute-start.16 = (bf16[192,512]{1,0:T(8,128)(2,1)S(1)}, bf16[192,512]{1,0:T(8,128)(2,1)S(1)}, u32[]{:S(2)}, u32[]{:S(2)}) collective-permute-start(bf16[192,512]{1,0:T(8,128)(2,1)S(1)} %get-tuple-element.125.refs_1_), channel_id=1, source_target_pairs={{0,1},{2,0},{4,2},{6,4},{7,6},{5,7},{3,5},{1,3},{8,9},{10,8},{12,1... | collective-permute-start | bytes 589832 | tf_op jit(solution)/shard_map/ppermute | solution.py:68
  94.9 6.5 %collective-permute-start.17 = (bf16[192,512]{1,0:T(8,128)(2,1)S(1)}, bf16[192,512]{1,0:T(8,128)(2,1)S(1)}, u32[]{:S(2)}, u32[]{:S(2)}) collective-permute-start(bf16[192,512]{1,0:T(8,128)(2,1)S(1)} %collective-permute-done.15.refs_2_), channel_id=1, source_target_pairs={{0,2},{2,4},{4,6},{6,7},{7,5},{5,3},{3,1},{1,0},{8,10},{10,12},{12... | collective-permute-start | bytes 589832 | tf_op jit(solution)/shard_map/ppermute | solution.py:68
  96.6 5.9 %collective-permute-start.18 = (bf16[192,512]{1,0:T(8,128)(2,1)S(1)}, bf16[192,512]{1,0:T(8,128)(2,1)S(1)}, u32[]{:S(2)}, u32[]{:S(2)}) collective-permute-start(bf16[192,512]{1,0:T(8,128)(2,1)S(1)} %collective-permute-done.16.refs_3_), channel_id=1, source_target_pairs={{0,1},{2,0},{4,2},{6,4},{7,6},{5,7},{3,5},{1,3},{8,9},{10,8},{12,1... | collective-permute-start | bytes 589832 | tf_op jit(solution)/shard_map/ppermute | solution.py:68
  96.9 7.6 %collective-permute-start.21 = (bf16[768,64]{1,0:T(8,128)(2,1)S(1)}, bf16[768,64]{1,0:T(8,128)(2,1)S(1)}, u32[]{:S(2)}, u32[]{:S(2)}) collective-permute-start(bf16[768,64]{1,0:T(8,128)(2,1)S(1)} %get-tuple-element.131), channel_id=1, source_target_pairs={{0,8},{8,0},{16,24},{24,16},{1,9},{9,1},{17,25},{25,17},{2,10},{10... | collective-permute-start | bytes 294920 | tf_op jit(solution)/shard_map/ppermute | solution.py:95
  102.5 7.9 %collective-permute-start.19 = (bf16[192,512]{1,0:T(8,128)(2,1)S(1)}, bf16[192,512]{1,0:T(8,128)(2,1)S(1)}, u32[]{:S(2)}, u32[]{:S(2)}) collective-permute-start(bf16[192,512]{1,0:T(8,128)(2,1)S(1)} %collective-permute-done.17.refs_4_), channel_id=1, source_target_pairs={{0,2},{2,4},{4,6},{6,7},{7,5},{5,3},{3,1},{1,0},{8,10},{10,12},{12... | collective-permute-start | bytes 589832 | tf_op jit(solution)/shard_map/ppermute | solution.py:68
  103.1 7.2 %collective-permute-start.20 = (bf16[192,512]{1,0:T(8,128)(2,1)S(1)}, bf16[192,512]{1,0:T(8,128)(2,1)S(1)}, u32[]{:S(2)}, u32[]{:S(2)}) collective-permute-start(bf16[192,512]{1,0:T(8,128)(2,1)S(1)} %collective-permute-done.18.refs_5_), channel_id=1, source_target_pairs={{0,1},{2,0},{4,2},{6,4},{7,6},{5,7},{3,5},{1,3},{8,9},{10,8},{12,1... | collective-permute-start | bytes 589832 | tf_op jit(solution)/shard_map/ppermute | solution.py:68
  104.6 39.7 %copy-start.21 = (f32[3584]{0:T(1024)S(1)}, f32[3584]{0:T(1024)}, u32[]{:S(2)}) copy-start(f32[3584]{0:T(1024)} %param.31) | copy-start | bytes 43012
  104.6 5.7 %collective-permute-start.22 = (bf16[768,64]{1,0:T(8,128)(2,1)S(1)}, bf16[768,64]{1,0:T(8,128)(2,1)S(1)}, u32[]{:S(2)}, u32[]{:S(2)}) collective-permute-start(bf16[768,64]{1,0:T(8,128)(2,1)S(1)} %add.6), channel_id=1, source_target_pairs={{0,16},{8,24},{16,0},{24,8},{1,17},{9,25},{17,1},{25,9},{2,18},{10... | collective-permute-start | bytes 294920 | tf_op jit(solution)/shard_map/ppermute | solution.py:95
  110.4 4.7 %collective-permute-start.23 = (bf16[96,512]{1,0:T(8,128)(2,1)S(1)}, bf16[96,512]{1,0:T(8,128)(2,1)S(1)}, u32[]{:S(2)}, u32[]{:S(2)}) collective-permute-start(bf16[96,512]{1,0:T(8,128)(2,1)S(1)} %slice.20), channel_id=1, source_target_pairs={{0,2},{2,4},{4,6},{6,7},{7,5},{5,3},{3,1},{1,0},{8,10},{10,12},{12... | collective-permute-start | bytes 294920 | tf_op jit(solution)/shard_map/ppermute | solution.py:70
  111.1 4.7 %collective-permute-start.24 = (bf16[96,512]{1,0:T(8,128)(2,1)S(1)}, bf16[96,512]{1,0:T(8,128)(2,1)S(1)}, u32[]{:S(2)}, u32[]{:S(2)}) collective-permute-start(bf16[96,512]{1,0:T(8,128)(2,1)S(1)} %slice.21), channel_id=1, source_target_pairs={{0,1},{2,0},{4,2},{6,4},{7,6},{5,7},{3,5},{1,3},{8,9},{10,8},{12,1... | collective-permute-start | bytes 294920 | tf_op jit(solution)/shard_map/ppermute | solution.py:70
  114.0 30.3 %copy-start.19 = (bf16[3,224,3584]{2,1,0:T(8,128)(2,1)S(1)}, bf16[3,224,3584]{2,1,0:T(8,128)(2,1)}, u32[]{:S(2)}) copy-start(bf16[3,224,3584]{2,1,0:T(8,128)(2,1)} %param.32) | copy-start | bytes 14450692
  117.6 7.7 %collective-permute-start.25 = (bf16[448,256]{1,0:T(8,128)(2,1)S(1)}, bf16[448,256]{1,0:T(8,128)(2,1)S(1)}, u32[]{:S(2)}, u32[]{:S(2)}) collective-permute-start(bf16[448,256]{1,0:T(8,128)(2,1)S(1)} %get-tuple-element.141.piece_refs_0_.refs_11__0_), channel_id=1, source_target_pairs={{0,2},{2,4},{4,6},{6,7},{7,5},{5,3},{3,1},{1,0},{8,10},{10,12},{12... | collective-permute-start | bytes 688136 | tf_op jit(solution)/shard_map/ppermute | solution.py:68
  119.0 7.8 %collective-permute-start.26 = (bf16[448,256]{1,0:T(8,128)(2,1)S(1)}, bf16[448,256]{1,0:T(8,128)(2,1)S(1)}, u32[]{:S(2)}, u32[]{:S(2)}) collective-permute-start(bf16[448,256]{1,0:T(8,128)(2,1)S(1)} %get-tuple-element.141.piece_refs_0_.refs_11__0_), channel_id=1, source_target_pairs={{0,1},{2,0},{4,2},{6,4},{7,6},{5,7},{3,5},{1,3},{8,9},{10,8},{12,1... | collective-permute-start | bytes 688136 | tf_op jit(solution)/shard_map/ppermute | solution.py:68
  119.7 10.5 %collective-permute-start.29 = (bf16[448,256]{1,0:T(8,128)(2,1)S(1)}, bf16[448,256]{1,0:T(8,128)(2,1)S(1)}, u32[]{:S(2)}, u32[]{:S(2)}) collective-permute-start(bf16[448,256]{1,0:T(8,128)(2,1)S(1)} %get-tuple-element.145.piece_refs_0_.refs_11__1_), channel_id=1, source_target_pairs={{0,2},{2,4},{4,6},{6,7},{7,5},{5,3},{3,1},{1,0},{8,10},{10,12},{12... | collective-permute-start | bytes 688136 | tf_op jit(solution)/shard_map/ppermute | solution.py:68
  121.0 10.7 %collective-permute-start.30 = (bf16[448,256]{1,0:T(8,128)(2,1)S(1)}, bf16[448,256]{1,0:T(8,128)(2,1)S(1)}, u32[]{:S(2)}, u32[]{:S(2)}) collective-permute-start(bf16[448,256]{1,0:T(8,128)(2,1)S(1)} %get-tuple-element.145.piece_refs_0_.refs_11__1_), channel_id=1, source_target_pairs={{0,1},{2,0},{4,2},{6,4},{7,6},{5,7},{3,5},{1,3},{8,9},{10,8},{12,1... | collective-permute-start | bytes 688136 | tf_op jit(solution)/shard_map/ppermute | solution.py:68
  126.9 8.5 %collective-permute-start.27 = (bf16[448,256]{1,0:T(8,128)(2,1)S(1)}, bf16[448,256]{1,0:T(8,128)(2,1)S(1)}, u32[]{:S(2)}, u32[]{:S(2)}) collective-permute-start(bf16[448,256]{1,0:T(8,128)(2,1)S(1)} %collective-permute-done.25.piece_refs_1_), channel_id=1, source_target_pairs={{0,2},{2,4},{4,6},{6,7},{7,5},{5,3},{3,1},{1,0},{8,10},{10,12},{12... | collective-permute-start | bytes 688136 | tf_op jit(solution)/shard_map/ppermute | solution.py:68
  129.2 8.5 %collective-permute-start.28 = (bf16[448,256]{1,0:T(8,128)(2,1)S(1)}, bf16[448,256]{1,0:T(8,128)(2,1)S(1)}, u32[]{:S(2)}, u32[]{:S(2)}) collective-permute-start(bf16[448,256]{1,0:T(8,128)(2,1)S(1)} %collective-permute-done.26.piece_refs_2_), channel_id=1, source_target_pairs={{0,1},{2,0},{4,2},{6,4},{7,6},{5,7},{3,5},{1,3},{8,9},{10,8},{12,1... | collective-permute-start | bytes 688136 | tf_op jit(solution)/shard_map/ppermute | solution.py:68
  131.8 8.5 %collective-permute-start.33 = (bf16[448,256]{1,0:T(8,128)(2,1)S(1)}, bf16[448,256]{1,0:T(8,128)(2,1)S(1)}, u32[]{:S(2)}, u32[]{:S(2)}) collective-permute-start(bf16[448,256]{1,0:T(8,128)(2,1)S(1)} %collective-permute-done.29.piece_refs_1_), channel_id=1, source_target_pairs={{0,2},{2,4},{4,6},{6,7},{7,5},{5,3},{3,1},{1,0},{8,10},{10,12},{12... | collective-permute-start | bytes 688136 | tf_op jit(solution)/shard_map/ppermute | solution.py:68
  134.1 8.1 %collective-permute-start.34 = (bf16[448,256]{1,0:T(8,128)(2,1)S(1)}, bf16[448,256]{1,0:T(8,128)(2,1)S(1)}, u32[]{:S(2)}, u32[]{:S(2)}) collective-permute-start(bf16[448,256]{1,0:T(8,128)(2,1)S(1)} %collective-permute-done.30.piece_refs_2_), channel_id=1, source_target_pairs={{0,1},{2,0},{4,2},{6,4},{7,6},{5,7},{3,5},{1,3},{8,9},{10,8},{12,1... | collective-permute-start | bytes 688136 | tf_op jit(solution)/shard_map/ppermute | solution.py:68
  137.7 8.1 %collective-permute-start.31 = (bf16[448,256]{1,0:T(8,128)(2,1)S(1)}, bf16[448,256]{1,0:T(8,128)(2,1)S(1)}, u32[]{:S(2)}, u32[]{:S(2)}) collective-permute-start(bf16[448,256]{1,0:T(8,128)(2,1)S(1)} %collective-permute-done.27.piece_refs_3_), channel_id=1, source_target_pairs={{0,2},{2,4},{4,6},{6,7},{7,5},{5,3},{3,1},{1,0},{8,10},{10,12},{12... | collective-permute-start | bytes 688136 | tf_op jit(solution)/shard_map/ppermute | solution.py:68
  139.1 6.7 %collective-permute-start.32 = (bf16[448,256]{1,0:T(8,128)(2,1)S(1)}, bf16[448,256]{1,0:T(8,128)(2,1)S(1)}, u32[]{:S(2)}, u32[]{:S(2)}) collective-permute-start(bf16[448,256]{1,0:T(8,128)(2,1)S(1)} %collective-permute-done.28.piece_refs_4_), channel_id=1, source_target_pairs={{0,1},{2,0},{4,2},{6,4},{7,6},{5,7},{3,5},{1,3},{8,9},{10,8},{12,1... | collective-permute-start | bytes 688136 | tf_op jit(solution)/shard_map/ppermute | solution.py:68
  142.2 6.0 %collective-permute-start.36 = (bf16[448,256]{1,0:T(8,128)(2,1)S(1)}, bf16[448,256]{1,0:T(8,128)(2,1)S(1)}, u32[]{:S(2)}, u32[]{:S(2)}) collective-permute-start(bf16[448,256]{1,0:T(8,128)(2,1)S(1)} %collective-permute-done.33.piece_refs_3_), channel_id=1, source_target_pairs={{0,2},{2,4},{4,6},{6,7},{7,5},{5,3},{3,1},{1,0},{8,10},{10,12},{12... | collective-permute-start | bytes 688136 | tf_op jit(solution)/shard_map/ppermute | solution.py:68
  144.0 6.1 %collective-permute-start.37 = (bf16[448,256]{1,0:T(8,128)(2,1)S(1)}, bf16[448,256]{1,0:T(8,128)(2,1)S(1)}, u32[]{:S(2)}, u32[]{:S(2)}) collective-permute-start(bf16[448,256]{1,0:T(8,128)(2,1)S(1)} %collective-permute-done.34.piece_refs_4_), channel_id=1, source_target_pairs={{0,1},{2,0},{4,2},{6,4},{7,6},{5,7},{3,5},{1,3},{8,9},{10,8},{12,1... | collective-permute-start | bytes 688136 | tf_op jit(solution)/shard_map/ppermute | solution.py:68
  145.8 6.0 %collective-permute-start.35 = (bf16[448,256]{1,0:T(8,128)(2,1)S(1)}, bf16[448,256]{1,0:T(8,128)(2,1)S(1)}, u32[]{:S(2)}, u32[]{:S(2)}) collective-permute-start(bf16[448,256]{1,0:T(8,128)(2,1)S(1)} %collective-permute-done.31.piece_refs_5_), channel_id=1, source_target_pairs={{0,2},{2,4},{4,6},{6,7},{7,5},{5,3},{3,1},{1,0},{8,10},{10,12},{12... | collective-permute-start | bytes 688136 | tf_op jit(solution)/shard_map/ppermute | solution.py:72
  150.1 6.0 %collective-permute-start.38 = (bf16[448,256]{1,0:T(8,128)(2,1)S(1)}, bf16[448,256]{1,0:T(8,128)(2,1)S(1)}, u32[]{:S(2)}, u32[]{:S(2)}) collective-permute-start(bf16[448,256]{1,0:T(8,128)(2,1)S(1)} %collective-permute-done.37.piece_refs_6_), channel_id=1, source_target_pairs={{0,1},{2,0},{4,2},{6,4},{7,6},{5,7},{3,5},{1,3},{8,9},{10,8},{12,1... | collective-permute-start | bytes 688136 | tf_op jit(solution)/shard_map/ppermute | solution.py:74
  154.5 11.1 %collective-permute-start.39 = (bf16[448,256]{1,0:T(8,128)(2,1)S(1)}, bf16[448,256]{1,0:T(8,128)(2,1)S(1)}, u32[]{:S(2)}, u32[]{:S(2)}) collective-permute-start(bf16[448,256]{1,0:T(8,128)(2,1)S(1)} %get-tuple-element.157.first_refs_0_.refs_2__0__0_), channel_id=1, source_target_pairs={{0,8},{16,24},{1,9},{17,25},{2,10},{18,26},{3,11},{19,27},{4,12},{... | collective-permute-start | bytes 688136 | tf_op jit(solution)/shard_map/ppermute | solution.py:678
  159.5 6.0 %collective-permute-start.40 = (bf16[448,256]{1,0:T(8,128)(2,1)S(1)}, bf16[448,256]{1,0:T(8,128)(2,1)S(1)}, u32[]{:S(2)}, u32[]{:S(2)}) collective-permute-start(bf16[448,256]{1,0:T(8,128)(2,1)S(1)} %get-tuple-element.159.refs_2__0__1_), channel_id=1, source_target_pairs={{0,8},{16,24},{1,9},{17,25},{2,10},{18,26},{3,11},{19,27},{4,12},{... | collective-permute-start | bytes 688136 | tf_op jit(solution)/shard_map/ppermute | solution.py:678
  160.8 6.9 %collective-permute-start.41 = (bf16[448,256]{1,0:T(8,128)(2,1)S(1)}, bf16[448,256]{1,0:T(8,128)(2,1)S(1)}, u32[]{:S(2)}, u32[]{:S(2)}) collective-permute-start(bf16[448,256]{1,0:T(8,128)(2,1)S(1)} %get-tuple-element.157.first_refs_0_.refs_2__0__0_), channel_id=1, source_target_pairs={{0,16},{8,24},{1,17},{9,25},{2,18},{10,26},{3,19},{11,27},{4,20},{... | collective-permute-start | bytes 688136 | tf_op jit(solution)/shard_map/ppermute | solution.py:681
  164.2 6.0 %collective-permute-start.42 = (bf16[448,256]{1,0:T(8,128)(2,1)S(1)}, bf16[448,256]{1,0:T(8,128)(2,1)S(1)}, u32[]{:S(2)}, u32[]{:S(2)}) collective-permute-start(bf16[448,256]{1,0:T(8,128)(2,1)S(1)} %get-tuple-element.159.refs_2__0__1_), channel_id=1, source_target_pairs={{0,16},{8,24},{1,17},{9,25},{2,18},{10,26},{3,19},{11,27},{4,20},{... | collective-permute-start | bytes 688136 | tf_op jit(solution)/shard_map/ppermute | solution.py:681
  170.2 16.2 %all-to-all-start.1 = ((bf16[8,56,448]{2,1,0:T(8,128)(2,1)}), bf16[8,56,448]{2,1,0:T(8,128)(2,1)}, u32[]{:S(2)}, u32[]{:S(2)}) async-start(bf16[8,56,448]{2,1,0:T(8,128)(2,1)} %get-tuple-element.167), calls=%async_computation.1 | async-start | bytes 917504 | tf_op jit(solution)/shard_map/all_to_all | solution.py:559
  174.5 31.1 %all-gather.6.cloned.1.call-start = ((), (), s32[]{:S(2)}) async-start(), calls=%async_computation.3 | async-start | bytes 2293760 | tf_op jit(solution)/shard_map/all_gather | solution.py:563
  174.6 1.4 collective-permute-start.43
  175.3 0.7 collective-permute-start.44
  187.9 6.1 %collective-permute-start.45 = (bf16[224,512]{1,0:T(8,128)(2,1)S(1)}, bf16[224,512]{1,0:T(8,128)(2,1)S(1)}, u32[]{:S(2)}, u32[]{:S(2)}) collective-permute-start(bf16[224,512]{1,0:T(8,128)(2,1)S(1)} %shard_map.212.refs_1_), channel_id=1, source_target_pairs={{0,2},{2,4},{4,6},{6,7},{7,5},{5,3},{3,1},{1,0},{8,10},{10,12},{12... | collective-permute-start | bytes 688136 | tf_op jit(solution)/shard_map/ppermute | solution.py:68
  188.0 6.2 %collective-permute-start.46 = (bf16[224,512]{1,0:T(8,128)(2,1)S(1)}, bf16[224,512]{1,0:T(8,128)(2,1)S(1)}, u32[]{:S(2)}, u32[]{:S(2)}) collective-permute-start(bf16[224,512]{1,0:T(8,128)(2,1)S(1)} %shard_map.212.refs_1_), channel_id=1, source_target_pairs={{0,1},{2,0},{4,2},{6,4},{7,6},{5,7},{3,5},{1,3},{8,9},{10,8},{12,1... | collective-permute-start | bytes 688136 | tf_op jit(solution)/shard_map/ppermute | solution.py:68
  194.2 6.0 %collective-permute-start.47 = (bf16[224,512]{1,0:T(8,128)(2,1)S(1)}, bf16[224,512]{1,0:T(8,128)(2,1)S(1)}, u32[]{:S(2)}, u32[]{:S(2)}) collective-permute-start(bf16[224,512]{1,0:T(8,128)(2,1)S(1)} %collective-permute-done.45.refs_2_), channel_id=1, source_target_pairs={{0,2},{2,4},{4,6},{6,7},{7,5},{5,3},{3,1},{1,0},{8,10},{10,12},{12... | collective-permute-start | bytes 688136 | tf_op jit(solution)/shard_map/ppermute | solution.py:68
  194.5 6.0 %collective-permute-start.48 = (bf16[224,512]{1,0:T(8,128)(2,1)S(1)}, bf16[224,512]{1,0:T(8,128)(2,1)S(1)}, u32[]{:S(2)}, u32[]{:S(2)}) collective-permute-start(bf16[224,512]{1,0:T(8,128)(2,1)S(1)} %collective-permute-done.46.refs_3_), channel_id=1, source_target_pairs={{0,1},{2,0},{4,2},{6,4},{7,6},{5,7},{3,5},{1,3},{8,9},{10,8},{12,1... | collective-permute-start | bytes 688136 | tf_op jit(solution)/shard_map/ppermute | solution.py:68
  200.5 7.2 %collective-permute-start.49 = (bf16[224,512]{1,0:T(8,128)(2,1)S(1)}, bf16[224,512]{1,0:T(8,128)(2,1)S(1)}, u32[]{:S(2)}, u32[]{:S(2)}) collective-permute-start(bf16[224,512]{1,0:T(8,128)(2,1)S(1)} %collective-permute-done.47.refs_4_), channel_id=1, source_target_pairs={{0,2},{2,4},{4,6},{6,7},{7,5},{5,3},{3,1},{1,0},{8,10},{10,12},{12... | collective-permute-start | bytes 688136 | tf_op jit(solution)/shard_map/ppermute | solution.py:68
  201.3 6.4 %collective-permute-start.50 = (bf16[224,512]{1,0:T(8,128)(2,1)S(1)}, bf16[224,512]{1,0:T(8,128)(2,1)S(1)}, u32[]{:S(2)}, u32[]{:S(2)}) collective-permute-start(bf16[224,512]{1,0:T(8,128)(2,1)S(1)} %collective-permute-done.48.refs_5_), channel_id=1, source_target_pairs={{0,1},{2,0},{4,2},{6,4},{7,6},{5,7},{3,5},{1,3},{8,9},{10,8},{12,1... | collective-permute-start | bytes 688136 | tf_op jit(solution)/shard_map/ppermute | solution.py:68
  207.7 5.3 %collective-permute-start.51 = (bf16[112,512]{1,0:T(8,128)(2,1)S(1)}, bf16[112,512]{1,0:T(8,128)(2,1)S(1)}, u32[]{:S(2)}, u32[]{:S(2)}) collective-permute-start(bf16[112,512]{1,0:T(8,128)(2,1)S(1)} %slice.22), channel_id=1, source_target_pairs={{0,2},{2,4},{4,6},{6,7},{7,5},{5,3},{3,1},{1,0},{8,10},{10,12},{12... | collective-permute-start | bytes 344072 | tf_op jit(solution)/shard_map/ppermute | solution.py:70
  209.3 5.0 %collective-permute-start.52 = (bf16[112,512]{1,0:T(8,128)(2,1)S(1)}, bf16[112,512]{1,0:T(8,128)(2,1)S(1)}, u32[]{:S(2)}, u32[]{:S(2)}) collective-permute-start(bf16[112,512]{1,0:T(8,128)(2,1)S(1)} %slice.23), channel_id=1, source_target_pairs={{0,1},{2,0},{4,2},{6,4},{7,6},{5,7},{3,5},{1,3},{8,9},{10,8},{12,1... | collective-permute-start | bytes 344072 | tf_op jit(solution)/shard_map/ppermute | solution.py:70
  (16 other events, 116.9 us)
Sparse Core Ops, SparseCore 0:
  77.5 22.5 all-gather.3
  186.5 19.0 all-gather.5

commit v4 on v3

--- a/solution.py
+++ b/solution.py
@@ -587,7 +587,7 @@
         strict=True,
     )
     tail = tails[-1]
-    out_columns = exchange(out_shares, tails)
+    out_columns = exchange(out_shares, raws)
     halo = lax.ppermute(tail, "seq", [(i, i + 1) for i in range(seq_count - 1)])
     y, c_rows, entry, pay, local = call(
         functools.partial(mix_kernel, tenants, heads),

time: 228 us -> 219 us (0.961)
  waiting for transfers between devices: 91.7 us -> 83.6 us
  local copies, waits for them, and re-layouts: 16.8 us -> 13 us
  other arithmetic: 2.04 us -> 4.77 us
    ppermute x36, waiting for transfers between devices: 55.6 us -> 48.1 us  [ring_gather(): got = (lax.ppermute(one, axis, ahead), lax.ppermute(two, axis, behind))]
    all_to_all x2, waiting for transfers between devices: 10.4 us -> 14.4 us  [exchange(): return lax.all_to_all(value, 'tp', 0, 0, tiled=False)]
    unnamed x48 -> x42, local copies, waits for them, and re-layouts: 14.1 us -> 10.2 us
    ppermute x2, waiting for transfers between devices: 2.88 us -> 0.01 us  [ring_gather(): got = (lax.ppermute(two, axis, behind),) * 2]
  transfers between devices with their start and end apart: 57 -> 57, of which waited for: 41 -> 39; matrix products, arithmetic and copies ran while one was open for 2% -> 3% of each run, Pallas kernels for 8% -> 9%
where the time goes in v4:
time: 219 us; the launch traced here: 216 us
  waiting for transfers between devices  83.6 us (38%)
  starting transfers between devices  68.8 us (31%)
  Pallas kernels  25.7 us (12%)
  between operations  14.5 us (7%)
  local copies, waits for them, and re-layouts  13 us (6%)
  blocking collectives  5.65 us (3%)
  other arithmetic  4.77 us (2%)
    ppermute x36, waiting for transfers between devices, ring_gather(): got = (lax.ppermute(one, axis, ahead), lax.ppermute(two, axis, behind))  48.1 us
    ppermute x36, starting transfers between devices, ring_gather(): got = (lax.ppermute(one, axis, ahead), lax.ppermute(two, axis, behind))  37.9 us
    pallas_call x12, Pallas kernels, call(): pl.pallas_call(kernel, out_shape=out_shape, in_specs=specs, out_specs=jax...  24.4 us
    all_to_all x2, waiting for transfers between devices, exchange(): return lax.all_to_all(value, 'tp', 0, 0, tiled=False)  14.4 us
    unnamed x42, local copies, waits for them, and re-layouts  10.2 us
    all_to_all x2, starting transfers between devices, exchange(): return lax.all_to_all(value, 'tp', 0, 0, tiled=False)  9.38 us
    all_gather x1, blocking collectives, on_device(): all_pays = lax.all_gather(pay, 'seq', axis=0, tiled=False)  5.65 us
    ppermute x2, starting transfers between devices, far(): return lax.ppermute(value, 'seq', [(0, 2), (1, 3)])  4.91 us
  transfers between devices with their start and end apart: 57, of which 39 were waited for; matrix products, arithmetic and copies ran while one was open for 3% of the time, Pallas kernels for 9%

profile of v4, /device:TPU:0, one launch (start us, length us, event | category | flops | bytes accessed | tf_op | source)
XLA Modules:
  0.0 216.0 jit_solution(4533845179671201311)
XLA Ops:
  8.4 3.1 %collective-permute-start = (bf16[448,256]{1,0:T(8,128)(2,1)S(1)}, bf16[448,256]{1,0:T(8,128)(2,1)}, u32[]{:S(2)}, u32[]{:S(2)}) collective-permute-start(bf16[448,256]{1,0:T(8,128)(2,1)S(1)} %get-tuple-element.90.refs_1_.refs_11__0_), channel_id=1, source_target_pairs={{0,2},{2,4},{4,6},{6,7},{7,5},{5,3},{3,1},{1,0},{8,10},{10,12},{12... | collective-permute-start | bytes 688136 | tf_op jit(solution)/shard_map/ppermute | solution.py:68
  11.5 2.0 collective-permute-start.4
  13.5 4.4 %collective-permute-done.refs_2_ = bf16[448,256]{1,0:T(8,128)(2,1)} collective-permute-done((bf16[448,256]{1,0:T(8,128)(2,1)S(1)}, bf16[448,256]{1,0:T(8,128)(2,1)}, u32[]{:S(2)}, u32[]{:S(2)}) %collective-permute-start) | collective-permute-done | bytes 229408 | tf_op jit(solution)/shard_map/ppermute | solution.py:68
  18.0 2.2 collective-permute-done.1.refs_3_
  20.1 1.6 collective-permute-start.2
  22.8 2.3 %collective-permute-done.5.refs_3_ = bf16[448,256]{1,0:T(8,128)(2,1)} collective-permute-done((bf16[448,256]{1,0:T(8,128)(2,1)S(1)}, bf16[448,256]{1,0:T(8,128)(2,1)}, u32[]{:S(2)}, u32[]{:S(2)}) %collective-permute-start.5) | collective-permute-done | bytes 229408 | tf_op jit(solution)/shard_map/ppermute | solution.py:68
  25.0 1.6 collective-permute-start.8
  27.8 1.4 copy-done.2
  29.3 1.3 copy-done.4
  31.9 1.6 collective-permute-start.6
  34.0 1.6 collective-permute-start.11
  40.7 1.7 collective-permute-start.10
  42.4 1.7 collective-permute-done.11.refs_6_
  44.2 1.4 collective-permute-start.13
  46.7 3.7 %shard_map.204 = (f32[320,256]{1,0:T(8,128)S(1)}, f32[192,256]{1,0:T(8,128)S(1)}, f32[8,256]{1,0:T(8,128)S(1)}, f32[8,320]{1,0:T(8,128)}) custom-call(s32[8,8]{1,0:T(8,128)S(1)} %copy-done.6, bf16[448,256]{1,0:T(8,128)(2,1)S(1)} %get-tuple-element.90.refs_1_.refs_11__0_, bf16[448,256]{1,0:T(8,128)(2,1)} %collective-permute-done.refs_2_, ...), custom_call_target="tpu_custom_call" | custom-call | flops 968884224 | bytes 5619968 | tf_op jit(solution)/shard_map/pallas_call | solution.py:131
  50.5 3.0 %shard_map.205 = (f32[320,256]{1,0:T(8,128)S(1)}, f32[192,256]{1,0:T(8,128)S(1)}, f32[8,256]{1,0:T(8,128)S(1)}, f32[8,320]{1,0:T(8,128)S(1)}) custom-call(s32[8,8]{1,0:T(8,128)S(1)} %copy-done.6, bf16[448,256]{1,0:T(8,128)(2,1)S(1)} %get-tuple-element.94.refs_1_.refs_11__1_, bf16[448,256]{1,0:T(8,128)(2,1)S(1)} %collective-permute-done.4.refs_2_, ...), custom_call_target="tpu_custom_call" | custom-call | flops 968884224 | bytes 5619968 | tf_op jit(solution)/shard_map/pallas_call | solution.py:131
  53.5 5.9 %all-to-all-start = ((bf16[8,48,448]{2,1,0:T(8,128)(2,1)}), bf16[8,48,448]{2,1,0:T(8,128)(2,1)S(1)}, u32[]{:S(2)}, u32[]{:S(2)}) async-start(bf16[8,48,448]{2,1,0:T(8,128)(2,1)} %get-tuple-element.135), calls=%async_computation | async-start | bytes 786432 | tf_op jit(solution)/shard_map/all_to_all | solution.py:559
  61.6 3.3 %shard_map.206 = (f32[192,512]{1,0:T(8,128)S(1)}, bf16[64,512]{1,0:T(8,128)(2,1)S(1)}, f32[8,512]{1,0:T(8,128)S(1)}, bf16[208,128]{1,0:T(8,128)(2,1)S(1)}, f32[768,128]{1,0:T(8,128)S(1)}) custom-call(s32[4,2]{1,0:T(4,128)S(1)} %copy.24.bounds_ref.refs_0_, f32[3]{0:T(128)S(1)} %copy-done.12, f32[3]{0:T(128)S(1)} %copy-done.13, f32[3]{0:T(128)S(1)} %copy-done.14, ...), custom_call_target="tpu_custom_call" | custom-call | flops 1000000000 | bytes 691268 | tf_op jit(solution)/shard_map/pallas_call | solution.py:131
  64.9 3.8 %all-to-all-done = bf16[8,48,448]{2,1,0:T(8,128)(2,1)S(1)} async-done(((bf16[8,48,448]{2,1,0:T(8,128)(2,1)}), bf16[8,48,448]{2,1,0:T(8,128)(2,1)S(1)}, u32[]{:S(2)}, u32[]{:S(2)}) %all-to-all-start) | async-done | bytes 344096 | tf_op jit(solution)/shard_map/all_to_all | solution.py:559
  69.5 5.7 %all-gather = bf16[832,128]{1,0:T(8,128)(2,1)S(1)} all-gather(bf16[208,128]{1,0:T(8,128)(2,1)S(1)} %get-tuple-element.116), channel_id=2, replica_groups=mesh['seq'=4,'tp'=8] {'seq'}, dimensions={0}, use_global_device_ids=true | all-gather | bytes 266240 | tf_op jit(solution)/shard_map/all_gather | solution.py:612
  78.3 5.1 %collective-permute-done.15.refs_2_ = bf16[192,512]{1,0:T(8,128)(2,1)S(1)} collective-permute-done((bf16[192,512]{1,0:T(8,128)(2,1)S(1)}, bf16[192,512]{1,0:T(8,128)(2,1)S(1)}, u32[]{:S(2)}, u32[]{:S(2)}) %collective-permute-start.15) | collective-permute-done | bytes 196640 | tf_op jit(solution)/shard_map/ppermute | solution.py:68
  84.1 1.5 collective-permute-start.17
  86.1 4.1 %collective-permute-done.17.refs_4_ = bf16[192,512]{1,0:T(8,128)(2,1)S(1)} collective-permute-done((bf16[192,512]{1,0:T(8,128)(2,1)S(1)}, bf16[192,512]{1,0:T(8,128)(2,1)S(1)}, u32[]{:S(2)}, u32[]{:S(2)}) %collective-permute-start.17) | collective-permute-done | bytes 196640 | tf_op jit(solution)/shard_map/ppermute | solution.py:68
  91.4 1.5 collective-permute-start.19
  93.5 1.7 collective-permute-start.22
  95.2 4.0 %collective-permute-done.22 = bf16[768,64]{1,0:T(8,128)(2,1)S(1)} collective-permute-done((bf16[768,64]{1,0:T(8,128)(2,1)S(1)}, bf16[768,64]{1,0:T(8,128)(2,1)S(1)}, u32[]{:S(2)}, u32[]{:S(2)}) %collective-permute-start.22) | collective-permute-done | bytes 98336 | tf_op jit(solution)/shard_map/ppermute | solution.py:95
  100.0 1.5 collective-permute-start.23
  102.1 1.4 copy-done.3
  104.6 1.5 collective-permute-done.24.refs_9_
  106.2 1.8 shard_map.209
  108.0 1.5 collective-permute-start.25
  110.1 1.5 collective-permute-start.29
  112.1 4.2 %collective-permute-done.25.piece_refs_1_ = bf16[448,256]{1,0:T(8,128)(2,1)S(1)} collective-permute-done((bf16[448,256]{1,0:T(8,128)(2,1)S(1)}, bf16[448,256]{1,0:T(8,128)(2,1)S(1)}, u32[]{:S(2)}, u32[]{:S(2)}) %collective-permute-start.25) | collective-permute-done | bytes 229408 | tf_op jit(solution)/shard_map/ppermute | solution.py:68
  116.2 1.7 collective-permute-done.26.piece_refs_2_
  118.5 1.4 collective-permute-start.28
  121.2 1.7 collective-permute-done.30.piece_refs_2_
  123.4 1.4 collective-permute-start.34
  124.9 1.6 collective-permute-done.27.piece_refs_3_
  128.3 1.4 collective-permute-start.32
  129.8 1.6 collective-permute-done.33.piece_refs_3_
  132.7 1.3 collective-permute-start.37
  134.0 3.2 %fusion.w_ref = bf16[672,3584]{1,0:T(8,128)(2,1)S(1)} fusion(bf16[3,224,3584]{2,1,0:T(8,128)(2,1)} %param.32, f32[3584]{0:T(1024)S(1)} %copy-done.18), kind=kLoop, calls=%fused_computation.1 | loop fusion | flops 7225344 | bytes 9648128 | tf_op jit(solution)/shard_map/convert_element_type | solution.py:653
  139.3 1.4 collective-permute-start.38
  140.8 2.5 %collective-permute-done.35.piece_refs_7_ = bf16[448,256]{1,0:T(8,128)(2,1)S(1)} collective-permute-done((bf16[448,256]{1,0:T(8,128)(2,1)S(1)}, bf16[448,256]{1,0:T(8,128)(2,1)S(1)}, u32[]{:S(2)}, u32[]{:S(2)}) %collective-permute-start.35) | collective-permute-done | bytes 229408 | tf_op jit(solution)/shard_map/ppermute | solution.py:72
  143.3 2.6 %shard_map.210 = (bf16[224,256]{1,0:T(8,128)(2,1)S(1)}, bf16[448,256]{1,0:T(8,128)(2,1)S(1)}) custom-call(s32[8,8]{1,0:T(8,128)S(1)} %copy-done.6, bf16[448,256]{1,0:T(8,128)(2,1)S(1)} %get-tuple-element.141.piece_refs_0_.refs_11__0_, bf16[448,256]{1,0:T(8,128)(2,1)S(1)} %collective-permute-done.25.piece_refs_1_, ...), custom_call_target="tpu_custom_call" | custom-call | flops 1233125376 | bytes 6652160 | tf_op jit(solution)/shard_map/pallas_call | solution.py:131
  145.9 1.3 collective-permute-start.39
  147.3 3.4 %shard_map.211 = (bf16[224,256]{1,0:T(8,128)(2,1)S(1)}, bf16[448,256]{1,0:T(8,128)(2,1)S(1)}, bf16[448,512]{1,0:T(8,128)(2,1)}) custom-call(s32[8,8]{1,0:T(8,128)S(1)} %copy-done.6, bf16[448,256]{1,0:T(8,128)(2,1)S(1)} %get-tuple-element.145.piece_refs_0_.refs_11__1_, bf16[448,256]{1,0:T(8,128)(2,1)S(1)} %collective-permute-done.29.piece_refs_1_, ...), custom_call_target="tpu_custom_call" | custom-call | flops 1233125376 | bytes 6881536 | tf_op jit(solution)/shard_map/pallas_call | solution.py:131
  152.0 3.6 %collective-permute-start.41 = (bf16[448,256]{1,0:T(8,128)(2,1)S(1)}, bf16[448,256]{1,0:T(8,128)(2,1)S(1)}, u32[]{:S(2)}, u32[]{:S(2)}) collective-permute-start(bf16[448,256]{1,0:T(8,128)(2,1)S(1)} %get-tuple-element.157.first_refs_0_.refs_2__0__0_), channel_id=1, source_target_pairs={{0,16},{8,24},{1,17},{9,25},{2,18},{10,26},{3,19},{11,27},{4,20},{... | collective-permute-start | bytes 688136 | tf_op jit(solution)/shard_map/ppermute | solution.py:681
  156.9 2.2 %collective-permute-done.41.refs_2__2__0_ = bf16[448,256]{1,0:T(8,128)(2,1)S(1)} collective-permute-done((bf16[448,256]{1,0:T(8,128)(2,1)S(1)}, bf16[448,256]{1,0:T(8,128)(2,1)S(1)}, u32[]{:S(2)}, u32[]{:S(2)}) %collective-permute-start.41) | collective-permute-done | bytes 229408 | tf_op jit(solution)/shard_map/ppermute | solution.py:681
  159.1 2.5 %collective-permute-done.42.refs_2__2__1_ = bf16[448,256]{1,0:T(8,128)(2,1)S(1)} collective-permute-done((bf16[448,256]{1,0:T(8,128)(2,1)S(1)}, bf16[448,256]{1,0:T(8,128)(2,1)S(1)}, u32[]{:S(2)}, u32[]{:S(2)}) %collective-permute-start.42) | collective-permute-done | bytes 229408 | tf_op jit(solution)/shard_map/ppermute | solution.py:681
  161.5 3.5 %all-to-all-start.1 = ((bf16[8,56,448]{2,1,0:T(8,128)(2,1)}), bf16[8,56,448]{2,1,0:T(8,128)(2,1)S(1)}, u32[]{:S(2)}, u32[]{:S(2)}) async-start(bf16[8,56,448]{2,1,0:T(8,128)(2,1)} %get-tuple-element.167), calls=%async_computation.1 | async-start | bytes 917504 | tf_op jit(solution)/shard_map/all_to_all | solution.py:559
  166.5 10.6 %all-to-all-done.1 = bf16[8,56,448]{2,1,0:T(8,128)(2,1)S(1)} async-done(((bf16[8,56,448]{2,1,0:T(8,128)(2,1)}), bf16[8,56,448]{2,1,0:T(8,128)(2,1)S(1)}, u32[]{:S(2)}, u32[]{:S(2)}) %all-to-all-start.1) | async-done | bytes 401440 | tf_op jit(solution)/shard_map/all_to_all | solution.py:559
  177.9 1.5 shard_map.212.refs_1_
  179.5 2.0 collective-permute-start.46
  181.5 4.8 %collective-permute-done.45.refs_2_ = bf16[224,512]{1,0:T(8,128)(2,1)S(1)} collective-permute-done((bf16[224,512]{1,0:T(8,128)(2,1)S(1)}, bf16[224,512]{1,0:T(8,128)(2,1)S(1)}, u32[]{:S(2)}, u32[]{:S(2)}) %collective-permute-start.45) | collective-permute-done | bytes 229408 | tf_op jit(solution)/shard_map/ppermute | solution.py:68
  186.4 2.2 %collective-permute-start.48 = (bf16[224,512]{1,0:T(8,128)(2,1)S(1)}, bf16[224,512]{1,0:T(8,128)(2,1)S(1)}, u32[]{:S(2)}, u32[]{:S(2)}) collective-permute-start(bf16[224,512]{1,0:T(8,128)(2,1)S(1)} %collective-permute-done.46.refs_3_), channel_id=1, source_target_pairs={{0,1},{2,0},{4,2},{6,4},{7,6},{5,7},{3,5},{1,3},{8,9},{10,8},{12,1... | collective-permute-start | bytes 688136 | tf_op jit(solution)/shard_map/ppermute | solution.py:68
  188.7 4.0 %collective-permute-done.47.refs_4_ = bf16[224,512]{1,0:T(8,128)(2,1)S(1)} collective-permute-done((bf16[224,512]{1,0:T(8,128)(2,1)S(1)}, bf16[224,512]{1,0:T(8,128)(2,1)S(1)}, u32[]{:S(2)}, u32[]{:S(2)}) %collective-permute-start.47) | collective-permute-done | bytes 229408 | tf_op jit(solution)/shard_map/ppermute | solution.py:68
  193.0 1.6 collective-permute-start.50
  194.7 2.0 all-gather.6.cloned.1.call-done
  196.7 1.5 copy-done.1
  199.1 2.1 collective-permute-start.51
  202.0 2.1 collective-permute-done.51.refs_8_
  204.1 1.9 collective-permute-done.52.refs_9_
  206.0 2.2 %shard_map.214 = bf16[512,448]{1,0:T(8,128)(2,1)S(1)} custom-call(s32[8,8]{1,0:T(8,128)S(1)} %copy-done.6, bf16[224,512]{1,0:T(8,128)(2,1)S(1)} %shard_map.212.refs_1_, bf16[224,512]{1,0:T(8,128)(2,1)S(1)} %collective-permute-done.45.refs_2_, bf16[224,512]{1,0:T(8,128)(2,1)S(1)} %collective-permute-done.46.refs_3_, ...), custom_call_target="tpu_custom_call" | custom-call | flops 822083584 | bytes 3899648 | tf_op jit(solution)/shard_map/pallas_call | solution.py:131
  (119 shorter events, 40.0 us)
Async XLA Ops:
  7.2 29.6 %copy-start = (bf16[2,192,3584]{2,1,0:T(8,128)(2,1)S(1)}, bf16[2,192,3584]{2,1,0:T(8,128)(2,1)}, u32[]{:S(2)}) copy-start(bf16[2,192,3584]{2,1,0:T(8,128)(2,1)} %xz_ref) | copy-start | bytes 8257540
  8.4 9.6 %collective-permute-start = (bf16[448,256]{1,0:T(8,128)(2,1)S(1)}, bf16[448,256]{1,0:T(8,128)(2,1)}, u32[]{:S(2)}, u32[]{:S(2)}) collective-permute-start(bf16[448,256]{1,0:T(8,128)(2,1)S(1)} %get-tuple-element.90.refs_1_.refs_11__0_), channel_id=1, source_target_pairs={{0,2},{2,4},{4,6},{6,7},{7,5},{5,3},{3,1},{1,0},{8,10},{10,12},{12... | collective-permute-start | bytes 688136 | tf_op jit(solution)/shard_map/ppermute | solution.py:68
  11.5 8.6 %collective-permute-start.1 = (bf16[448,256]{1,0:T(8,128)(2,1)S(1)}, bf16[448,256]{1,0:T(8,128)(2,1)}, u32[]{:S(2)}, u32[]{:S(2)}) collective-permute-start(bf16[448,256]{1,0:T(8,128)(2,1)S(1)} %get-tuple-element.90.refs_1_.refs_11__0_), channel_id=1, source_target_pairs={{0,1},{2,0},{4,2},{6,4},{7,6},{5,7},{3,5},{1,3},{8,9},{10,8},{12,1... | collective-permute-start | bytes 688136 | tf_op jit(solution)/shard_map/ppermute | solution.py:68
  11.5 11.3 %collective-permute-start.4 = (bf16[448,256]{1,0:T(8,128)(2,1)S(1)}, bf16[448,256]{1,0:T(8,128)(2,1)S(1)}, u32[]{:S(2)}, u32[]{:S(2)}) collective-permute-start(bf16[448,256]{1,0:T(8,128)(2,1)S(1)} %get-tuple-element.94.refs_1_.refs_11__1_), channel_id=1, source_target_pairs={{0,2},{2,4},{4,6},{6,7},{7,5},{5,3},{3,1},{1,0},{8,10},{10,12},{12... | collective-permute-start | bytes 688136 | tf_op jit(solution)/shard_map/ppermute | solution.py:68
  13.5 11.5 %collective-permute-start.5 = (bf16[448,256]{1,0:T(8,128)(2,1)S(1)}, bf16[448,256]{1,0:T(8,128)(2,1)}, u32[]{:S(2)}, u32[]{:S(2)}) collective-permute-start(bf16[448,256]{1,0:T(8,128)(2,1)S(1)} %get-tuple-element.94.refs_1_.refs_11__1_), channel_id=1, source_target_pairs={{0,1},{2,0},{4,2},{6,4},{7,6},{5,7},{3,5},{1,3},{8,9},{10,8},{12,1... | collective-permute-start | bytes 688136 | tf_op jit(solution)/shard_map/ppermute | solution.py:68
  20.1 11.7 %collective-permute-start.2 = (bf16[448,256]{1,0:T(8,128)(2,1)}, bf16[448,256]{1,0:T(8,128)(2,1)}, u32[]{:S(2)}, u32[]{:S(2)}) collective-permute-start(bf16[448,256]{1,0:T(8,128)(2,1)} %collective-permute-done.refs_2_), channel_id=1, source_target_pairs={{0,2},{2,4},{4,6},{6,7},{7,5},{5,3},{3,1},{1,0},{8,10},{10,12},{12... | collective-permute-start | bytes 688136 | tf_op jit(solution)/shard_map/ppermute | solution.py:68
  21.7 10.2 %collective-permute-start.3 = (bf16[448,256]{1,0:T(8,128)(2,1)}, bf16[448,256]{1,0:T(8,128)(2,1)}, u32[]{:S(2)}, u32[]{:S(2)}) collective-permute-start(bf16[448,256]{1,0:T(8,128)(2,1)} %collective-permute-done.1.refs_3_), channel_id=1, source_target_pairs={{0,1},{2,0},{4,2},{6,4},{7,6},{5,7},{3,5},{1,3},{8,9},{10,8},{12,1... | collective-permute-start | bytes 688136 | tf_op jit(solution)/shard_map/ppermute | solution.py:68
  25.0 8.9 %collective-permute-start.8 = (bf16[448,256]{1,0:T(8,128)(2,1)S(1)}, bf16[448,256]{1,0:T(8,128)(2,1)}, u32[]{:S(2)}, u32[]{:S(2)}) collective-permute-start(bf16[448,256]{1,0:T(8,128)(2,1)S(1)} %collective-permute-done.4.refs_2_), channel_id=1, source_target_pairs={{0,2},{2,4},{4,6},{6,7},{7,5},{5,3},{3,1},{1,0},{8,10},{10,12},{12... | collective-permute-start | bytes 688136 | tf_op jit(solution)/shard_map/ppermute | solution.py:68
  26.6 7.4 %collective-permute-start.9 = (bf16[448,256]{1,0:T(8,128)(2,1)}, bf16[448,256]{1,0:T(8,128)(2,1)}, u32[]{:S(2)}, u32[]{:S(2)}) collective-permute-start(bf16[448,256]{1,0:T(8,128)(2,1)} %collective-permute-done.5.refs_3_), channel_id=1, source_target_pairs={{0,1},{2,0},{4,2},{6,4},{7,6},{5,7},{3,5},{1,3},{8,9},{10,8},{12,1... | collective-permute-start | bytes 688136 | tf_op jit(solution)/shard_map/ppermute | solution.py:68
  31.8 14.8 %copy-start.6 = (s32[8,8]{1,0:T(8,128)S(1)}, s32[8,8]{1,0:T(8,128)}, u32[]{:S(2)}) copy-start(s32[8,8]{1,0:T(8,128)} %constant.7.clone.refs_0_.slots_ref) | copy-start | bytes 772
  31.9 7.6 %collective-permute-start.6 = (bf16[448,256]{1,0:T(8,128)(2,1)}, bf16[448,256]{1,0:T(8,128)(2,1)S(1)}, u32[]{:S(2)}, u32[]{:S(2)}) collective-permute-start(bf16[448,256]{1,0:T(8,128)(2,1)} %collective-permute-done.2.refs_4_), channel_id=1, source_target_pairs={{0,2},{2,4},{4,6},{6,7},{7,5},{5,3},{3,1},{1,0},{8,10},{10,12},{12... | collective-permute-start | bytes 688136 | tf_op jit(solution)/shard_map/ppermute | solution.py:68
  33.5 7.2 %collective-permute-start.7 = (bf16[448,256]{1,0:T(8,128)(2,1)}, bf16[448,256]{1,0:T(8,128)(2,1)S(1)}, u32[]{:S(2)}, u32[]{:S(2)}) collective-permute-start(bf16[448,256]{1,0:T(8,128)(2,1)} %collective-permute-done.3.refs_5_), channel_id=1, source_target_pairs={{0,1},{2,0},{4,2},{6,4},{7,6},{5,7},{3,5},{1,3},{8,9},{10,8},{12,1... | collective-permute-start | bytes 688136 | tf_op jit(solution)/shard_map/ppermute | solution.py:68
  34.0 10.1 %collective-permute-start.11 = (bf16[448,256]{1,0:T(8,128)(2,1)}, bf16[448,256]{1,0:T(8,128)(2,1)S(1)}, u32[]{:S(2)}, u32[]{:S(2)}) collective-permute-start(bf16[448,256]{1,0:T(8,128)(2,1)} %collective-permute-done.8.refs_4_), channel_id=1, source_target_pairs={{0,2},{2,4},{4,6},{6,7},{7,5},{5,3},{3,1},{1,0},{8,10},{10,12},{12... | collective-permute-start | bytes 688136 | tf_op jit(solution)/shard_map/ppermute | solution.py:68
  35.6 8.6 %collective-permute-start.12 = (bf16[448,256]{1,0:T(8,128)(2,1)}, bf16[448,256]{1,0:T(8,128)(2,1)S(1)}, u32[]{:S(2)}, u32[]{:S(2)}) collective-permute-start(bf16[448,256]{1,0:T(8,128)(2,1)} %collective-permute-done.9.refs_5_), channel_id=1, source_target_pairs={{0,1},{2,0},{4,2},{6,4},{7,6},{5,7},{3,5},{1,3},{8,9},{10,8},{12,1... | collective-permute-start | bytes 688136 | tf_op jit(solution)/shard_map/ppermute | solution.py:68
  40.7 6.0 %collective-permute-start.10 = (bf16[448,256]{1,0:T(8,128)(2,1)S(1)}, bf16[448,256]{1,0:T(8,128)(2,1)S(1)}, u32[]{:S(2)}, u32[]{:S(2)}) collective-permute-start(bf16[448,256]{1,0:T(8,128)(2,1)S(1)} %collective-permute-done.6.refs_6_), channel_id=1, source_target_pairs={{0,2},{2,4},{4,6},{6,7},{7,5},{5,3},{3,1},{1,0},{8,10},{10,12},{12... | collective-permute-start | bytes 688136 | tf_op jit(solution)/shard_map/ppermute | solution.py:72
  44.2 6.3 %collective-permute-start.13 = (bf16[448,256]{1,0:T(8,128)(2,1)S(1)}, bf16[448,256]{1,0:T(8,128)(2,1)S(1)}, u32[]{:S(2)}, u32[]{:S(2)}) collective-permute-start(bf16[448,256]{1,0:T(8,128)(2,1)S(1)} %collective-permute-done.12.refs_7_), channel_id=1, source_target_pairs={{0,1},{2,0},{4,2},{6,4},{7,6},{5,7},{3,5},{1,3},{8,9},{10,8},{12,1... | collective-permute-start | bytes 688136 | tf_op jit(solution)/shard_map/ppermute | solution.py:74
  50.4 11.1 %copy-start.8 = (f32[4,192]{1,0:T(4,128)S(1)}, f32[4,192]{1,0:T(4,128)}, u32[]{:S(2)}) copy-start(f32[4,192]{1,0:T(4,128)} %conv_x_ref.1) | copy-start | bytes 9220
  50.4 11.1 %copy-start.9 = (f32[4,128]{1,0:T(4,128)S(1)}, f32[4,128]{1,0:T(4,128)}, u32[]{:S(2)}) copy-start(f32[4,128]{1,0:T(4,128)} %conv_bc_ref.1) | copy-start | bytes 6148
  50.4 11.1 %copy-start.10 = (s32[512]{0:T(512)S(1)}, s32[512]{0:T(512)}, u32[]{:S(2)}) copy-start(s32[512]{0:T(512)} %param.35) | copy-start | bytes 6148
  53.5 15.2 %all-to-all-start = ((bf16[8,48,448]{2,1,0:T(8,128)(2,1)}), bf16[8,48,448]{2,1,0:T(8,128)(2,1)S(1)}, u32[]{:S(2)}, u32[]{:S(2)}) async-start(bf16[8,48,448]{2,1,0:T(8,128)(2,1)} %get-tuple-element.135), calls=%async_computation | async-start | bytes 786432 | tf_op jit(solution)/shard_map/all_to_all | solution.py:559
  59.4 42.7 %all-gather.4.cloned.1.call-start = ((), (), s32[]{:S(2)}) async-start(), calls=%async_computation.2 | async-start | bytes 1966080 | tf_op jit(solution)/shard_map/all_gather | solution.py:563
  59.4 2.1 collective-permute-start.14
  76.2 7.2 %collective-permute-start.15 = (bf16[192,512]{1,0:T(8,128)(2,1)S(1)}, bf16[192,512]{1,0:T(8,128)(2,1)S(1)}, u32[]{:S(2)}, u32[]{:S(2)}) collective-permute-start(bf16[192,512]{1,0:T(8,128)(2,1)S(1)} %get-tuple-element.125.refs_1_), channel_id=1, source_target_pairs={{0,2},{2,4},{4,6},{6,7},{7,5},{5,3},{3,1},{1,0},{8,10},{10,12},{12... | collective-permute-start | bytes 589832 | tf_op jit(solution)/shard_map/ppermute | solution.py:68
  77.2 6.9 %collective-permute-start.16 = (bf16[192,512]{1,0:T(8,128)(2,1)S(1)}, bf16[192,512]{1,0:T(8,128)(2,1)S(1)}, u32[]{:S(2)}, u32[]{:S(2)}) collective-permute-start(bf16[192,512]{1,0:T(8,128)(2,1)S(1)} %get-tuple-element.125.refs_1_), channel_id=1, source_target_pairs={{0,1},{2,0},{4,2},{6,4},{7,6},{5,7},{3,5},{1,3},{8,9},{10,8},{12,1... | collective-permute-start | bytes 589832 | tf_op jit(solution)/shard_map/ppermute | solution.py:68
  84.1 6.1 %collective-permute-start.17 = (bf16[192,512]{1,0:T(8,128)(2,1)S(1)}, bf16[192,512]{1,0:T(8,128)(2,1)S(1)}, u32[]{:S(2)}, u32[]{:S(2)}) collective-permute-start(bf16[192,512]{1,0:T(8,128)(2,1)S(1)} %collective-permute-done.15.refs_2_), channel_id=1, source_target_pairs={{0,2},{2,4},{4,6},{6,7},{7,5},{5,3},{3,1},{1,0},{8,10},{10,12},{12... | collective-permute-start | bytes 589832 | tf_op jit(solution)/shard_map/ppermute | solution.py:68
  85.5 5.9 %collective-permute-start.18 = (bf16[192,512]{1,0:T(8,128)(2,1)S(1)}, bf16[192,512]{1,0:T(8,128)(2,1)S(1)}, u32[]{:S(2)}, u32[]{:S(2)}) collective-permute-start(bf16[192,512]{1,0:T(8,128)(2,1)S(1)} %collective-permute-done.16.refs_3_), channel_id=1, source_target_pairs={{0,1},{2,0},{4,2},{6,4},{7,6},{5,7},{3,5},{1,3},{8,9},{10,8},{12,1... | collective-permute-start | bytes 589832 | tf_op jit(solution)/shard_map/ppermute | solution.py:68
  86.1 7.3 %collective-permute-start.21 = (bf16[768,64]{1,0:T(8,128)(2,1)S(1)}, bf16[768,64]{1,0:T(8,128)(2,1)S(1)}, u32[]{:S(2)}, u32[]{:S(2)}) collective-permute-start(bf16[768,64]{1,0:T(8,128)(2,1)S(1)} %get-tuple-element.131), channel_id=1, source_target_pairs={{0,8},{8,0},{16,24},{24,16},{1,9},{9,1},{17,25},{25,17},{2,10},{10... | collective-permute-start | bytes 294920 | tf_op jit(solution)/shard_map/ppermute | solution.py:95
  91.4 8.6 %collective-permute-start.19 = (bf16[192,512]{1,0:T(8,128)(2,1)S(1)}, bf16[192,512]{1,0:T(8,128)(2,1)S(1)}, u32[]{:S(2)}, u32[]{:S(2)}) collective-permute-start(bf16[192,512]{1,0:T(8,128)(2,1)S(1)} %collective-permute-done.17.refs_4_), channel_id=1, source_target_pairs={{0,2},{2,4},{4,6},{6,7},{7,5},{5,3},{3,1},{1,0},{8,10},{10,12},{12... | collective-permute-start | bytes 589832 | tf_op jit(solution)/shard_map/ppermute | solution.py:68
  92.9 7.1 %collective-permute-start.20 = (bf16[192,512]{1,0:T(8,128)(2,1)S(1)}, bf16[192,512]{1,0:T(8,128)(2,1)S(1)}, u32[]{:S(2)}, u32[]{:S(2)}) collective-permute-start(bf16[192,512]{1,0:T(8,128)(2,1)S(1)} %collective-permute-done.18.refs_5_), channel_id=1, source_target_pairs={{0,1},{2,0},{4,2},{6,4},{7,6},{5,7},{3,5},{1,3},{8,9},{10,8},{12,1... | collective-permute-start | bytes 589832 | tf_op jit(solution)/shard_map/ppermute | solution.py:68
  93.5 40.5 %copy-start.18 = (f32[3584]{0:T(1024)S(1)}, f32[3584]{0:T(1024)}, u32[]{:S(2)}) copy-start(f32[3584]{0:T(1024)} %param.31) | copy-start | bytes 43012
  93.5 5.7 %collective-permute-start.22 = (bf16[768,64]{1,0:T(8,128)(2,1)S(1)}, bf16[768,64]{1,0:T(8,128)(2,1)S(1)}, u32[]{:S(2)}, u32[]{:S(2)}) collective-permute-start(bf16[768,64]{1,0:T(8,128)(2,1)S(1)} %add.6), channel_id=1, source_target_pairs={{0,16},{8,24},{16,0},{24,8},{1,17},{9,25},{17,1},{25,9},{2,18},{10... | collective-permute-start | bytes 294920 | tf_op jit(solution)/shard_map/ppermute | solution.py:95
  100.0 4.7 %collective-permute-start.23 = (bf16[96,512]{1,0:T(8,128)(2,1)S(1)}, bf16[96,512]{1,0:T(8,128)(2,1)S(1)}, u32[]{:S(2)}, u32[]{:S(2)}) collective-permute-start(bf16[96,512]{1,0:T(8,128)(2,1)S(1)} %slice.20), channel_id=1, source_target_pairs={{0,2},{2,4},{4,6},{6,7},{7,5},{5,3},{3,1},{1,0},{8,10},{10,12},{12... | collective-permute-start | bytes 294920 | tf_op jit(solution)/shard_map/ppermute | solution.py:70
  101.5 4.7 %collective-permute-start.24 = (bf16[96,512]{1,0:T(8,128)(2,1)S(1)}, bf16[96,512]{1,0:T(8,128)(2,1)S(1)}, u32[]{:S(2)}, u32[]{:S(2)}) collective-permute-start(bf16[96,512]{1,0:T(8,128)(2,1)S(1)} %slice.21), channel_id=1, source_target_pairs={{0,1},{2,0},{4,2},{6,4},{7,6},{5,7},{3,5},{1,3},{8,9},{10,8},{12,1... | collective-permute-start | bytes 294920 | tf_op jit(solution)/shard_map/ppermute | solution.py:70
  108.0 8.3 %collective-permute-start.25 = (bf16[448,256]{1,0:T(8,128)(2,1)S(1)}, bf16[448,256]{1,0:T(8,128)(2,1)S(1)}, u32[]{:S(2)}, u32[]{:S(2)}) collective-permute-start(bf16[448,256]{1,0:T(8,128)(2,1)S(1)} %get-tuple-element.141.piece_refs_0_.refs_11__0_), channel_id=1, source_target_pairs={{0,2},{2,4},{4,6},{6,7},{7,5},{5,3},{3,1},{1,0},{8,10},{10,12},{12... | collective-permute-start | bytes 688136 | tf_op jit(solution)/shard_map/ppermute | solution.py:68
  109.5 8.4 %collective-permute-start.26 = (bf16[448,256]{1,0:T(8,128)(2,1)S(1)}, bf16[448,256]{1,0:T(8,128)(2,1)S(1)}, u32[]{:S(2)}, u32[]{:S(2)}) collective-permute-start(bf16[448,256]{1,0:T(8,128)(2,1)S(1)} %get-tuple-element.141.piece_refs_0_.refs_11__0_), channel_id=1, source_target_pairs={{0,1},{2,0},{4,2},{6,4},{7,6},{5,7},{3,5},{1,3},{8,9},{10,8},{12,1... | collective-permute-start | bytes 688136 | tf_op jit(solution)/shard_map/ppermute | solution.py:68
  110.1 11.1 %collective-permute-start.29 = (bf16[448,256]{1,0:T(8,128)(2,1)S(1)}, bf16[448,256]{1,0:T(8,128)(2,1)S(1)}, u32[]{:S(2)}, u32[]{:S(2)}) collective-permute-start(bf16[448,256]{1,0:T(8,128)(2,1)S(1)} %get-tuple-element.145.piece_refs_0_.refs_11__1_), channel_id=1, source_target_pairs={{0,2},{2,4},{4,6},{6,7},{7,5},{5,3},{3,1},{1,0},{8,10},{10,12},{12... | collective-permute-start | bytes 688136 | tf_op jit(solution)/shard_map/ppermute | solution.py:68
  111.5 11.3 %collective-permute-start.30 = (bf16[448,256]{1,0:T(8,128)(2,1)S(1)}, bf16[448,256]{1,0:T(8,128)(2,1)S(1)}, u32[]{:S(2)}, u32[]{:S(2)}) collective-permute-start(bf16[448,256]{1,0:T(8,128)(2,1)S(1)} %get-tuple-element.145.piece_refs_0_.refs_11__1_), channel_id=1, source_target_pairs={{0,1},{2,0},{4,2},{6,4},{7,6},{5,7},{3,5},{1,3},{8,9},{10,8},{12,1... | collective-permute-start | bytes 688136 | tf_op jit(solution)/shard_map/ppermute | solution.py:68
  117.9 8.5 %collective-permute-start.27 = (bf16[448,256]{1,0:T(8,128)(2,1)S(1)}, bf16[448,256]{1,0:T(8,128)(2,1)S(1)}, u32[]{:S(2)}, u32[]{:S(2)}) collective-permute-start(bf16[448,256]{1,0:T(8,128)(2,1)S(1)} %collective-permute-done.25.piece_refs_1_), channel_id=1, source_target_pairs={{0,2},{2,4},{4,6},{6,7},{7,5},{5,3},{3,1},{1,0},{8,10},{10,12},{12... | collective-permute-start | bytes 688136 | tf_op jit(solution)/shard_map/ppermute | solution.py:68
  118.5 9.2 %collective-permute-start.28 = (bf16[448,256]{1,0:T(8,128)(2,1)S(1)}, bf16[448,256]{1,0:T(8,128)(2,1)S(1)}, u32[]{:S(2)}, u32[]{:S(2)}) collective-permute-start(bf16[448,256]{1,0:T(8,128)(2,1)S(1)} %collective-permute-done.26.piece_refs_2_), channel_id=1, source_target_pairs={{0,1},{2,0},{4,2},{6,4},{7,6},{5,7},{3,5},{1,3},{8,9},{10,8},{12,1... | collective-permute-start | bytes 688136 | tf_op jit(solution)/shard_map/ppermute | solution.py:68
  122.8 8.5 %collective-permute-start.33 = (bf16[448,256]{1,0:T(8,128)(2,1)S(1)}, bf16[448,256]{1,0:T(8,128)(2,1)S(1)}, u32[]{:S(2)}, u32[]{:S(2)}) collective-permute-start(bf16[448,256]{1,0:T(8,128)(2,1)S(1)} %collective-permute-done.29.piece_refs_1_), channel_id=1, source_target_pairs={{0,2},{2,4},{4,6},{6,7},{7,5},{5,3},{3,1},{1,0},{8,10},{10,12},{12... | collective-permute-start | bytes 688136 | tf_op jit(solution)/shard_map/ppermute | solution.py:68
  123.4 8.5 %collective-permute-start.34 = (bf16[448,256]{1,0:T(8,128)(2,1)S(1)}, bf16[448,256]{1,0:T(8,128)(2,1)S(1)}, u32[]{:S(2)}, u32[]{:S(2)}) collective-permute-start(bf16[448,256]{1,0:T(8,128)(2,1)S(1)} %collective-permute-done.30.piece_refs_2_), channel_id=1, source_target_pairs={{0,1},{2,0},{4,2},{6,4},{7,6},{5,7},{3,5},{1,3},{8,9},{10,8},{12,1... | collective-permute-start | bytes 688136 | tf_op jit(solution)/shard_map/ppermute | solution.py:68
  127.7 9.5 %collective-permute-start.31 = (bf16[448,256]{1,0:T(8,128)(2,1)S(1)}, bf16[448,256]{1,0:T(8,128)(2,1)S(1)}, u32[]{:S(2)}, u32[]{:S(2)}) collective-permute-start(bf16[448,256]{1,0:T(8,128)(2,1)S(1)} %collective-permute-done.27.piece_refs_3_), channel_id=1, source_target_pairs={{0,2},{2,4},{4,6},{6,7},{7,5},{5,3},{3,1},{1,0},{8,10},{10,12},{12... | collective-permute-start | bytes 688136 | tf_op jit(solution)/shard_map/ppermute | solution.py:68
  128.3 8.9 %collective-permute-start.32 = (bf16[448,256]{1,0:T(8,128)(2,1)S(1)}, bf16[448,256]{1,0:T(8,128)(2,1)S(1)}, u32[]{:S(2)}, u32[]{:S(2)}) collective-permute-start(bf16[448,256]{1,0:T(8,128)(2,1)S(1)} %collective-permute-done.28.piece_refs_4_), channel_id=1, source_target_pairs={{0,1},{2,0},{4,2},{6,4},{7,6},{5,7},{3,5},{1,3},{8,9},{10,8},{12,1... | collective-permute-start | bytes 688136 | tf_op jit(solution)/shard_map/ppermute | solution.py:68
  132.0 6.7 %collective-permute-start.36 = (bf16[448,256]{1,0:T(8,128)(2,1)S(1)}, bf16[448,256]{1,0:T(8,128)(2,1)S(1)}, u32[]{:S(2)}, u32[]{:S(2)}) collective-permute-start(bf16[448,256]{1,0:T(8,128)(2,1)S(1)} %collective-permute-done.33.piece_refs_3_), channel_id=1, source_target_pairs={{0,2},{2,4},{4,6},{6,7},{7,5},{5,3},{3,1},{1,0},{8,10},{10,12},{12... | collective-permute-start | bytes 688136 | tf_op jit(solution)/shard_map/ppermute | solution.py:68
  132.7 6.7 %collective-permute-start.37 = (bf16[448,256]{1,0:T(8,128)(2,1)S(1)}, bf16[448,256]{1,0:T(8,128)(2,1)S(1)}, u32[]{:S(2)}, u32[]{:S(2)}) collective-permute-start(bf16[448,256]{1,0:T(8,128)(2,1)S(1)} %collective-permute-done.34.piece_refs_4_), channel_id=1, source_target_pairs={{0,1},{2,0},{4,2},{6,4},{7,6},{5,7},{3,5},{1,3},{8,9},{10,8},{12,1... | collective-permute-start | bytes 688136 | tf_op jit(solution)/shard_map/ppermute | solution.py:68
  137.2 6.1 %collective-permute-start.35 = (bf16[448,256]{1,0:T(8,128)(2,1)S(1)}, bf16[448,256]{1,0:T(8,128)(2,1)S(1)}, u32[]{:S(2)}, u32[]{:S(2)}) collective-permute-start(bf16[448,256]{1,0:T(8,128)(2,1)S(1)} %collective-permute-done.31.piece_refs_5_), channel_id=1, source_target_pairs={{0,2},{2,4},{4,6},{6,7},{7,5},{5,3},{3,1},{1,0},{8,10},{10,12},{12... | collective-permute-start | bytes 688136 | tf_op jit(solution)/shard_map/ppermute | solution.py:72
  139.3 7.9 %collective-permute-start.38 = (bf16[448,256]{1,0:T(8,128)(2,1)S(1)}, bf16[448,256]{1,0:T(8,128)(2,1)S(1)}, u32[]{:S(2)}, u32[]{:S(2)}) collective-permute-start(bf16[448,256]{1,0:T(8,128)(2,1)S(1)} %collective-permute-done.37.piece_refs_6_), channel_id=1, source_target_pairs={{0,1},{2,0},{4,2},{6,4},{7,6},{5,7},{3,5},{1,3},{8,9},{10,8},{12,1... | collective-permute-start | bytes 688136 | tf_op jit(solution)/shard_map/ppermute | solution.py:74
  145.9 11.0 %collective-permute-start.39 = (bf16[448,256]{1,0:T(8,128)(2,1)S(1)}, bf16[448,256]{1,0:T(8,128)(2,1)S(1)}, u32[]{:S(2)}, u32[]{:S(2)}) collective-permute-start(bf16[448,256]{1,0:T(8,128)(2,1)S(1)} %get-tuple-element.157.first_refs_0_.refs_2__0__0_), channel_id=1, source_target_pairs={{0,8},{16,24},{1,9},{17,25},{2,10},{18,26},{3,11},{19,27},{4,12},{... | collective-permute-start | bytes 688136 | tf_op jit(solution)/shard_map/ppermute | solution.py:678
  150.7 6.2 %collective-permute-start.40 = (bf16[448,256]{1,0:T(8,128)(2,1)S(1)}, bf16[448,256]{1,0:T(8,128)(2,1)S(1)}, u32[]{:S(2)}, u32[]{:S(2)}) collective-permute-start(bf16[448,256]{1,0:T(8,128)(2,1)S(1)} %get-tuple-element.159.refs_2__0__1_), channel_id=1, source_target_pairs={{0,8},{16,24},{1,9},{17,25},{2,10},{18,26},{3,11},{19,27},{4,12},{... | collective-permute-start | bytes 688136 | tf_op jit(solution)/shard_map/ppermute | solution.py:678
  152.0 7.1 %collective-permute-start.41 = (bf16[448,256]{1,0:T(8,128)(2,1)S(1)}, bf16[448,256]{1,0:T(8,128)(2,1)S(1)}, u32[]{:S(2)}, u32[]{:S(2)}) collective-permute-start(bf16[448,256]{1,0:T(8,128)(2,1)S(1)} %get-tuple-element.157.first_refs_0_.refs_2__0__0_), channel_id=1, source_target_pairs={{0,16},{8,24},{1,17},{9,25},{2,18},{10,26},{3,19},{11,27},{4,20},{... | collective-permute-start | bytes 688136 | tf_op jit(solution)/shard_map/ppermute | solution.py:681
  155.6 6.0 %collective-permute-start.42 = (bf16[448,256]{1,0:T(8,128)(2,1)S(1)}, bf16[448,256]{1,0:T(8,128)(2,1)S(1)}, u32[]{:S(2)}, u32[]{:S(2)}) collective-permute-start(bf16[448,256]{1,0:T(8,128)(2,1)S(1)} %get-tuple-element.159.refs_2__0__1_), channel_id=1, source_target_pairs={{0,16},{8,24},{1,17},{9,25},{2,18},{10,26},{3,19},{11,27},{4,20},{... | collective-permute-start | bytes 688136 | tf_op jit(solution)/shard_map/ppermute | solution.py:681
  161.5 15.5 %all-to-all-start.1 = ((bf16[8,56,448]{2,1,0:T(8,128)(2,1)}), bf16[8,56,448]{2,1,0:T(8,128)(2,1)S(1)}, u32[]{:S(2)}, u32[]{:S(2)}) async-start(bf16[8,56,448]{2,1,0:T(8,128)(2,1)} %get-tuple-element.167), calls=%async_computation.1 | async-start | bytes 917504 | tf_op jit(solution)/shard_map/all_to_all | solution.py:559
  165.0 31.6 %all-gather.6.cloned.1.call-start = ((), (), s32[]{:S(2)}) async-start(), calls=%async_computation.3 | async-start | bytes 2293760 | tf_op jit(solution)/shard_map/all_gather | solution.py:563
  165.1 1.4 collective-permute-start.43
  165.8 0.7 collective-permute-start.44
  177.9 23.4 %copy-start.17 = (bf16[768,64]{1,0:T(8,128)(2,1)S(1)}, bf16[768,64]{1,0:T(8,128)(2,1)}, u32[]{:S(2)}) copy-start(bf16[768,64]{1,0:T(8,128)(2,1)} %add.7) | copy-start | bytes 294916
  179.4 6.9 %collective-permute-start.45 = (bf16[224,512]{1,0:T(8,128)(2,1)S(1)}, bf16[224,512]{1,0:T(8,128)(2,1)S(1)}, u32[]{:S(2)}, u32[]{:S(2)}) collective-permute-start(bf16[224,512]{1,0:T(8,128)(2,1)S(1)} %shard_map.212.refs_1_), channel_id=1, source_target_pairs={{0,2},{2,4},{4,6},{6,7},{7,5},{5,3},{3,1},{1,0},{8,10},{10,12},{12... | collective-permute-start | bytes 688136 | tf_op jit(solution)/shard_map/ppermute | solution.py:68
  179.5 7.0 %collective-permute-start.46 = (bf16[224,512]{1,0:T(8,128)(2,1)S(1)}, bf16[224,512]{1,0:T(8,128)(2,1)S(1)}, u32[]{:S(2)}, u32[]{:S(2)}) collective-permute-start(bf16[224,512]{1,0:T(8,128)(2,1)S(1)} %shard_map.212.refs_1_), channel_id=1, source_target_pairs={{0,1},{2,0},{4,2},{6,4},{7,6},{5,7},{3,5},{1,3},{8,9},{10,8},{12,1... | collective-permute-start | bytes 688136 | tf_op jit(solution)/shard_map/ppermute | solution.py:68
  186.4 6.2 %collective-permute-start.47 = (bf16[224,512]{1,0:T(8,128)(2,1)S(1)}, bf16[224,512]{1,0:T(8,128)(2,1)S(1)}, u32[]{:S(2)}, u32[]{:S(2)}) collective-permute-start(bf16[224,512]{1,0:T(8,128)(2,1)S(1)} %collective-permute-done.45.refs_2_), channel_id=1, source_target_pairs={{0,2},{2,4},{4,6},{6,7},{7,5},{5,3},{3,1},{1,0},{8,10},{10,12},{12... | collective-permute-start | bytes 688136 | tf_op jit(solution)/shard_map/ppermute | solution.py:68
  186.4 6.2 %collective-permute-start.48 = (bf16[224,512]{1,0:T(8,128)(2,1)S(1)}, bf16[224,512]{1,0:T(8,128)(2,1)S(1)}, u32[]{:S(2)}, u32[]{:S(2)}) collective-permute-start(bf16[224,512]{1,0:T(8,128)(2,1)S(1)} %collective-permute-done.46.refs_3_), channel_id=1, source_target_pairs={{0,1},{2,0},{4,2},{6,4},{7,6},{5,7},{3,5},{1,3},{8,9},{10,8},{12,1... | collective-permute-start | bytes 688136 | tf_op jit(solution)/shard_map/ppermute | solution.py:68
  192.7 6.1 %collective-permute-start.49 = (bf16[224,512]{1,0:T(8,128)(2,1)S(1)}, bf16[224,512]{1,0:T(8,128)(2,1)S(1)}, u32[]{:S(2)}, u32[]{:S(2)}) collective-permute-start(bf16[224,512]{1,0:T(8,128)(2,1)S(1)} %collective-permute-done.47.refs_4_), channel_id=1, source_target_pairs={{0,2},{2,4},{4,6},{6,7},{7,5},{5,3},{3,1},{1,0},{8,10},{10,12},{12... | collective-permute-start | bytes 688136 | tf_op jit(solution)/shard_map/ppermute | solution.py:68
  193.0 6.0 %collective-permute-start.50 = (bf16[224,512]{1,0:T(8,128)(2,1)S(1)}, bf16[224,512]{1,0:T(8,128)(2,1)S(1)}, u32[]{:S(2)}, u32[]{:S(2)}) collective-permute-start(bf16[224,512]{1,0:T(8,128)(2,1)S(1)} %collective-permute-done.48.refs_5_), channel_id=1, source_target_pairs={{0,1},{2,0},{4,2},{6,4},{7,6},{5,7},{3,5},{1,3},{8,9},{10,8},{12,1... | collective-permute-start | bytes 688136 | tf_op jit(solution)/shard_map/ppermute | solution.py:68
  199.1 5.0 %collective-permute-start.51 = (bf16[112,512]{1,0:T(8,128)(2,1)S(1)}, bf16[112,512]{1,0:T(8,128)(2,1)S(1)}, u32[]{:S(2)}, u32[]{:S(2)}) collective-permute-start(bf16[112,512]{1,0:T(8,128)(2,1)S(1)} %slice.22), channel_id=1, source_target_pairs={{0,2},{2,4},{4,6},{6,7},{7,5},{5,3},{3,1},{1,0},{8,10},{10,12},{12... | collective-permute-start | bytes 344072 | tf_op jit(solution)/shard_map/ppermute | solution.py:70
  201.2 4.8 %collective-permute-start.52 = (bf16[112,512]{1,0:T(8,128)(2,1)S(1)}, bf16[112,512]{1,0:T(8,128)(2,1)S(1)}, u32[]{:S(2)}, u32[]{:S(2)}) collective-permute-start(bf16[112,512]{1,0:T(8,128)(2,1)S(1)} %slice.23), channel_id=1, source_target_pairs={{0,1},{2,0},{4,2},{6,4},{7,6},{5,7},{3,5},{1,3},{8,9},{10,8},{12,1... | collective-permute-start | bytes 344072 | tf_op jit(solution)/shard_map/ppermute | solution.py:70
  (13 other events, 63.9 us)
Sparse Core Ops, SparseCore 0:
  69.6 20.1 all-gather.3
  178.0 18.6 all-gather.5
